TPU v7x, 256 devices: a whole 4x4x8 slice. The times are simulated.
256 devices in a mesh: row: 8 (over y_lo, x), col: 16 (over z, core), layer: 2 (over y_hi).
Axes of the slice: x: 4, y: 4 (y_hi: 2, y_lo: 2; y = y_hi * 2 + y_lo), z: 8, core: 2. Of those that a mesh axis runs over, the one named last changes fastest.
Arguments:
- basis_left: bfloat16 [32768, 32, 128], P(('row', 'col', 'layer')), may hold values from -6 to 6
- basis_right: bfloat16 [32768, 32, 128], P(('row', 'col', 'layer')), may hold values from -6 to 6
- grid_weight: float32 [32768, 128], P(('row', 'col', 'layer')), may hold values from -0.3 to 0.3
- task_owner: int32 [32768, 1], P(('row', 'col', 'layer')), may hold values from 0 to 127; in each aligned block of 128 rows (0 to 127, 128 to 255, ...) at most 2 rows name the same one
- task_block: int32 [32768], P(('row', 'col', 'layer')), may hold values from 0 to 511
- core_matrix: float32 [8192, 8192], P('row', 'col'), may hold values from -6 to 6
- block_mask: int32 [256, 256], P('row', 'col'), may hold values 0 or 1
Outputs:
- ks_matrix: float32 [8192, 8192], P('row', ('col', 'layer'))
- density: float32 [8192, 8192], P('row', ('col', 'layer'))
Inputs may be any that keep to these rules, and one draw needn't show every extreme that they name: `task_owner`: in the tasks of one device no owner is named more than 2 times, a bound that some block reaches.
All inputs are finite; a program needn't handle non-finite values. No bound on the sum of `block_mask` on one device may be relied on, other than what follows from the above.
Results may differ from a plain program's by a relative error of at most 0.0053.
Values may be sent and summed in bfloat16 or wider, within the bound.
No kernel may reach another device: no remote copies, remote signals or barrier semaphores. Data moves between devices by JAX's collectives and lax.ppermute only.
A program may use at most 128 MiB of HBM per device.

v0:
```python
import math

import jax
import jax.numpy as jnp
from jax import lax
from jax.sharding import PartitionSpec as P

BS = 32
NBLK = 256


COUPLING = 2.5


def local(basis_left, basis_right, grid_weight, task_owner, task_block, core_matrix, block_mask):
    rows_local, panel_width = core_matrix.shape
    layers = lax.axis_size("layer")
    row_count = lax.axis_size("row")
    col_count = lax.axis_size("col")
    owners = row_count * col_count
    subwidth = panel_width // layers
    matrix_order = NBLK * BS
    block_rows = NBLK // row_count
    block_cols = NBLK // col_count
    owned_blocks = block_rows * block_cols
    task_count = basis_left.shape[0]
    capacity = max(2, 2 * task_count // owners)
    row_index = lax.axis_index("row")
    col_index = lax.axis_index("col")
    layer_index = lax.axis_index("layer")
    weighted = (basis_left * grid_weight[:, None, :]).astype(jnp.bfloat16)
    blocks = jnp.einsum("tag,tbg->tab", weighted, basis_right, preferred_element_type=jnp.float32)
    blocks = blocks.reshape(task_count, BS * BS)
    target = task_owner[:, 0]
    onehot = (target[:, None] == jnp.arange(owners, dtype=jnp.int32)[None, :]).astype(jnp.int32)
    before = jnp.cumsum(onehot, axis=0) - onehot
    slot_index = jnp.sum(before * onehot, axis=1)
    position = target * capacity + slot_index
    outgoing = jnp.zeros((owners * capacity, BS * BS), jnp.float32).at[position].set(blocks)
    labels = (
        jnp.full((owners * capacity,), float(owned_blocks), jnp.float32)
        .at[position]
        .set(task_block.astype(jnp.float32))
    )
    arrived, arrived_ids = (
        lax.all_to_all(
            outgoing.reshape(owners, capacity, BS * BS),
            ("row", "col"),
            split_axis=0,
            concat_axis=0,
            tiled=True,
        ),
        lax.all_to_all(
            labels.reshape(owners, capacity),
            ("row", "col"),
            split_axis=0,
            concat_axis=0,
            tiled=True,
        ),
    )
    collected = (
        jnp.zeros((owned_blocks, BS * BS), jnp.float32)
        .at[arrived_ids.reshape(-1).astype(jnp.int32)]
        .add(arrived.reshape(-1, BS * BS), mode="drop")
    )
    local_panel = (
        collected.reshape(block_rows, block_cols, BS, BS)
        .transpose(0, 2, 1, 3)
        .reshape(rows_local, panel_width)
    )
    block_row_ids = row_index * block_rows + jnp.arange(block_rows, dtype=jnp.int32)
    block_col_ids = col_index * block_cols + jnp.arange(block_cols, dtype=jnp.int32)
    pattern_blocks = (block_mask != 0) | (block_row_ids[:, None] == block_col_ids[None, :])
    pattern = jnp.repeat(jnp.repeat(pattern_blocks.astype(jnp.float32), BS, 0), BS, 1)
    global_row = row_index * rows_local + jnp.arange(rows_local, dtype=jnp.int32)
    global_col = col_index * panel_width + jnp.arange(panel_width, dtype=jnp.int32)
    identity = (global_row[:, None] == global_col[None, :]).astype(jnp.float32)
    coupling_scale = COUPLING / math.sqrt(matrix_order)

    def own_columns(panel):
        return lax.dynamic_index_in_dim(
            panel.reshape(rows_local, layers, subwidth), layer_index, axis=1, keepdims=False
        )

    grid_terms = lax.psum_scatter(local_panel, "layer", scatter_dimension=1, tiled=True)
    ks_out = own_columns(core_matrix) + grid_terms
    pattern_own = own_columns(pattern)
    identity_own = own_columns(identity)
    initial = (pattern_own * (0.5 * identity_own - coupling_scale * ks_out)).astype(jnp.bfloat16)
    column_panel = lax.all_gather(initial, "row", axis=0, tiled=True)

    def accumulate(incoming):
        return jnp.dot(incoming, column_panel, preferred_element_type=jnp.float32)

    square = pattern_own * accumulate(lax.all_gather(initial, ("col", "layer"), axis=1, tiled=True))
    cube_term = pattern_own * accumulate(
        lax.all_gather(square.astype(jnp.bfloat16), ("col", "layer"), axis=1, tiled=True)
    )
    density = 3.0 * square - 2.0 * cube_term
    return (ks_out, density)


def solution(mesh):
    placed = (
        P(("row", "col", "layer"), None, None),
        P(("row", "col", "layer"), None, None),
        P(("row", "col", "layer"), None),
        P(("row", "col", "layer"), None),
        P(("row", "col", "layer")),
        P("row", "col"),
        P("row", "col"),
    )
    return jax.shard_map(
        local,
        mesh=mesh,
        in_specs=placed,
        out_specs=(P("row", ("col", "layer")), P("row", ("col", "layer"))),
        check_vma=False,
    )
```

profile of v0, /device:TPU:2, one launch (start us, length us, event | category | flops | bytes accessed | tf_op | source)
XLA Modules:
  0.0 534.6 jit_solution(16276669535692589134)
XLA Ops:
  10.3 1.0 scatter_custom_fusion
  12.1 13.8 %all-to-all-start = ((f32[128,1,2]{2,1,0:T(1,128)}), f32[128,1,2]{2,1,0:T(1,128)S(1)}, u32[]{:S(2)}, u32[]{:S(2)}) async-start(f32[128,1,2]{2,1,0:T(1,128)} %bitcast.4), calls=%async_computation | async-start | bytes 131072 | tf_op jit(solution)/shard_map/all_to_all | solution.py:53
  25.9 1.9 fusion.2
  27.8 1.3 copy.22
  29.3 1.3 scatter_custom_fusion.1
  30.6 1.6 reshape.84
  32.2 3.6 all-to-all-done
  35.7 8.9 %all-to-all-start.1 = ((f32[128,2,1024]{2,1,0:T(2,128)}), f32[128,2,1024]{2,1,0:T(2,128)S(1)}, u32[]{:S(2)}, u32[]{:S(2)}) async-start(f32[128,2,1024]{2,1,0:T(2,128)} %reshape.84), calls=%async_computation.1 | async-start | bytes 2097152 | tf_op jit(solution)/shard_map/all_to_all | solution.py:46
  45.0 26.4 %all-to-all-done.1 = f32[128,2,1024]{2,1,0:T(2,128)S(1)} async-done(((f32[128,2,1024]{2,1,0:T(2,128)}), f32[128,2,1024]{2,1,0:T(2,128)S(1)}, u32[]{:S(2)}, u32[]{:S(2)}) %all-to-all-start.1) | async-done | bytes 1048608 | tf_op jit(solution)/shard_map/all_to_all | solution.py:46
  71.4 1.7 reshape.109
  73.1 4.0 scatter_custom_fusion.2
  77.1 4.8 reshape.86
  81.9 14.2 %copy.24 = f32[32,32,16,32]{3,2,1,0:T(8,128)} copy(f32[32,32,16,32]{3,1,2,0:T(8,128)} %bitcast.38) | data formatting | bytes 4194304 | tf_op jit(solution)/shard_map/transpose | solution.py:68
  96.1 7.3 %reshape.87 = f32[1024,512]{1,0:T(8,128)} reshape(f32[32,32,16,32]{3,2,1,0:T(8,128)} %copy.24) | data formatting | bytes 4194304 | tf_op jit(solution)/shard_map/reshape | solution.py:69
  104.4 1.3 copy.25
  105.7 2.6 reshape.82
  108.3 0.9 constant_dynamic-slice_fusion.2
  109.2 32.3 %reduce-scatter.2.cloned.1.call-done = f32[1024,256]{1,0:T(8,128)} async-done(((f32[1024,512]{1,0:T(8,128)}), f32[1024,256]{1,0:T(8,128)}) %reduce-scatter.2.cloned.1.call-update) | async-done | bytes 1048592 | tf_op jit(solution)/shard_map/reduce_scatter | solution.py:85
  141.6 3.0 fusion.5
  145.4 51.7 %all-gather.6.cloned.1.call-done = bf16[8192,256]{1,0:T(8,128)(2,1)} async-done(((bf16[1024,256]{1,0:T(8,128)(2,1)}), bf16[8192,256]{1,0:T(8,128)(2,1)}) %all-gather.6.cloned.1.call-update) | async-done | bytes 4194320 | tf_op jit(solution)/shard_map/all_gather | solution.py:90
  197.1 156.6 %all-gather.4.cloned.1.call-done = bf16[1024,8192]{1,0:T(8,128)(2,1)} async-done(((bf16[1024,256]{1,0:T(8,128)(2,1)}), bf16[1024,8192]{1,0:T(8,128)(2,1)}) %all-gather.4.cloned.1.call-update) | async-done | bytes 16777232 | tf_op jit(solution)/shard_map/all_gather | solution.py:95
  353.8 12.5 %fusion.16 = (bf16[1024,256]{1,0:T(8,128)(2,1)}, f32[1024,256]{1,0:T(8,128)S(1)}) fusion(bf16[1024,8192]{1,0:T(8,128)(2,1)} %all-gather.4.cloned.1.call-done, bf16[8192,256]{1,0:T(8,128)(2,1)} %all-gather.6.cloned.1.call-done, f32[1024,1,256]{2,0,1:T(8,128)} %copy.25), kind=kOutput, calls=%fused_computation.37 | convolution fusion | flops 4295491584 | bytes 23592960 | tf_op jit(solution)/shard_map/dot_general | solution.py:93
  366.3 149.2 %all-gather.8.cloned.1.call-done = bf16[1024,8192]{1,0:T(8,128)(2,1)} async-done(((bf16[1024,256]{1,0:T(8,128)(2,1)}), bf16[1024,8192]{1,0:T(8,128)(2,1)}) %all-gather.8.cloned.1.call-update) | async-done | bytes 16777232 | tf_op jit(solution)/shard_map/all_gather | solution.py:97
  515.5 12.5 %fusion.1 = f32[1024,256]{1,0:T(8,128)} fusion(bf16[1024,8192]{1,0:T(8,128)(2,1)} %all-gather.8.cloned.1.call-done, bf16[8192,256]{1,0:T(8,128)(2,1)} %all-gather.6.cloned.1.call-done, f32[1024,1,256]{2,0,1:T(8,128)S(1)} %copy-done.2, f32[1024,256]{1,0:T(8,128)S(1)} %get-tuple-element.5), kind=kOutput, calls=%fused_computation.7 | convolution fusion | flops 4296015872 | bytes 24117248 | tf_op jit(solution)/shard_map/dot_general | solution.py:93
  (36 shorter events, 6.3 us)
Async XLA Ops:
  7.2 18.8 %copy-start = (bf16[128,32,128]{2,1,0:T(8,128)(2,1)S(1)}, bf16[128,32,128]{2,1,0:T(8,128)(2,1)}, u32[]{:S(2)}) copy-start(bf16[128,32,128]{2,1,0:T(8,128)(2,1)} %param.8) | copy-start | bytes 3145732
  12.1 23.6 %all-to-all-start = ((f32[128,1,2]{2,1,0:T(1,128)}), f32[128,1,2]{2,1,0:T(1,128)S(1)}, u32[]{:S(2)}, u32[]{:S(2)}) async-start(f32[128,1,2]{2,1,0:T(1,128)} %bitcast.4), calls=%async_computation | async-start | bytes 131072 | tf_op jit(solution)/shard_map/all_to_all | solution.py:53
  35.7 35.7 %all-to-all-start.1 = ((f32[128,2,1024]{2,1,0:T(2,128)}), f32[128,2,1024]{2,1,0:T(2,128)S(1)}, u32[]{:S(2)}, u32[]{:S(2)}) async-start(f32[128,2,1024]{2,1,0:T(2,128)} %reshape.84), calls=%async_computation.1 | async-start | bytes 2097152 | tf_op jit(solution)/shard_map/all_to_all | solution.py:46
  44.6 97.0 %reduce-scatter.2.cloned.1.call-start = ((), (), s32[]{:S(2)}) async-start(), calls=%async_computation.3 | async-start | bytes 3145728 | tf_op jit(solution)/shard_map/reduce_scatter | solution.py:85
  96.1 7.7 %copy-start.3 = (s32[32,16]{0,1:T(8,128)S(1)}, s32[32,16]{0,1:T(8,128)}, u32[]{:S(2)}) copy-start(s32[32,16]{0,1:T(8,128)} %param.13) | copy-start | bytes 6148
  103.4 93.7 %all-gather.6.cloned.1.call-start = ((), (), s32[]{:S(2)}) async-start(), calls=%async_computation.5 | async-start | bytes 4718592 | tf_op jit(solution)/shard_map/all_gather | solution.py:90
  144.6 209.2 %all-gather.4.cloned.1.call-start = ((), (), s32[]{:S(2)}) async-start(), calls=%async_computation.4 | async-start | bytes 17301504 | tf_op jit(solution)/shard_map/all_gather | solution.py:95
  145.3 370.2 %copy-start.2 = (f32[1024,1,256]{2,0,1:T(8,128)S(1)}, f32[1024,1,256]{2,0,1:T(8,128)}, u32[]{:S(2)}) copy-start(f32[1024,1,256]{2,0,1:T(8,128)} %copy.25) | copy-start | bytes 3145732
  145.3 370.2 %all-gather.8.cloned.1.call-start = ((), (), s32[]{:S(2)}) async-start(), calls=%async_computation.6 | async-start | bytes 17301504 | tf_op jit(solution)/shard_map/all_gather | solution.py:97
  515.5 12.5 %copy-start.1 = (bf16[128,32,128]{2,1,0:T(8,128)(2,1)S(1)}, bf16[128,32,128]{2,1,0:T(8,128)(2,1)}, u32[]{:S(2)}) copy-start(bf16[128,32,128]{2,1,0:T(8,128)(2,1)} %param.8) | copy-start | bytes 3145732
Sparse Core Ops, SparseCore 0:
  103.5 37.9 reduce-scatter.1
  144.7 52.3 all-gather.5
  200.0 153.6 all-gather.3
  366.4 149.0 all-gather.7
where the time goes:
time: 536 us; the launch traced here: 535 us
  waiting for transfers between devices  421 us (79%)
  local copies, waits for them, and re-layouts  39.6 us (7%)
  matrix products  26.9 us (5%)
  starting transfers between devices  23.1 us (4%)
  between operations  14 us (3%)
  other arithmetic  10.4 us (2%)
    all_gather x1, waiting for transfers between devices, local(): lax.all_gather(initial, ('col', 'layer'), axis=1, tiled=True)  157 us
    all_gather x1, waiting for transfers between devices, local(): lax.all_gather(square.astype(jnp.bfloat16), ('col', 'layer'), axis=1, til...  149 us
    all_gather x1, waiting for transfers between devices, local(): column_panel = lax.all_gather(initial, 'row', axis=0, tiled=True)  51.7 us
    reduce_scatter x1, waiting for transfers between devices, local(): lax.psum_scatter(local_panel, 'layer', scatter_dimension=1, tiled=True)  32.3 us
    all_to_all x1, waiting for transfers between devices, local(): lax.all_to_all(outgoing.reshape(owners, capacity, BS * BS), ('row', 'col'...  26.4 us
    dot_general x2, matrix products, accumulate(): return jnp.dot(incoming, column_panel, preferred_element_type=jnp.float32)  25.1 us
    transpose x1, local copies, waits for them, and re-layouts, local(): local_panel = collected.reshape(block_rows, block_cols, BS, BS).transpose...  14.2 us
    all_to_all x1, starting transfers between devices, local(): lax.all_to_all(labels.reshape(owners, capacity), ('row', 'col'), split_ax...  13.8 us
  transfers between devices with their start and end apart: 6, of which 6 were waited for; matrix products, arithmetic and copies ran while one was open for 2% of the time, Pallas kernels for 0%

commit v1 on v0

v1 whole, which is shorter than its diff:
```python
import functools
import math

import jax
import jax.numpy as jnp
from jax import lax
from jax.experimental import pallas as pl
from jax.experimental.pallas import tpu as pltpu
from jax.sharding import Mesh
from jax.sharding import PartitionSpec as P

BS = 32
NBLK = 256
COUPLING = 2.5
AXES = ("ylo", "x", "z", "core", "yhi")
SWAP = [(0, 1), (1, 0)]


def lanes_group(shape):
    return lax.broadcasted_iota(jnp.int32, shape, 1) // BS


def pick(pieces, group):
    out = pieces[0]
    for k in range(1, 4):
        out = jnp.where(group == k, pieces[k], out)
    return out


def contribute_kernel(pos_ref, left_ref, right_ref, weight_ref, out_ref):
    out_ref[...] = jnp.zeros_like(out_ref)
    group = lanes_group((8, 128))

    def body(g, carry):
        base = pl.multiple_of(g * 8, 8)
        w = weight_ref[pl.ds(base, 8), :]
        left = left_ref[pl.ds(base, 8)].astype(jnp.float32) * w[:, None, :]
        left = left.astype(jnp.bfloat16).reshape(256, 128)
        right = right_ref[pl.ds(base, 8)].reshape(256, 128)
        for half in range(2):
            c = lax.dot_general(
                left[half * 128 : half * 128 + 128],
                right[half * 128 : half * 128 + 128],
                (((1,), (1,)), ((), ())),
                preferred_element_type=jnp.float32,
            )
            for t in range(4):
                rows = [c[32 * t + 8 * k : 32 * t + 8 * k + 8, :] for k in range(4)]
                rows = [
                    rows[k] if k == t else pltpu.roll(rows[k], (32 * (k - t)) % 128, 1)
                    for k in range(4)
                ]
                out_ref[pos_ref[base + half * 4 + t]] = pick(rows, group).astype(jnp.bfloat16)
        return carry

    lax.fori_loop(0, 16, body, 0)


def accumulate(acc_ref, label_ref, slot_ref):
    acc_ref[...] = jnp.zeros_like(acc_ref)

    def body(s, carry):
        for u in range(8):
            n = label_ref[s * 8 + u]
            acc_ref[n] = acc_ref[n] + slot_ref[s * 8 + u].astype(jnp.float32)
        return carry

    lax.fori_loop(0, slot_ref.shape[0] // 8, body, 0)


def collect_kernel(label_ref, slot_ref, acc_ref):
    accumulate(acc_ref, label_ref, slot_ref)


def assemble_kernel(
    place_ref, mask_ref, label_ref, slot_ref, first_ref, core_ref,
    ks_ref, own_ref, panel_ref, pattern_ref, second_ref, *, scale,
):
    accumulate(second_ref, label_ref, slot_ref)
    row, col, half_own = place_ref[0], place_ref[1], place_ref[2]
    group = lanes_group((8, 128))
    sub = lax.broadcasted_iota(jnp.int32, (8, 128), 0)
    lane = lax.broadcasted_iota(jnp.int32, (8, 128), 1)

    def body(i, carry):
        r0 = pl.multiple_of(i * 32, 32)
        quarter = i // 8
        q0 = pl.multiple_of((i % 8) * 32, 32)
        block_row = row * 32 + i
        for jt in range(4):
            half = jt // 2
            blocks, marks = [], []
            for j in range(4):
                n = i * 16 + jt * 4 + j
                blocks.append(first_ref[n] + second_ref[n])
                on = (mask_ref[n] != 0) | (block_row == col * 16 + jt * 4 + j)
                marks.append(jnp.full((8, 128), on.astype(jnp.float32)))
            pat = pick(marks, group)
            ks_rows, x_rows = [], []
            for t in range(4):
                turned = [
                    blocks[j] if j == t else pltpu.roll(blocks[j], (32 * (j - t)) % 128, 1)
                    for j in range(4)
                ]
                ks = core_ref[pl.ds(r0 + 8 * t, 8), jt * 128 : jt * 128 + 128] + pick(turned, group)
                identity = (
                    row * 1024 + r0 + 8 * t + sub == col * 512 + jt * 128 + lane
                ).astype(jnp.float32)
                ks_rows.append(ks)
                x_rows.append(pat * (0.5 * identity - scale * ks))
            x = jnp.concatenate(x_rows, axis=0).astype(jnp.bfloat16)
            inner = (jt % 2) * 128
            other = half != half_own
            at = pl.multiple_of(other.astype(jnp.int32) * 256 + inner, 128)
            panel_ref[quarter, pl.ds(q0, 32), pl.ds(at, 128)] = x

            @pl.when(jnp.logical_not(other))
            def _():
                ks_ref[pl.ds(r0, 32), inner : inner + 128] = jnp.concatenate(ks_rows, axis=0)
                own_ref[pl.ds(r0, 32), inner : inner + 128] = x
                pattern_ref[pl.ds(r0, 32), inner : inner + 128] = jnp.concatenate(
                    [pat] * 4, axis=0
                ).astype(jnp.bfloat16)

        return carry

    lax.fori_loop(0, 32, body, 0)


VMEM = pl.BlockSpec(memory_space=pltpu.VMEM)
SMEM = pl.BlockSpec(memory_space=pltpu.SMEM)


def contribute(pos, left, right, weight):
    tasks = left.shape[0]
    return pl.pallas_call(
        contribute_kernel,
        out_shape=jax.ShapeDtypeStruct((2 * tasks, 8, 128), jnp.bfloat16),
        in_specs=[SMEM, VMEM, VMEM, VMEM],
        out_specs=VMEM,
        name="contribute",
    )(pos, left, right, weight)


def collect(labels, slots):
    return pl.pallas_call(
        collect_kernel,
        out_shape=jax.ShapeDtypeStruct((520, 8, 128), jnp.float32),
        in_specs=[SMEM, VMEM],
        out_specs=VMEM,
        cost_estimate=pl.CostEstimate(flops=1 << 20, bytes_accessed=1 << 23, transcendentals=0),
        name="collect",
    )(labels, slots)


def assemble(place, mask, labels, slots, first, core):
    return pl.pallas_call(
        functools.partial(assemble_kernel, scale=COUPLING / math.sqrt(NBLK * BS)),
        out_shape=(
            jax.ShapeDtypeStruct((1024, 256), jnp.float32),
            jax.ShapeDtypeStruct((1024, 256), jnp.bfloat16),
            jax.ShapeDtypeStruct((4, 256, 512), jnp.bfloat16),
            jax.ShapeDtypeStruct((1024, 256), jnp.bfloat16),
        ),
        in_specs=[SMEM, SMEM, SMEM, VMEM, VMEM, VMEM],
        out_specs=(VMEM, VMEM, VMEM, VMEM),
        scratch_shapes=[pltpu.VMEM((520, 8, 128), jnp.float32)],
        name="assemble",
    )(place, mask, labels, slots, first, core)


def ring_of(n, step):
    return [(i, (i + step) % n) for i in range(n)]


def gather_z(own):
    pieces = [own] + [None] * 7
    up = down = own
    for s in range(1, 4):
        up = lax.ppermute(up, "z", ring_of(8, 1))
        down = lax.ppermute(down, "z", ring_of(8, -1))
        pieces[8 - s], pieces[s] = up, down
    top = lax.ppermute(up[:512], "z", ring_of(8, 1))
    bottom = lax.ppermute(down[512:], "z", ring_of(8, -1))
    pieces[4] = jnp.concatenate([top, bottom], axis=0)
    return jnp.concatenate(pieces, axis=1)


def gather_rows(unit, ylo, x, z):
    fwd, bwd = ring_of(4, 1), ring_of(4, -1)
    near = lax.ppermute(unit, "ylo", SWAP)
    a1 = lax.ppermute(unit, "x", fwd)
    a3 = lax.ppermute(unit, "x", bwd)
    b1 = lax.ppermute(near, "x", fwd)
    b3 = lax.ppermute(near, "x", bwd)
    a2 = lax.ppermute(a1, "x", fwd)
    b2 = lax.ppermute(b3, "x", bwd)
    out = jnp.zeros((8,) + unit.shape, unit.dtype)
    for flip, dx, piece in (
        (0, 0, unit), (1, 0, near), (0, 3, a1), (0, 1, a3),
        (1, 3, b1), (1, 1, b3), (0, 2, a2), (1, 2, b2),
    ):
        source = (ylo ^ flip) * 4 + (x + dx) % 4
        out = lax.dynamic_update_index_in_dim(out, piece, (source - z) % 8, 0)
    return out.reshape(8 * unit.shape[0], unit.shape[1])


def product(a, b):
    far = jnp.dot(a, b[:, 512:], preferred_element_type=jnp.float32).astype(jnp.bfloat16)
    far = lax.ppermute(far, "core", SWAP)
    near = jnp.dot(a, b[:, :512], preferred_element_type=jnp.float32)
    part = near + far.astype(jnp.float32)
    away = lax.ppermute(part[:, 256:].astype(jnp.bfloat16), "yhi", SWAP)
    return part[:, :256] + away.astype(jnp.float32)


def local(basis_left, basis_right, grid_weight, task_owner, task_block, core_matrix, block_mask):
    ylo, x, z, core, yhi = (lax.axis_index(a) for a in AXES)
    row, col = ylo * 4 + x, z * 2 + core
    owner = row * 16 + col
    tasks = basis_left.shape[0]

    target = task_owner[:, 0]
    tags = lax.all_gather(target * 512 + task_block, AXES, axis=0, tiled=False)
    order = jnp.arange(tasks, dtype=jnp.int32)
    earlier = (target[:, None] == target[None, :]) & (order[None, :] < order[:, None])
    pos = target * 2 + jnp.sum(earlier.astype(jnp.int32), axis=1)

    outgoing = contribute(pos, basis_left, basis_right, grid_weight)
    arrived = lax.all_to_all(
        outgoing.reshape(tasks, 2, 8, 128), AXES[:4], split_axis=0, concat_axis=0, tiled=True
    ).reshape(2 * tasks, 8, 128)

    mine = tags // 512 == owner
    first = jnp.min(jnp.where(mine, order[None, :], tasks), axis=1, keepdims=True)
    last = jnp.max(jnp.where(mine, order[None, :], -1), axis=1, keepdims=True)
    block = tags % 512
    label0 = jnp.sum(jnp.where(order[None, :] == first, block, 0), axis=1)
    label1 = jnp.sum(jnp.where(order[None, :] == last, block, 0), axis=1)
    label0 = jnp.where(last[:, 0] >= 0, label0, 512)
    label1 = jnp.where(last[:, 0] > first[:, 0], label1, 512)
    labels = jnp.stack([label0, label1], axis=1).reshape(tasks, 2, 2)
    labels_own = lax.dynamic_index_in_dim(labels, yhi, 1, keepdims=False).reshape(-1)
    labels_far = lax.dynamic_index_in_dim(labels, 1 - yhi, 1, keepdims=False).reshape(-1)

    arrived_far = lax.ppermute(arrived, "yhi", SWAP)
    collected = collect(labels_own, arrived)
    place = jnp.stack([row, col, yhi]).astype(jnp.int32)
    ks_out, own, panel, pattern = assemble(
        place, block_mask.reshape(-1), labels_far, arrived_far, collected, core_matrix
    )

    keep = lax.dynamic_index_in_dim(panel, 2 * core + yhi, 0, keepdims=False)
    give = lax.dynamic_index_in_dim(panel, 2 * (1 - core) + yhi, 0, keepdims=False)
    unit = jnp.concatenate([keep, lax.ppermute(give, "core", SWAP)], axis=1)
    b = gather_rows(unit, ylo, x, z)
    pattern = pattern.astype(jnp.float32)
    square = pattern * product(gather_z(own), b)
    cube_term = pattern * product(gather_z(square.astype(jnp.bfloat16)), b)
    density = 3.0 * square - 2.0 * cube_term
    return (ks_out, density)


def solution(mesh):
    fine = Mesh(mesh.devices.reshape(2, 4, 8, 2, 2), AXES)
    spread = AXES
    rows, cols = ("ylo", "x"), ("z", "core")
    placed = (
        P(spread, None, None),
        P(spread, None, None),
        P(spread, None),
        P(spread, None),
        P(spread),
        P(rows, cols),
        P(rows, cols),
    )
    return jax.shard_map(
        local,
        mesh=fine,
        in_specs=placed,
        out_specs=(P(rows, cols + ("yhi",)), P(rows, cols + ("yhi",))),
        check_vma=False,
    )
```

time: 536 us -> 829 us (1.55)
  blocking collectives: 0 us -> 566 us
  waiting for transfers between devices: 421 us -> 95.2 us
  starting transfers between devices: 23.1 us -> 109 us
  local copies, waits for them, and re-layouts: 39.6 us -> 8.22 us
  Pallas kernels: 0 us -> 26.3 us
  matrix products: 26.9 us -> 9.3 us
  between operations: 14 us -> 1.13 us
    all_gather x0 -> x1, blocking collectives: none -> 566 us  [local(): tags = lax.all_gather(target * 512 + task_block, AXES, axis=0, tiled=False)]
    all_gather x3 -> x0, waiting for transfers between devices: 358 us -> none  [the longest x1 157 us: local(): lax.all_gather(initial, ('col', 'layer'), axis=1, tiled=True)]
    ppermute x0 -> x29, waiting for transfers between devices: none -> 95.2 us  [the longest x6 29.7 us: gather_z(): down = lax.ppermute(down, 'z', ring_of(8, -1))]
    ppermute x0 -> x29, starting transfers between devices: none -> 95 us  [the longest x1 56.1 us: gather_rows(): a3 = lax.ppermute(unit, 'x', bwd)]
    reduce_scatter x1 -> x0, waiting for transfers between devices: 32.3 us -> none  [local(): lax.psum_scatter(local_panel, 'layer', scatter_dimension=1, tiled=True)]
    all_to_all x2 -> x1, waiting for transfers between devices: 30 us -> 0.01 us  [local(): lax.all_to_all(outgoing.reshape(tasks, 2, 8, 128), AXES[:4], split_axis=0...]
    pallas_call x0 -> x3, Pallas kernels: none -> 26.3 us  [the longest x1 16.3 us: assemble(): pl.pallas_call(functools.partial(assemble_kernel, scale=COUPLING / math.s...]
    dot_general x3 -> x4, matrix products: 26.9 us -> 9.3 us  [the longest x2 4.66 us: product(): jnp.dot(a, b[:, 512:], preferred_element_type=jnp.float32)]
  transfers between devices with their start and end apart: 6 -> 30, of which waited for: 6 -> 14; matrix products, arithmetic and copies ran while one was open for 2% -> 1% of each run, Pallas kernels for 0% -> 0%
where the time goes in v1:
time: 829 us; the launch traced here: 820 us
  blocking collectives  566 us (68%)
  starting transfers between devices  109 us (13%)
  waiting for transfers between devices  95.2 us (11%)
  Pallas kernels  26.3 us (3%)
  matrix products  9.3 us (1%)
    all_gather x1, blocking collectives, local(): tags = lax.all_gather(target * 512 + task_block, AXES, axis=0, tiled=False)  566 us
    ppermute x1, starting transfers between devices, gather_rows(): a3 = lax.ppermute(unit, 'x', bwd)  56.1 us
    ppermute x6, waiting for transfers between devices, gather_z(): down = lax.ppermute(down, 'z', ring_of(8, -1))  29.7 us
    ppermute x2, waiting for transfers between devices, product(): away = lax.ppermute(part[:, 256:].astype(jnp.bfloat16), 'yhi', SWAP)  27.3 us
  transfers between devices with their start and end apart: 30, of which 14 were waited for; matrix products, arithmetic and copies ran while one was open for 1% of the time, Pallas kernels for 0%

profile of v1, /device:TPU:2, one launch (start us, length us, event | category | flops | bytes accessed | tf_op | source)
XLA Modules:
  0.0 819.6 jit_solution(11587282415725705780)
XLA Ops:
  2.7 6.4 contribute.1
  9.1 13.8 %all-to-all-start = ((bf16[128,2,8,128]{3,2,1,0:T(8,128)(2,1)}), bf16[128,2,8,128]{3,2,1,0:T(8,128)(2,1)S(1)}, u32[]{:S(2)}, u32[]{:S(2)}) async-start(bf16[128,2,8,128]{3,2,1,0:T(8,128)(2,1)} %bitcast.46), calls=%async_computation | async-start | bytes 1048576 | tf_op jit(solution)/shard_map/all_to_all | solution.py:230
  24.4 565.7 %all-gather.1 = s32[256,1,128]{2,1,0:T(1,128)S(1)} all-gather(s32[1,1,128]{2,1,0:T(1,128)S(1)} %get-tuple-element.23), channel_id=2, replica_groups=mesh['ylo'=2,'x'=4,'z'=8,'core'=2,'yhi'=2] {'ylo','x','z','core','yhi'}, dimensions={0}, use_global_device_ids=true | all-gather | bytes 131584 | tf_op jit(solution)/shard_map/all_gather | solution.py:224
  595.9 3.6 collect.1.first_ref
  599.4 3.0 collective-permute-done.slot_ref
  603.3 16.3 %assemble.1 = (f32[1024,256]{1,0:T(8,128)}, bf16[1024,256]{1,0:T(8,128)(2,1)}, bf16[4,256,512]{2,1,0:T(8,128)(2,1)}, bf16[1024,256]{1,0:T(8,128)(2,1)}) custom-call(s32[3]{0:T(128)} %pad_add_fusion.place_ref, s32[512]{0:T(512)} %reshape.89.mask_ref, s32[256]{0:T(256)} %reshape.90.label_ref, bf16[256,8,128]{2,1,0:T(8,128)(2,1)} %copy-done.2, ...), custom_call_target="tpu_custom_call" | custom-call | tf_op jit(solution)/shard_map/assemble/pallas_call | solution.py:157
  627.0 56.1 %collective-permute-start.12 = (bf16[256,1024]{1,0:T(8,128)(2,1)S(1)}, bf16[256,1024]{1,0:T(8,128)(2,1)S(1)}, u32[]{:S(2)}, u32[]{:S(2)}) collective-permute-start(bf16[256,1024]{1,0:T(8,128)(2,1)S(1)} %pad_maximum_fusion), channel_id=1, source_target_pairs={{0,96},{32,0},{64,32},{96,64},{1,97},{33,1},{65,33},{97,65},{2,98}... | collective-permute-start | bytes 1572872 | tf_op jit(solution)/shard_map/ppermute | solution.py:193
  686.0 7.8 collective-permute-done.11
  693.8 3.0 collective-permute-start.14
  700.0 7.2 collective-permute-done.14
  707.2 3.2 collective-permute-start.16
  710.5 3.4 collective-permute-start.8
  714.0 4.7 collective-permute-done.15
  718.8 2.8 collective-permute-done.7
  731.3 13.7 %collective-permute-done.18 = bf16[1024,256]{1,0:T(8,128)(2,1)S(1)} collective-permute-done((bf16[1024,256]{1,0:T(8,128)(2,1)S(1)}, bf16[1024,256]{1,0:T(8,128)(2,1)S(1)}, u32[]{:S(2)}, u32[]{:S(2)}) %collective-permute-start.18) | collective-permute-done | bytes 524320 | tf_op jit(solution)/shard_map/ppermute | solution.py:213
  747.3 11.1 %collective-permute-done.19 = bf16[1024,256]{1,0:T(8,128)(2,1)S(1)} collective-permute-done((bf16[1024,256]{1,0:T(8,128)(2,1)S(1)}, bf16[1024,256]{1,0:T(8,128)(2,1)S(1)}, u32[]{:S(2)}, u32[]{:S(2)}) %collective-permute-start.19) | collective-permute-done | bytes 524320 | tf_op jit(solution)/shard_map/ppermute | solution.py:181
  758.4 2.7 collective-permute-start.20
  761.2 9.7 %collective-permute-done.20 = bf16[1024,256]{1,0:T(8,128)(2,1)S(1)} collective-permute-done((bf16[1024,256]{1,0:T(8,128)(2,1)S(1)}, bf16[1024,256]{1,0:T(8,128)(2,1)S(1)}, u32[]{:S(2)}, u32[]{:S(2)}) %collective-permute-start.20) | collective-permute-done | bytes 524320 | tf_op jit(solution)/shard_map/ppermute | solution.py:181
  770.9 3.7 collective-permute-start.21
  774.6 8.8 %collective-permute-done.21 = bf16[1024,256]{1,0:T(8,128)(2,1)S(1)} collective-permute-done((bf16[1024,256]{1,0:T(8,128)(2,1)S(1)}, bf16[1024,256]{1,0:T(8,128)(2,1)S(1)}, u32[]{:S(2)}, u32[]{:S(2)}) %collective-permute-start.21) | collective-permute-done | bytes 524320 | tf_op jit(solution)/shard_map/ppermute | solution.py:181
  783.4 3.8 collective-permute-start.26
  787.5 3.6 collective-permute-done.26
  791.1 3.8 collective-permute-done.25
  804.5 13.7 %collective-permute-done.28 = bf16[1024,256]{1,0:T(8,128)(2,1)S(1)} collective-permute-done((bf16[1024,256]{1,0:T(8,128)(2,1)S(1)}, bf16[1024,256]{1,0:T(8,128)(2,1)S(1)}, u32[]{:S(2)}, u32[]{:S(2)}) %collective-permute-start.28) | collective-permute-done | bytes 524320 | tf_op jit(solution)/shard_map/ppermute | solution.py:213
  (101 shorter events, 47.0 us)
Async XLA Ops:
  9.1 581.1 %all-to-all-start = ((bf16[128,2,8,128]{3,2,1,0:T(8,128)(2,1)}), bf16[128,2,8,128]{3,2,1,0:T(8,128)(2,1)S(1)}, u32[]{:S(2)}, u32[]{:S(2)}) async-start(bf16[128,2,8,128]{3,2,1,0:T(8,128)(2,1)} %bitcast.46), calls=%async_computation | async-start | bytes 1048576 | tf_op jit(solution)/shard_map/all_to_all | solution.py:230
  590.3 12.2 %collective-permute-start = (bf16[256,8,128]{2,1,0:T(8,128)(2,1)S(1)}, bf16[256,8,128]{2,1,0:T(8,128)(2,1)S(1)}, u32[]{:S(2)}, u32[]{:S(2)}) collective-permute-start(bf16[256,8,128]{2,1,0:T(8,128)(2,1)S(1)} %bitcast.44), channel_id=1, source_target_pairs={{0,1},{1,0},{2,3},{3,2},{4,5},{5,4},{6,7},{7,6},{8,9},{9,8},{10,11... | collective-permute-start | bytes 1572872 | tf_op jit(solution)/shard_map/ppermute | solution.py:246
  620.8 62.9 %collective-permute-start.1 = (bf16[1024,256]{1,0:T(8,128)(2,1)}, bf16[1024,256]{1,0:T(8,128)(2,1)S(1)}, u32[]{:S(2)}, u32[]{:S(2)}) collective-permute-start(bf16[1024,256]{1,0:T(8,128)(2,1)} %get-tuple-element.8), channel_id=1, source_target_pairs={{0,28},{4,0},{8,4},{12,8},{16,12},{20,16},{24,20},{28,24},{1,29},{... | collective-permute-start | bytes 1572872 | tf_op jit(solution)/shard_map/ppermute | solution.py:181
  620.9 64.3 %collective-permute-start.4 = (bf16[1024,256]{1,0:T(8,128)(2,1)}, bf16[1024,256]{1,0:T(8,128)(2,1)S(1)}, u32[]{:S(2)}, u32[]{:S(2)}) collective-permute-start(bf16[1024,256]{1,0:T(8,128)(2,1)} %get-tuple-element.8), channel_id=1, source_target_pairs={{0,4},{4,8},{8,12},{12,16},{16,20},{20,24},{24,28},{28,0},{1,5},{5... | collective-permute-start | bytes 1572872 | tf_op jit(solution)/shard_map/ppermute | solution.py:180
  623.0 63.0 %collective-permute-start.10 = (bf16[256,1024]{1,0:T(8,128)(2,1)S(1)}, bf16[256,1024]{1,0:T(8,128)(2,1)S(1)}, u32[]{:S(2)}, u32[]{:S(2)}) collective-permute-start(bf16[256,1024]{1,0:T(8,128)(2,1)S(1)} %pad_maximum_fusion), channel_id=1, source_target_pairs={{0,128},{128,0},{1,129},{129,1},{2,130},{130,2},{3,131},{131,3},{4... | collective-permute-start | bytes 1572872 | tf_op jit(solution)/shard_map/ppermute | solution.py:191
  624.3 69.6 %collective-permute-start.11 = (bf16[256,1024]{1,0:T(8,128)(2,1)S(1)}, bf16[256,1024]{1,0:T(8,128)(2,1)S(1)}, u32[]{:S(2)}, u32[]{:S(2)}) collective-permute-start(bf16[256,1024]{1,0:T(8,128)(2,1)S(1)} %pad_maximum_fusion), channel_id=1, source_target_pairs={{0,32},{32,64},{64,96},{96,0},{1,33},{33,65},{65,97},{97,1},{2,34}... | collective-permute-start | bytes 1572872 | tf_op jit(solution)/shard_map/ppermute | solution.py:192
  627.0 69.9 %collective-permute-start.12 = (bf16[256,1024]{1,0:T(8,128)(2,1)S(1)}, bf16[256,1024]{1,0:T(8,128)(2,1)S(1)}, u32[]{:S(2)}, u32[]{:S(2)}) collective-permute-start(bf16[256,1024]{1,0:T(8,128)(2,1)S(1)} %pad_maximum_fusion), channel_id=1, source_target_pairs={{0,96},{32,0},{64,32},{96,64},{1,97},{33,1},{65,33},{97,65},{2,98}... | collective-permute-start | bytes 1572872 | tf_op jit(solution)/shard_map/ppermute | solution.py:193
  683.7 13.7 %collective-permute-start.2 = (bf16[1024,256]{1,0:T(8,128)(2,1)S(1)}, bf16[1024,256]{1,0:T(8,128)(2,1)S(1)}, u32[]{:S(2)}, u32[]{:S(2)}) collective-permute-start(bf16[1024,256]{1,0:T(8,128)(2,1)S(1)} %collective-permute-done.1), channel_id=1, source_target_pairs={{0,28},{4,0},{8,4},{12,8},{16,12},{20,16},{24,20},{28,24},{1,29},{... | collective-permute-start | bytes 1572872 | tf_op jit(solution)/shard_map/ppermute | solution.py:181
  685.1 14.7 %collective-permute-start.5 = (bf16[1024,256]{1,0:T(8,128)(2,1)S(1)}, bf16[1024,256]{1,0:T(8,128)(2,1)S(1)}, u32[]{:S(2)}, u32[]{:S(2)}) collective-permute-start(bf16[1024,256]{1,0:T(8,128)(2,1)S(1)} %collective-permute-done.4), channel_id=1, source_target_pairs={{0,4},{4,8},{8,12},{12,16},{16,20},{20,24},{24,28},{28,0},{1,5},{5... | collective-permute-start | bytes 1572872 | tf_op jit(solution)/shard_map/ppermute | solution.py:180
  686.0 24.4 %collective-permute-start.13 = (bf16[256,1024]{1,0:T(8,128)(2,1)S(1)}, bf16[256,1024]{1,0:T(8,128)(2,1)S(1)}, u32[]{:S(2)}, u32[]{:S(2)}) collective-permute-start(bf16[256,1024]{1,0:T(8,128)(2,1)S(1)} %collective-permute-done.10), channel_id=1, source_target_pairs={{0,32},{32,64},{64,96},{96,0},{1,33},{33,65},{65,97},{97,1},{2,34}... | collective-permute-start | bytes 1572872 | tf_op jit(solution)/shard_map/ppermute | solution.py:194
  693.8 13.3 %collective-permute-start.14 = (bf16[256,1024]{1,0:T(8,128)(2,1)S(1)}, bf16[256,1024]{1,0:T(8,128)(2,1)S(1)}, u32[]{:S(2)}, u32[]{:S(2)}) collective-permute-start(bf16[256,1024]{1,0:T(8,128)(2,1)S(1)} %collective-permute-done.10), channel_id=1, source_target_pairs={{0,96},{32,0},{64,32},{96,64},{1,97},{33,1},{65,33},{97,65},{2,98}... | collective-permute-start | bytes 1572872 | tf_op jit(solution)/shard_map/ppermute | solution.py:195
  696.9 21.8 %collective-permute-start.15 = (bf16[256,1024]{1,0:T(8,128)(2,1)S(1)}, bf16[256,1024]{1,0:T(8,128)(2,1)S(1)}, u32[]{:S(2)}, u32[]{:S(2)}) collective-permute-start(bf16[256,1024]{1,0:T(8,128)(2,1)S(1)} %collective-permute-done.11), channel_id=1, source_target_pairs={{0,32},{32,64},{64,96},{96,0},{1,33},{33,65},{65,97},{97,1},{2,34}... | collective-permute-start | bytes 1572872 | tf_op jit(solution)/shard_map/ppermute | solution.py:196
  697.4 13.1 %collective-permute-start.3 = (bf16[1024,256]{1,0:T(8,128)(2,1)S(1)}, bf16[1024,256]{1,0:T(8,128)(2,1)S(1)}, u32[]{:S(2)}, u32[]{:S(2)}) collective-permute-start(bf16[1024,256]{1,0:T(8,128)(2,1)S(1)} %collective-permute-done.2), channel_id=1, source_target_pairs={{0,28},{4,0},{8,4},{12,8},{16,12},{20,16},{24,20},{28,24},{1,29},{... | collective-permute-start | bytes 1572872 | tf_op jit(solution)/shard_map/ppermute | solution.py:181
  699.9 14.0 %collective-permute-start.6 = (bf16[1024,256]{1,0:T(8,128)(2,1)S(1)}, bf16[1024,256]{1,0:T(8,128)(2,1)S(1)}, u32[]{:S(2)}, u32[]{:S(2)}) collective-permute-start(bf16[1024,256]{1,0:T(8,128)(2,1)S(1)} %collective-permute-done.5), channel_id=1, source_target_pairs={{0,4},{4,8},{8,12},{12,16},{16,20},{20,24},{24,28},{28,0},{1,5},{5... | collective-permute-start | bytes 1572872 | tf_op jit(solution)/shard_map/ppermute | solution.py:180
  707.2 14.7 %collective-permute-start.16 = (bf16[256,1024]{1,0:T(8,128)(2,1)S(1)}, bf16[256,1024]{1,0:T(8,128)(2,1)S(1)}, u32[]{:S(2)}, u32[]{:S(2)}) collective-permute-start(bf16[256,1024]{1,0:T(8,128)(2,1)S(1)} %collective-permute-done.14), channel_id=1, source_target_pairs={{0,96},{32,0},{64,32},{96,64},{1,97},{33,1},{65,33},{97,65},{2,98}... | collective-permute-start | bytes 1572872 | tf_op jit(solution)/shard_map/ppermute | solution.py:197
  710.5 8.3 %collective-permute-start.8 = (bf16[512,256]{1,0:T(8,128)(2,1)S(1)}, bf16[512,256]{1,0:T(8,128)(2,1)S(1)}, u32[]{:S(2)}, u32[]{:S(2)}) collective-permute-start(bf16[512,256]{1,0:T(8,128)(2,1)S(1)} %slice.45), channel_id=1, source_target_pairs={{0,28},{4,0},{8,4},{12,8},{16,12},{20,16},{24,20},{28,24},{1,29},{... | collective-permute-start | bytes 786440 | tf_op jit(solution)/shard_map/ppermute | solution.py:184
  729.4 15.6 %collective-permute-start.18 = (bf16[1024,256]{1,0:T(8,128)(2,1)S(1)}, bf16[1024,256]{1,0:T(8,128)(2,1)S(1)}, u32[]{:S(2)}, u32[]{:S(2)}) collective-permute-start(bf16[1024,256]{1,0:T(8,128)(2,1)S(1)} %slice.83), channel_id=1, source_target_pairs={{0,1},{1,0},{2,3},{3,2},{4,5},{5,4},{6,7},{7,6},{8,9},{9,8},{10,11... | collective-permute-start | bytes 1572872 | tf_op jit(solution)/shard_map/ppermute | solution.py:213
  745.2 13.2 %collective-permute-start.19 = (bf16[1024,256]{1,0:T(8,128)(2,1)S(1)}, bf16[1024,256]{1,0:T(8,128)(2,1)S(1)}, u32[]{:S(2)}, u32[]{:S(2)}) collective-permute-start(bf16[1024,256]{1,0:T(8,128)(2,1)S(1)} %get-tuple-element.15), channel_id=1, source_target_pairs={{0,28},{4,0},{8,4},{12,8},{16,12},{20,16},{24,20},{28,24},{1,29},{... | collective-permute-start | bytes 1572872 | tf_op jit(solution)/shard_map/ppermute | solution.py:181
  746.8 14.4 %collective-permute-start.22 = (bf16[1024,256]{1,0:T(8,128)(2,1)S(1)}, bf16[1024,256]{1,0:T(8,128)(2,1)S(1)}, u32[]{:S(2)}, u32[]{:S(2)}) collective-permute-start(bf16[1024,256]{1,0:T(8,128)(2,1)S(1)} %get-tuple-element.15), channel_id=1, source_target_pairs={{0,4},{4,8},{8,12},{12,16},{16,20},{20,24},{24,28},{28,0},{1,5},{5... | collective-permute-start | bytes 1572872 | tf_op jit(solution)/shard_map/ppermute | solution.py:180
  758.4 12.4 %collective-permute-start.20 = (bf16[1024,256]{1,0:T(8,128)(2,1)S(1)}, bf16[1024,256]{1,0:T(8,128)(2,1)S(1)}, u32[]{:S(2)}, u32[]{:S(2)}) collective-permute-start(bf16[1024,256]{1,0:T(8,128)(2,1)S(1)} %collective-permute-done.19), channel_id=1, source_target_pairs={{0,28},{4,0},{8,4},{12,8},{16,12},{20,16},{24,20},{28,24},{1,29},{... | collective-permute-start | bytes 1572872 | tf_op jit(solution)/shard_map/ppermute | solution.py:181
  761.1 13.4 %collective-permute-start.23 = (bf16[1024,256]{1,0:T(8,128)(2,1)S(1)}, bf16[1024,256]{1,0:T(8,128)(2,1)S(1)}, u32[]{:S(2)}, u32[]{:S(2)}) collective-permute-start(bf16[1024,256]{1,0:T(8,128)(2,1)S(1)} %collective-permute-done.22), channel_id=1, source_target_pairs={{0,4},{4,8},{8,12},{12,16},{16,20},{20,24},{24,28},{28,0},{1,5},{5... | collective-permute-start | bytes 1572872 | tf_op jit(solution)/shard_map/ppermute | solution.py:180
  770.9 12.5 %collective-permute-start.21 = (bf16[1024,256]{1,0:T(8,128)(2,1)S(1)}, bf16[1024,256]{1,0:T(8,128)(2,1)S(1)}, u32[]{:S(2)}, u32[]{:S(2)}) collective-permute-start(bf16[1024,256]{1,0:T(8,128)(2,1)S(1)} %collective-permute-done.20), channel_id=1, source_target_pairs={{0,28},{4,0},{8,4},{12,8},{16,12},{20,16},{24,20},{28,24},{1,29},{... | collective-permute-start | bytes 1572872 | tf_op jit(solution)/shard_map/ppermute | solution.py:181
  774.6 12.6 %collective-permute-start.24 = (bf16[1024,256]{1,0:T(8,128)(2,1)S(1)}, bf16[1024,256]{1,0:T(8,128)(2,1)S(1)}, u32[]{:S(2)}, u32[]{:S(2)}) collective-permute-start(bf16[1024,256]{1,0:T(8,128)(2,1)S(1)} %collective-permute-done.23), channel_id=1, source_target_pairs={{0,4},{4,8},{8,12},{12,16},{16,20},{20,24},{24,28},{28,0},{1,5},{5... | collective-permute-start | bytes 1572872 | tf_op jit(solution)/shard_map/ppermute | solution.py:180
  802.6 15.6 %collective-permute-start.28 = (bf16[1024,256]{1,0:T(8,128)(2,1)S(1)}, bf16[1024,256]{1,0:T(8,128)(2,1)S(1)}, u32[]{:S(2)}, u32[]{:S(2)}) collective-permute-start(bf16[1024,256]{1,0:T(8,128)(2,1)S(1)} %slice.82), channel_id=1, source_target_pairs={{0,1},{1,0},{2,3},{3,2},{4,5},{5,4},{6,7},{7,6},{8,9},{9,8},{10,11... | collective-permute-start | bytes 1572872 | tf_op jit(solution)/shard_map/ppermute | solution.py:213
  (9 other events, 57.8 us)

commit v2 on v1

--- a/solution.py
+++ b/solution.py
@@ -27,9 +27,11 @@
     return out
 
 
-def contribute_kernel(pos_ref, left_ref, right_ref, weight_ref, out_ref):
-    out_ref[...] = jnp.zeros_like(out_ref)
+def contribute_kernel(pos_ref, block_ref, left_ref, right_ref, weight_ref, out_ref):
+    out_ref[...] = jnp.full(out_ref.shape, 32.0, out_ref.dtype)
     group = lanes_group((8, 128))
+    sub = lax.broadcasted_iota(jnp.int32, (8, 128), 0)
+    lane = lax.broadcasted_iota(jnp.int32, (8, 128), 1)
 
     def body(g, carry):
         base = pl.multiple_of(g * 8, 8)
@@ -50,78 +52,79 @@
                     rows[k] if k == t else pltpu.roll(rows[k], (32 * (k - t)) % 128, 1)
                     for k in range(4)
                 ]
-                out_ref[pos_ref[base + half * 4 + t]] = pick(rows, group).astype(jnp.bfloat16)
+                task = base + half * 4 + t
+                owner, slot = pos_ref[task] >> 1, pos_ref[task] & 1
+                out_ref[owner * 3 + slot] = pick(rows, group).astype(jnp.bfloat16)
+                block = block_ref[task]
+                high = (block >> 4).astype(jnp.float32)
+                low = (block & 15).astype(jnp.float32)
+                tag = out_ref[owner * 3 + 2].astype(jnp.float32)
+                tag = jnp.where(sub == slot, jnp.where(lane == 0, high, low), tag)
+                out_ref[owner * 3 + 2] = tag.astype(jnp.bfloat16)
         return carry
 
     lax.fori_loop(0, 16, body, 0)
 
 
-def accumulate(acc_ref, label_ref, slot_ref):
-    acc_ref[...] = jnp.zeros_like(acc_ref)
-
+def accumulate(acc_ref, label_ref, slot_ref, stride):
     def body(s, carry):
         for u in range(8):
             n = label_ref[s * 8 + u]
-            acc_ref[n] = acc_ref[n] + slot_ref[s * 8 + u].astype(jnp.float32)
+            at = (s * 4 + u // 2) * stride + u % 2
+            acc_ref[n] = acc_ref[n] + slot_ref[at].astype(jnp.float32)
         return carry
 
-    lax.fori_loop(0, slot_ref.shape[0] // 8, body, 0)
+    lax.fori_loop(0, label_ref.shape[0] // 8, body, 0)
 
 
 def collect_kernel(label_ref, slot_ref, acc_ref):
-    accumulate(acc_ref, label_ref, slot_ref)
+    acc_ref[...] = jnp.zeros_like(acc_ref)
+    accumulate(acc_ref, label_ref, slot_ref, 3)
 
 
 def assemble_kernel(
     place_ref, mask_ref, label_ref, slot_ref, first_ref, core_ref,
-    ks_ref, own_ref, panel_ref, pattern_ref, second_ref, *, scale,
+    ks_ref, own_ref, panel_ref, pattern_ref, acc_ref, *, scale,
 ):
-    accumulate(second_ref, label_ref, slot_ref)
+    acc_ref[...] = first_ref[...]
+    accumulate(acc_ref, label_ref, slot_ref, 2)
     row, col, half_own = place_ref[0], place_ref[1], place_ref[2]
     group = lanes_group((8, 128))
     sub = lax.broadcasted_iota(jnp.int32, (8, 128), 0)
     lane = lax.broadcasted_iota(jnp.int32, (8, 128), 1)
+    slant = sub - lane
 
     def body(i, carry):
         r0 = pl.multiple_of(i * 32, 32)
         quarter = i // 8
         q0 = pl.multiple_of((i % 8) * 32, 32)
-        block_row = row * 32 + i
-        for jt in range(4):
-            half = jt // 2
-            blocks, marks = [], []
-            for j in range(4):
-                n = i * 16 + jt * 4 + j
-                blocks.append(first_ref[n] + second_ref[n])
-                on = (mask_ref[n] != 0) | (block_row == col * 16 + jt * 4 + j)
-                marks.append(jnp.full((8, 128), on.astype(jnp.float32)))
-            pat = pick(marks, group)
-            ks_rows, x_rows = [], []
-            for t in range(4):
-                turned = [
-                    blocks[j] if j == t else pltpu.roll(blocks[j], (32 * (j - t)) % 128, 1)
-                    for j in range(4)
-                ]
-                ks = core_ref[pl.ds(r0 + 8 * t, 8), jt * 128 : jt * 128 + 128] + pick(turned, group)
-                identity = (
-                    row * 1024 + r0 + 8 * t + sub == col * 512 + jt * 128 + lane
-                ).astype(jnp.float32)
-                ks_rows.append(ks)
-                x_rows.append(pat * (0.5 * identity - scale * ks))
-            x = jnp.concatenate(x_rows, axis=0).astype(jnp.bfloat16)
-            inner = (jt % 2) * 128
-            other = half != half_own
-            at = pl.multiple_of(other.astype(jnp.int32) * 256 + inner, 128)
-            panel_ref[quarter, pl.ds(q0, 32), pl.ds(at, 128)] = x
-
-            @pl.when(jnp.logical_not(other))
-            def _():
-                ks_ref[pl.ds(r0, 32), inner : inner + 128] = jnp.concatenate(ks_rows, axis=0)
-                own_ref[pl.ds(r0, 32), inner : inner + 128] = x
-                pattern_ref[pl.ds(r0, 32), inner : inner + 128] = jnp.concatenate(
-                    [pat] * 4, axis=0
-                ).astype(jnp.bfloat16)
-
+        for side in range(2):
+            half = half_own if side == 0 else 1 - half_own
+            for jt in range(2):
+                n = i * 16 + half * 8 + jt * 4
+                blocks = [acc_ref[n + j] for j in range(4)]
+                pat = pick([jnp.full((8, 128), mask_ref[n + j]) for j in range(4)], group)
+                c0 = pl.multiple_of(half * 256 + jt * 128, 128)
+                gap = col * 512 + c0 - row * 1024 - r0
+                ks_rows, x_rows = [], []
+                for t in range(4):
+                    turned = [
+                        blocks[j] if j == t else pltpu.roll(blocks[j], (32 * (j - t)) % 128, 1)
+                        for j in range(4)
+                    ]
+                    ks = core_ref[pl.ds(r0 + 8 * t, 8), pl.ds(c0, 128)] + pick(turned, group)
+                    identity = jnp.where(slant == gap - 8 * t, 0.5, 0.0)
+                    ks_rows.append(ks)
+                    x_rows.append(pat * (identity - scale * ks))
+                x = jnp.concatenate(x_rows, axis=0).astype(jnp.bfloat16)
+                panel_ref[quarter, pl.ds(q0, 32), side * 256 + jt * 128 : side * 256 + jt * 128 + 128] = x
+                if side == 0:
+                    at = slice(jt * 128, jt * 128 + 128)
+                    ks_ref[pl.ds(r0, 32), at] = jnp.concatenate(ks_rows, axis=0)
+                    own_ref[pl.ds(r0, 32), at] = x
+                    pattern_ref[pl.ds(r0, 32), at] = jnp.concatenate([pat] * 4, axis=0).astype(
+                        jnp.bfloat16
+                    )
         return carry
 
     lax.fori_loop(0, 32, body, 0)
@@ -131,15 +134,15 @@
 SMEM = pl.BlockSpec(memory_space=pltpu.SMEM)
 
 
-def contribute(pos, left, right, weight):
+def contribute(pos, block, left, right, weight):
     tasks = left.shape[0]
     return pl.pallas_call(
         contribute_kernel,
-        out_shape=jax.ShapeDtypeStruct((2 * tasks, 8, 128), jnp.bfloat16),
-        in_specs=[SMEM, VMEM, VMEM, VMEM],
+        out_shape=jax.ShapeDtypeStruct((3 * tasks, 8, 128), jnp.bfloat16),
+        in_specs=[SMEM, SMEM, VMEM, VMEM, VMEM],
         out_specs=VMEM,
         name="contribute",
-    )(pos, left, right, weight)
+    )(pos, block, left, right, weight)
 
 
 def collect(labels, slots):
@@ -217,37 +220,28 @@
 def local(basis_left, basis_right, grid_weight, task_owner, task_block, core_matrix, block_mask):
     ylo, x, z, core, yhi = (lax.axis_index(a) for a in AXES)
     row, col = ylo * 4 + x, z * 2 + core
-    owner = row * 16 + col
     tasks = basis_left.shape[0]
 
     target = task_owner[:, 0]
-    tags = lax.all_gather(target * 512 + task_block, AXES, axis=0, tiled=False)
     order = jnp.arange(tasks, dtype=jnp.int32)
     earlier = (target[:, None] == target[None, :]) & (order[None, :] < order[:, None])
     pos = target * 2 + jnp.sum(earlier.astype(jnp.int32), axis=1)
 
-    outgoing = contribute(pos, basis_left, basis_right, grid_weight)
+    outgoing = contribute(pos, task_block, basis_left, basis_right, grid_weight)
     arrived = lax.all_to_all(
-        outgoing.reshape(tasks, 2, 8, 128), AXES[:4], split_axis=0, concat_axis=0, tiled=True
-    ).reshape(2 * tasks, 8, 128)
-
-    mine = tags // 512 == owner
-    first = jnp.min(jnp.where(mine, order[None, :], tasks), axis=1, keepdims=True)
-    last = jnp.max(jnp.where(mine, order[None, :], -1), axis=1, keepdims=True)
-    block = tags % 512
-    label0 = jnp.sum(jnp.where(order[None, :] == first, block, 0), axis=1)
-    label1 = jnp.sum(jnp.where(order[None, :] == last, block, 0), axis=1)
-    label0 = jnp.where(last[:, 0] >= 0, label0, 512)
-    label1 = jnp.where(last[:, 0] > first[:, 0], label1, 512)
-    labels = jnp.stack([label0, label1], axis=1).reshape(tasks, 2, 2)
-    labels_own = lax.dynamic_index_in_dim(labels, yhi, 1, keepdims=False).reshape(-1)
-    labels_far = lax.dynamic_index_in_dim(labels, 1 - yhi, 1, keepdims=False).reshape(-1)
-
-    arrived_far = lax.ppermute(arrived, "yhi", SWAP)
-    collected = collect(labels_own, arrived)
+        outgoing.reshape(tasks, 3, 8, 128), AXES[:4], split_axis=0, concat_axis=0, tiled=True
+    )
+    tag = arrived[:, 2, :2, :2].astype(jnp.float32)
+    labels = jnp.minimum(tag[:, :, 0] * 16 + tag[:, :, 1], 512.0).astype(jnp.int32).reshape(-1)
+    labels_far = lax.ppermute(labels, "yhi", SWAP)
+    arrived_far = lax.ppermute(arrived[:, :2].reshape(2 * tasks, 8, 128), "yhi", SWAP)
+    collected = collect(labels, arrived.reshape(3 * tasks, 8, 128))
+    block_rows = row * 32 + jnp.arange(32, dtype=jnp.int32)
+    block_cols = col * 16 + jnp.arange(16, dtype=jnp.int32)
+    mask = (block_mask != 0) | (block_rows[:, None] == block_cols[None, :])
     place = jnp.stack([row, col, yhi]).astype(jnp.int32)
     ks_out, own, panel, pattern = assemble(
-        place, block_mask.reshape(-1), labels_far, arrived_far, collected, core_matrix
+        place, mask.astype(jnp.float32).reshape(-1), labels_far, arrived_far, collected, core_matrix
     )
 
     keep = lax.dynamic_index_in_dim(panel, 2 * core + yhi, 0, keepdims=False)

time: 829 us -> 227 us (0.27)
  blocking collectives: 566 us -> 0 us
  starting transfers between devices: 109 us -> 55.6 us
  waiting for transfers between devices: 95.2 us -> 125 us
    all_gather x1 -> x0, blocking collectives: 566 us -> none  [local(): tags = lax.all_gather(target * 512 + task_block, AXES, axis=0, tiled=False)]
    ppermute x1, starting transfers between devices: 56.1 us -> 0.83 us  [gather_rows(): a3 = lax.ppermute(unit, 'x', bwd)]
    all_to_all x1, waiting for transfers between devices: 0.01 us -> 22.2 us  [local(): lax.all_to_all(outgoing.reshape(tasks, 3, 8, 128), AXES[:4], split_axis=0...]
    ppermute x6, waiting for transfers between devices: 29.7 us -> 44.7 us  [gather_z(): down = lax.ppermute(down, 'z', ring_of(8, -1))]
  transfers between devices with their start and end apart: 30 -> 31, of which waited for: 14 -> 17; matrix products, arithmetic and copies ran while one was open for 1% -> 3% of each run, Pallas kernels for 0% -> 2%
where the time goes in v2:
time: 227 us; the launch traced here: 224 us
  waiting for transfers between devices  125 us (55%)
  starting transfers between devices  55.6 us (24%)
  Pallas kernels  19.9 us (9%)
  matrix products  9.31 us (4%)
  other arithmetic  7.05 us (3%)
  local copies, waits for them, and re-layouts  6.22 us (3%)
    ppermute x6, waiting for transfers between devices, gather_z(): down = lax.ppermute(down, 'z', ring_of(8, -1))  44.7 us
    ppermute x2, waiting for transfers between devices, product(): away = lax.ppermute(part[:, 256:].astype(jnp.bfloat16), 'yhi', SWAP)  25.1 us
    all_to_all x1, waiting for transfers between devices, local(): lax.all_to_all(outgoing.reshape(tasks, 3, 8, 128), AXES[:4], split_axis=0...  22.2 us
    all_to_all x1, starting transfers between devices, local(): lax.all_to_all(outgoing.reshape(tasks, 3, 8, 128), AXES[:4], split_axis=0...  13.8 us
    ppermute x6, starting transfers between devices, gather_z(): down = lax.ppermute(down, 'z', ring_of(8, -1))  11.8 us
    pallas_call x1, Pallas kernels, assemble(): pl.pallas_call(functools.partial(assemble_kernel, scale=COUPLING / math.s...  9.27 us
    ppermute x1, waiting for transfers between devices, gather_rows(): a2 = lax.ppermute(a1, 'x', fwd)  8.48 us
    ppermute x2, waiting for transfers between devices, gather_z(): top = lax.ppermute(up[:512], 'z', ring_of(8, 1))  7.59 us
  transfers between devices with their start and end apart: 31, of which 17 were waited for; matrix products, arithmetic and copies ran while one was open for 3% of the time, Pallas kernels for 2%

profile of v2, /device:TPU:2, one launch (start us, length us, event | category | flops | bytes accessed | tf_op | source)
XLA Modules:
  0.0 224.5 jit_solution(10316377203951423791)
XLA Ops:
  2.7 7.0 %contribute.1 = bf16[384,8,128]{2,1,0:T(8,128)(2,1)} custom-call(s32[128]{0:T(128)} %multiply_add_fusion.pos_ref, s32[128]{0:T(128)} %block_ref.1, bf16[128,32,128]{2,1,0:T(8,128)(2,1)} %left_ref.1, bf16[128,32,128]{2,1,0:T(8,128)(2,1)} %right_ref.1, f32[128,128]{1,0:T(8,128)} %weight_ref.1), custom_call_target="tpu_custom_call" | custom-call | tf_op jit(solution)/shard_map/contribute/pallas_call | solution.py:139
  9.7 13.8 %all-to-all-start = ((bf16[128,3,8,128]{3,2,1,0:T(8,128)(2,1)}), bf16[128,3,8,128]{3,2,1,0:T(8,128)(2,1)S(1)}, u32[]{:S(2)}, u32[]{:S(2)}) async-start(bf16[128,3,8,128]{3,2,1,0:T(8,128)(2,1)} %bitcast.43), calls=%async_computation | async-start | bytes 1572864 | tf_op jit(solution)/shard_map/all_to_all | solution.py:231
  23.6 22.2 %all-to-all-done = bf16[128,3,8,128]{3,2,1,0:T(8,128)(2,1)S(1)} async-done(((bf16[128,3,8,128]{3,2,1,0:T(8,128)(2,1)}), bf16[128,3,8,128]{3,2,1,0:T(8,128)(2,1)S(1)}, u32[]{:S(2)}, u32[]{:S(2)}) %all-to-all-start) | async-done | bytes 786464 | tf_op jit(solution)/shard_map/all_to_all | solution.py:231
  45.8 3.0 %collective-permute-start.1 = (bf16[256,8,128]{2,1,0:T(8,128)(2,1)S(1)}, bf16[256,8,128]{2,1,0:T(8,128)(2,1)S(1)}, u32[]{:S(2)}, u32[]{:S(2)}) collective-permute-start(bf16[256,8,128]{2,1,0:T(8,128)(2,1)S(1)} %bitcast.44), channel_id=1, source_target_pairs={{0,1},{1,0},{2,3},{3,2},{4,5},{5,4},{6,7},{7,6},{8,9},{9,8},{10,11... | collective-permute-start | bytes 1572872 | tf_op jit(solution)/shard_map/ppermute | solution.py:237
  53.5 3.6 %collect.1.first_ref = f32[520,8,128]{2,1,0:T(8,128)} custom-call(s32[256]{0:T(256)} %copy-done.4, bf16[384,8,128]{2,1,0:T(8,128)(2,1)} %bitcast.38), custom_call_target="tpu_custom_call" | custom-call | flops 1048576 | bytes 8388608 | tf_op jit(solution)/shard_map/collect/pallas_call | solution.py:149
  57.2 4.5 %collective-permute-done.label_ref = s32[256]{0:T(256)S(1)} collective-permute-done((s32[256]{0:T(256)S(1)}, s32[256]{0:T(256)S(1)}, u32[]{:S(2)}, u32[]{:S(2)}) %collective-permute-start) | collective-permute-done | bytes 1056 | tf_op jit(solution)/shard_map/ppermute | solution.py:236
  63.0 9.3 %assemble.1 = (f32[1024,256]{1,0:T(8,128)}, bf16[1024,256]{1,0:T(8,128)(2,1)}, bf16[4,256,512]{2,1,0:T(8,128)(2,1)}, bf16[1024,256]{1,0:T(8,128)(2,1)}) custom-call(s32[3]{0:T(128)} %pad_add_fusion.place_ref, f32[512]{0:T(512)} %reshape.48.mask_ref, s32[256]{0:T(256)} %copy-done.5, bf16[256,8,128]{2,1,0:T(8,128)(2,1)} %copy-done.2, ...), custom_call_target="tpu_custom_call" | custom-call | tf_op jit(solution)/shard_map/assemble/pallas_call | solution.py:160
  81.7 6.7 %collective-permute-done.2 = bf16[1024,256]{1,0:T(8,128)(2,1)S(1)} collective-permute-done((bf16[1024,256]{1,0:T(8,128)(2,1)}, bf16[1024,256]{1,0:T(8,128)(2,1)S(1)}, u32[]{:S(2)}, u32[]{:S(2)}) %collective-permute-start.2) | collective-permute-done | bytes 524320 | tf_op jit(solution)/shard_map/ppermute | solution.py:184
  94.4 7.6 %collective-permute-done.3 = bf16[1024,256]{1,0:T(8,128)(2,1)S(1)} collective-permute-done((bf16[1024,256]{1,0:T(8,128)(2,1)S(1)}, bf16[1024,256]{1,0:T(8,128)(2,1)S(1)}, u32[]{:S(2)}, u32[]{:S(2)}) %collective-permute-start.3) | collective-permute-done | bytes 524320 | tf_op jit(solution)/shard_map/ppermute | solution.py:184
  102.0 3.4 %collective-permute-start.4 = (bf16[1024,256]{1,0:T(8,128)(2,1)S(1)}, bf16[1024,256]{1,0:T(8,128)(2,1)S(1)}, u32[]{:S(2)}, u32[]{:S(2)}) collective-permute-start(bf16[1024,256]{1,0:T(8,128)(2,1)S(1)} %collective-permute-done.3), channel_id=1, source_target_pairs={{0,28},{4,0},{8,4},{12,8},{16,12},{20,16},{24,20},{28,24},{1,29},{... | collective-permute-start | bytes 1572872 | tf_op jit(solution)/shard_map/ppermute | solution.py:184
  107.1 8.5 %collective-permute-done.16 = bf16[256,1024]{1,0:T(8,128)(2,1)S(1)} collective-permute-done((bf16[256,1024]{1,0:T(8,128)(2,1)S(1)}, bf16[256,1024]{1,0:T(8,128)(2,1)S(1)}, u32[]{:S(2)}, u32[]{:S(2)}) %collective-permute-start.16) | collective-permute-done | bytes 524320 | tf_op jit(solution)/shard_map/ppermute | solution.py:199
  115.6 3.6 %collective-permute-start.9 = (bf16[512,256]{1,0:T(8,128)(2,1)S(1)}, bf16[512,256]{1,0:T(8,128)(2,1)S(1)}, u32[]{:S(2)}, u32[]{:S(2)}) collective-permute-start(bf16[512,256]{1,0:T(8,128)(2,1)S(1)} %slice.65), channel_id=1, source_target_pairs={{0,28},{4,0},{8,4},{12,8},{16,12},{20,16},{24,20},{28,24},{1,29},{... | collective-permute-start | bytes 786440 | tf_op jit(solution)/shard_map/ppermute | solution.py:187
  119.5 3.6 %collective-permute-done.9 = bf16[512,256]{1,0:T(8,128)(2,1)S(1)} collective-permute-done((bf16[512,256]{1,0:T(8,128)(2,1)S(1)}, bf16[512,256]{1,0:T(8,128)(2,1)S(1)}, u32[]{:S(2)}, u32[]{:S(2)}) %collective-permute-start.9) | collective-permute-done | bytes 262176 | tf_op jit(solution)/shard_map/ppermute | solution.py:187
  123.1 3.8 %collective-permute-done.8 = bf16[512,256]{1,0:T(8,128)(2,1)S(1)} collective-permute-done((bf16[512,256]{1,0:T(8,128)(2,1)S(1)}, bf16[512,256]{1,0:T(8,128)(2,1)S(1)}, u32[]{:S(2)}, u32[]{:S(2)}) %collective-permute-start.8) | collective-permute-done | bytes 262176 | tf_op jit(solution)/shard_map/ppermute | solution.py:186
  137.7 12.6 %collective-permute-done.19 = bf16[1024,256]{1,0:T(8,128)(2,1)S(1)} collective-permute-done((bf16[1024,256]{1,0:T(8,128)(2,1)S(1)}, bf16[1024,256]{1,0:T(8,128)(2,1)S(1)}, u32[]{:S(2)}, u32[]{:S(2)}) %collective-permute-start.19) | collective-permute-done | bytes 524320 | tf_op jit(solution)/shard_map/ppermute | solution.py:216
  152.8 11.1 %collective-permute-done.20 = bf16[1024,256]{1,0:T(8,128)(2,1)S(1)} collective-permute-done((bf16[1024,256]{1,0:T(8,128)(2,1)S(1)}, bf16[1024,256]{1,0:T(8,128)(2,1)S(1)}, u32[]{:S(2)}, u32[]{:S(2)}) %collective-permute-start.20) | collective-permute-done | bytes 524320 | tf_op jit(solution)/shard_map/ppermute | solution.py:184
  166.0 10.2 %collective-permute-done.21 = bf16[1024,256]{1,0:T(8,128)(2,1)S(1)} collective-permute-done((bf16[1024,256]{1,0:T(8,128)(2,1)S(1)}, bf16[1024,256]{1,0:T(8,128)(2,1)S(1)}, u32[]{:S(2)}, u32[]{:S(2)}) %collective-permute-start.21) | collective-permute-done | bytes 524320 | tf_op jit(solution)/shard_map/ppermute | solution.py:184
  176.2 3.0 %collective-permute-start.22 = (bf16[1024,256]{1,0:T(8,128)(2,1)S(1)}, bf16[1024,256]{1,0:T(8,128)(2,1)S(1)}, u32[]{:S(2)}, u32[]{:S(2)}) collective-permute-start(bf16[1024,256]{1,0:T(8,128)(2,1)S(1)} %collective-permute-done.21), channel_id=1, source_target_pairs={{0,28},{4,0},{8,4},{12,8},{16,12},{20,16},{24,20},{28,24},{1,29},{... | collective-permute-start | bytes 1572872 | tf_op jit(solution)/shard_map/ppermute | solution.py:184
  179.2 9.1 %collective-permute-done.22 = bf16[1024,256]{1,0:T(8,128)(2,1)S(1)} collective-permute-done((bf16[1024,256]{1,0:T(8,128)(2,1)S(1)}, bf16[1024,256]{1,0:T(8,128)(2,1)S(1)}, u32[]{:S(2)}, u32[]{:S(2)}) %collective-permute-start.22) | collective-permute-done | bytes 524320 | tf_op jit(solution)/shard_map/ppermute | solution.py:184
  188.3 3.8 %collective-permute-start.27 = (bf16[512,256]{1,0:T(8,128)(2,1)S(1)}, bf16[512,256]{1,0:T(8,128)(2,1)S(1)}, u32[]{:S(2)}, u32[]{:S(2)}) collective-permute-start(bf16[512,256]{1,0:T(8,128)(2,1)S(1)} %slice.71), channel_id=1, source_target_pairs={{0,28},{4,0},{8,4},{12,8},{16,12},{20,16},{24,20},{28,24},{1,29},{... | collective-permute-start | bytes 786440 | tf_op jit(solution)/shard_map/ppermute | solution.py:187
  192.4 3.6 %collective-permute-done.27 = bf16[512,256]{1,0:T(8,128)(2,1)S(1)} collective-permute-done((bf16[512,256]{1,0:T(8,128)(2,1)S(1)}, bf16[512,256]{1,0:T(8,128)(2,1)S(1)}, u32[]{:S(2)}, u32[]{:S(2)}) %collective-permute-start.27) | collective-permute-done | bytes 262176 | tf_op jit(solution)/shard_map/ppermute | solution.py:187
  196.0 3.8 %collective-permute-done.26 = bf16[512,256]{1,0:T(8,128)(2,1)S(1)} collective-permute-done((bf16[512,256]{1,0:T(8,128)(2,1)S(1)}, bf16[512,256]{1,0:T(8,128)(2,1)S(1)}, u32[]{:S(2)}, u32[]{:S(2)}) %collective-permute-start.26) | collective-permute-done | bytes 262176 | tf_op jit(solution)/shard_map/ppermute | solution.py:186
  207.5 3.0 %collective-permute-start.29 = (bf16[1024,256]{1,0:T(8,128)(2,1)S(1)}, bf16[1024,256]{1,0:T(8,128)(2,1)S(1)}, u32[]{:S(2)}, u32[]{:S(2)}) collective-permute-start(bf16[1024,256]{1,0:T(8,128)(2,1)S(1)} %slice.115), channel_id=1, source_target_pairs={{0,1},{1,0},{2,3},{3,2},{4,5},{5,4},{6,7},{7,6},{8,9},{9,8},{10,11... | collective-permute-start | bytes 1572872 | tf_op jit(solution)/shard_map/ppermute | solution.py:216
  210.5 12.6 %collective-permute-done.29 = bf16[1024,256]{1,0:T(8,128)(2,1)S(1)} collective-permute-done((bf16[1024,256]{1,0:T(8,128)(2,1)S(1)}, bf16[1024,256]{1,0:T(8,128)(2,1)S(1)}, u32[]{:S(2)}, u32[]{:S(2)}) %collective-permute-start.29) | collective-permute-done | bytes 524320 | tf_op jit(solution)/shard_map/ppermute | solution.py:216
  (103 shorter events, 50.1 us)
Async XLA Ops:
  9.7 36.1 %all-to-all-start = ((bf16[128,3,8,128]{3,2,1,0:T(8,128)(2,1)}), bf16[128,3,8,128]{3,2,1,0:T(8,128)(2,1)S(1)}, u32[]{:S(2)}, u32[]{:S(2)}) async-start(bf16[128,3,8,128]{3,2,1,0:T(8,128)(2,1)} %bitcast.43), calls=%async_computation | async-start | bytes 1572864 | tf_op jit(solution)/shard_map/all_to_all | solution.py:231
  45.8 15.8 %collective-permute-start.1 = (bf16[256,8,128]{2,1,0:T(8,128)(2,1)S(1)}, bf16[256,8,128]{2,1,0:T(8,128)(2,1)S(1)}, u32[]{:S(2)}, u32[]{:S(2)}) collective-permute-start(bf16[256,8,128]{2,1,0:T(8,128)(2,1)S(1)} %bitcast.44), channel_id=1, source_target_pairs={{0,1},{1,0},{2,3},{3,2},{4,5},{5,4},{6,7},{7,6},{8,9},{9,8},{10,11... | collective-permute-start | bytes 1572872 | tf_op jit(solution)/shard_map/ppermute | solution.py:237
  51.5 10.2 %collective-permute-start = (s32[256]{0:T(256)S(1)}, s32[256]{0:T(256)S(1)}, u32[]{:S(2)}, u32[]{:S(2)}) collective-permute-start(s32[256]{0:T(256)S(1)} %convert_element_type.47.label_ref), channel_id=1, source_target_pairs={{0,1},{1,0},{2,3},{3,2},{4,5},{5,4},{6,7},{7,6},{8,9},{9,8},{10,11... | collective-permute-start | bytes 3080 | tf_op jit(solution)/shard_map/ppermute | solution.py:236
  73.7 14.7 %collective-permute-start.2 = (bf16[1024,256]{1,0:T(8,128)(2,1)}, bf16[1024,256]{1,0:T(8,128)(2,1)S(1)}, u32[]{:S(2)}, u32[]{:S(2)}) collective-permute-start(bf16[1024,256]{1,0:T(8,128)(2,1)} %get-tuple-element.8), channel_id=1, source_target_pairs={{0,28},{4,0},{8,4},{12,8},{16,12},{20,16},{24,20},{28,24},{1,29},{... | collective-permute-start | bytes 1572872 | tf_op jit(solution)/shard_map/ppermute | solution.py:184
  75.0 15.8 %collective-permute-start.5 = (bf16[1024,256]{1,0:T(8,128)(2,1)}, bf16[1024,256]{1,0:T(8,128)(2,1)S(1)}, u32[]{:S(2)}, u32[]{:S(2)}) collective-permute-start(bf16[1024,256]{1,0:T(8,128)(2,1)} %get-tuple-element.8), channel_id=1, source_target_pairs={{0,4},{4,8},{8,12},{12,16},{16,20},{20,24},{24,28},{28,0},{1,5},{5... | collective-permute-start | bytes 1572872 | tf_op jit(solution)/shard_map/ppermute | solution.py:183
  75.8 15.2 %collective-permute-start.11 = (bf16[256,1024]{1,0:T(8,128)(2,1)S(1)}, bf16[256,1024]{1,0:T(8,128)(2,1)S(1)}, u32[]{:S(2)}, u32[]{:S(2)}) collective-permute-start(bf16[256,1024]{1,0:T(8,128)(2,1)S(1)} %pad_maximum_fusion), channel_id=1, source_target_pairs={{0,128},{128,0},{1,129},{129,1},{2,130},{130,2},{3,131},{131,3},{4... | collective-permute-start | bytes 1572872 | tf_op jit(solution)/shard_map/ppermute | solution.py:194
  77.9 14.2 %collective-permute-start.12 = (bf16[256,1024]{1,0:T(8,128)(2,1)S(1)}, bf16[256,1024]{1,0:T(8,128)(2,1)S(1)}, u32[]{:S(2)}, u32[]{:S(2)}) collective-permute-start(bf16[256,1024]{1,0:T(8,128)(2,1)S(1)} %pad_maximum_fusion), channel_id=1, source_target_pairs={{0,32},{32,64},{64,96},{96,0},{1,33},{33,65},{65,97},{97,1},{2,34}... | collective-permute-start | bytes 1572872 | tf_op jit(solution)/shard_map/ppermute | solution.py:195
  80.2 13.2 %collective-permute-start.13 = (bf16[256,1024]{1,0:T(8,128)(2,1)S(1)}, bf16[256,1024]{1,0:T(8,128)(2,1)S(1)}, u32[]{:S(2)}, u32[]{:S(2)}) collective-permute-start(bf16[256,1024]{1,0:T(8,128)(2,1)S(1)} %pad_maximum_fusion), channel_id=1, source_target_pairs={{0,96},{32,0},{64,32},{96,64},{1,97},{33,1},{65,33},{97,65},{2,98}... | collective-permute-start | bytes 1572872 | tf_op jit(solution)/shard_map/ppermute | solution.py:196
  88.4 13.6 %collective-permute-start.3 = (bf16[1024,256]{1,0:T(8,128)(2,1)S(1)}, bf16[1024,256]{1,0:T(8,128)(2,1)S(1)}, u32[]{:S(2)}, u32[]{:S(2)}) collective-permute-start(bf16[1024,256]{1,0:T(8,128)(2,1)S(1)} %collective-permute-done.2), channel_id=1, source_target_pairs={{0,28},{4,0},{8,4},{12,8},{16,12},{20,16},{24,20},{28,24},{1,29},{... | collective-permute-start | bytes 1572872 | tf_op jit(solution)/shard_map/ppermute | solution.py:184
  90.8 14.7 %collective-permute-start.6 = (bf16[1024,256]{1,0:T(8,128)(2,1)S(1)}, bf16[1024,256]{1,0:T(8,128)(2,1)S(1)}, u32[]{:S(2)}, u32[]{:S(2)}) collective-permute-start(bf16[1024,256]{1,0:T(8,128)(2,1)S(1)} %collective-permute-done.5), channel_id=1, source_target_pairs={{0,4},{4,8},{8,12},{12,16},{16,20},{20,24},{24,28},{28,0},{1,5},{5... | collective-permute-start | bytes 1572872 | tf_op jit(solution)/shard_map/ppermute | solution.py:183
  91.0 15.9 %collective-permute-start.14 = (bf16[256,1024]{1,0:T(8,128)(2,1)S(1)}, bf16[256,1024]{1,0:T(8,128)(2,1)S(1)}, u32[]{:S(2)}, u32[]{:S(2)}) collective-permute-start(bf16[256,1024]{1,0:T(8,128)(2,1)S(1)} %collective-permute-done.11), channel_id=1, source_target_pairs={{0,32},{32,64},{64,96},{96,0},{1,33},{33,65},{65,97},{97,1},{2,34}... | collective-permute-start | bytes 1572872 | tf_op jit(solution)/shard_map/ppermute | solution.py:197
  92.1 13.5 %collective-permute-start.15 = (bf16[256,1024]{1,0:T(8,128)(2,1)S(1)}, bf16[256,1024]{1,0:T(8,128)(2,1)S(1)}, u32[]{:S(2)}, u32[]{:S(2)}) collective-permute-start(bf16[256,1024]{1,0:T(8,128)(2,1)S(1)} %collective-permute-done.11), channel_id=1, source_target_pairs={{0,96},{32,0},{64,32},{96,64},{1,97},{33,1},{65,33},{97,65},{2,98}... | collective-permute-start | bytes 1572872 | tf_op jit(solution)/shard_map/ppermute | solution.py:198
  93.5 22.1 %collective-permute-start.16 = (bf16[256,1024]{1,0:T(8,128)(2,1)S(1)}, bf16[256,1024]{1,0:T(8,128)(2,1)S(1)}, u32[]{:S(2)}, u32[]{:S(2)}) collective-permute-start(bf16[256,1024]{1,0:T(8,128)(2,1)S(1)} %collective-permute-done.12), channel_id=1, source_target_pairs={{0,32},{32,64},{64,96},{96,0},{1,33},{33,65},{65,97},{97,1},{2,34}... | collective-permute-start | bytes 1572872 | tf_op jit(solution)/shard_map/ppermute | solution.py:199
  102.0 13.6 %collective-permute-start.4 = (bf16[1024,256]{1,0:T(8,128)(2,1)S(1)}, bf16[1024,256]{1,0:T(8,128)(2,1)S(1)}, u32[]{:S(2)}, u32[]{:S(2)}) collective-permute-start(bf16[1024,256]{1,0:T(8,128)(2,1)S(1)} %collective-permute-done.3), channel_id=1, source_target_pairs={{0,28},{4,0},{8,4},{12,8},{16,12},{20,16},{24,20},{28,24},{1,29},{... | collective-permute-start | bytes 1572872 | tf_op jit(solution)/shard_map/ppermute | solution.py:184
  105.4 13.8 %collective-permute-start.7 = (bf16[1024,256]{1,0:T(8,128)(2,1)S(1)}, bf16[1024,256]{1,0:T(8,128)(2,1)S(1)}, u32[]{:S(2)}, u32[]{:S(2)}) collective-permute-start(bf16[1024,256]{1,0:T(8,128)(2,1)S(1)} %collective-permute-done.6), channel_id=1, source_target_pairs={{0,4},{4,8},{8,12},{12,16},{16,20},{20,24},{24,28},{28,0},{1,5},{5... | collective-permute-start | bytes 1572872 | tf_op jit(solution)/shard_map/ppermute | solution.py:183
  105.5 13.9 %collective-permute-start.17 = (bf16[256,1024]{1,0:T(8,128)(2,1)S(1)}, bf16[256,1024]{1,0:T(8,128)(2,1)S(1)}, u32[]{:S(2)}, u32[]{:S(2)}) collective-permute-start(bf16[256,1024]{1,0:T(8,128)(2,1)S(1)} %collective-permute-done.15), channel_id=1, source_target_pairs={{0,96},{32,0},{64,32},{96,64},{1,97},{33,1},{65,33},{97,65},{2,98}... | collective-permute-start | bytes 1572872 | tf_op jit(solution)/shard_map/ppermute | solution.py:200
  134.7 15.6 %collective-permute-start.19 = (bf16[1024,256]{1,0:T(8,128)(2,1)S(1)}, bf16[1024,256]{1,0:T(8,128)(2,1)S(1)}, u32[]{:S(2)}, u32[]{:S(2)}) collective-permute-start(bf16[1024,256]{1,0:T(8,128)(2,1)S(1)} %slice.116), channel_id=1, source_target_pairs={{0,1},{1,0},{2,3},{3,2},{4,5},{5,4},{6,7},{7,6},{8,9},{9,8},{10,11... | collective-permute-start | bytes 1572872 | tf_op jit(solution)/shard_map/ppermute | solution.py:216
  150.5 13.4 %collective-permute-start.20 = (bf16[1024,256]{1,0:T(8,128)(2,1)S(1)}, bf16[1024,256]{1,0:T(8,128)(2,1)S(1)}, u32[]{:S(2)}, u32[]{:S(2)}) collective-permute-start(bf16[1024,256]{1,0:T(8,128)(2,1)S(1)} %get-tuple-element.11), channel_id=1, source_target_pairs={{0,28},{4,0},{8,4},{12,8},{16,12},{20,16},{24,20},{28,24},{1,29},{... | collective-permute-start | bytes 1572872 | tf_op jit(solution)/shard_map/ppermute | solution.py:184
  150.8 14.6 %collective-permute-start.23 = (bf16[1024,256]{1,0:T(8,128)(2,1)S(1)}, bf16[1024,256]{1,0:T(8,128)(2,1)S(1)}, u32[]{:S(2)}, u32[]{:S(2)}) collective-permute-start(bf16[1024,256]{1,0:T(8,128)(2,1)S(1)} %get-tuple-element.11), channel_id=1, source_target_pairs={{0,4},{4,8},{8,12},{12,16},{16,20},{20,24},{24,28},{28,0},{1,5},{5... | collective-permute-start | bytes 1572872 | tf_op jit(solution)/shard_map/ppermute | solution.py:183
  164.0 12.2 %collective-permute-start.21 = (bf16[1024,256]{1,0:T(8,128)(2,1)S(1)}, bf16[1024,256]{1,0:T(8,128)(2,1)S(1)}, u32[]{:S(2)}, u32[]{:S(2)}) collective-permute-start(bf16[1024,256]{1,0:T(8,128)(2,1)S(1)} %collective-permute-done.20), channel_id=1, source_target_pairs={{0,28},{4,0},{8,4},{12,8},{16,12},{20,16},{24,20},{28,24},{1,29},{... | collective-permute-start | bytes 1572872 | tf_op jit(solution)/shard_map/ppermute | solution.py:184
  165.5 13.7 %collective-permute-start.24 = (bf16[1024,256]{1,0:T(8,128)(2,1)S(1)}, bf16[1024,256]{1,0:T(8,128)(2,1)S(1)}, u32[]{:S(2)}, u32[]{:S(2)}) collective-permute-start(bf16[1024,256]{1,0:T(8,128)(2,1)S(1)} %collective-permute-done.23), channel_id=1, source_target_pairs={{0,4},{4,8},{8,12},{12,16},{16,20},{20,24},{24,28},{28,0},{1,5},{5... | collective-permute-start | bytes 1572872 | tf_op jit(solution)/shard_map/ppermute | solution.py:183
  176.2 12.1 %collective-permute-start.22 = (bf16[1024,256]{1,0:T(8,128)(2,1)S(1)}, bf16[1024,256]{1,0:T(8,128)(2,1)S(1)}, u32[]{:S(2)}, u32[]{:S(2)}) collective-permute-start(bf16[1024,256]{1,0:T(8,128)(2,1)S(1)} %collective-permute-done.21), channel_id=1, source_target_pairs={{0,28},{4,0},{8,4},{12,8},{16,12},{20,16},{24,20},{28,24},{1,29},{... | collective-permute-start | bytes 1572872 | tf_op jit(solution)/shard_map/ppermute | solution.py:184
  179.2 12.9 %collective-permute-start.25 = (bf16[1024,256]{1,0:T(8,128)(2,1)S(1)}, bf16[1024,256]{1,0:T(8,128)(2,1)S(1)}, u32[]{:S(2)}, u32[]{:S(2)}) collective-permute-start(bf16[1024,256]{1,0:T(8,128)(2,1)S(1)} %collective-permute-done.24), channel_id=1, source_target_pairs={{0,4},{4,8},{8,12},{12,16},{16,20},{20,24},{24,28},{28,0},{1,5},{5... | collective-permute-start | bytes 1572872 | tf_op jit(solution)/shard_map/ppermute | solution.py:183
  207.5 15.6 %collective-permute-start.29 = (bf16[1024,256]{1,0:T(8,128)(2,1)S(1)}, bf16[1024,256]{1,0:T(8,128)(2,1)S(1)}, u32[]{:S(2)}, u32[]{:S(2)}) collective-permute-start(bf16[1024,256]{1,0:T(8,128)(2,1)S(1)} %slice.115), channel_id=1, source_target_pairs={{0,1},{1,0},{2,3},{3,2},{4,5},{5,4},{6,7},{7,6},{8,9},{9,8},{10,11... | collective-permute-start | bytes 1572872 | tf_op jit(solution)/shard_map/ppermute | solution.py:216
  (13 other events, 118.5 us)

commit v3 on v2

--- a/solution.py
+++ b/solution.py
@@ -176,17 +176,22 @@
     return [(i, (i + step) % n) for i in range(n)]
 
 
-def gather_z(own):
-    pieces = [own] + [None] * 7
+def gather_z(own, last_up):
+    pieces = [own]
     up = down = own
-    for s in range(1, 4):
-        up = lax.ppermute(up, "z", ring_of(8, 1))
-        down = lax.ppermute(down, "z", ring_of(8, -1))
-        pieces[8 - s], pieces[s] = up, down
-    top = lax.ppermute(up[:512], "z", ring_of(8, 1))
-    bottom = lax.ppermute(down[512:], "z", ring_of(8, -1))
-    pieces[4] = jnp.concatenate([top, bottom], axis=0)
-    return jnp.concatenate(pieces, axis=1)
+    for s in range(1, 5):
+        if s < 4 or last_up:
+            up = lax.ppermute(up, "z", ring_of(8, 1))
+            pieces.append(up)
+        if s < 4 or not last_up:
+            down = lax.ppermute(down, "z", ring_of(8, -1))
+            pieces.append(down)
+    return jnp.stack(pieces)
+
+
+def place_in_ring(distance):
+    distance = distance & 7
+    return jnp.where(distance >= 4, 15 - 2 * distance, 2 * distance)
 
 
 def gather_rows(unit, ylo, x, z):
@@ -194,27 +199,34 @@
     near = lax.ppermute(unit, "ylo", SWAP)
     a1 = lax.ppermute(unit, "x", fwd)
     a3 = lax.ppermute(unit, "x", bwd)
-    b1 = lax.ppermute(near, "x", fwd)
+    b1, a2 = lax.ppermute(jnp.stack([near, a1]), "x", fwd)
     b3 = lax.ppermute(near, "x", bwd)
-    a2 = lax.ppermute(a1, "x", fwd)
     b2 = lax.ppermute(b3, "x", bwd)
     out = jnp.zeros((8,) + unit.shape, unit.dtype)
     for flip, dx, piece in (
         (0, 0, unit), (1, 0, near), (0, 3, a1), (0, 1, a3),
         (1, 3, b1), (1, 1, b3), (0, 2, a2), (1, 2, b2),
     ):
-        source = (ylo ^ flip) * 4 + (x + dx) % 4
-        out = lax.dynamic_update_index_in_dim(out, piece, (source - z) % 8, 0)
-    return out.reshape(8 * unit.shape[0], unit.shape[1])
-
-
-def product(a, b):
-    far = jnp.dot(a, b[:, 512:], preferred_element_type=jnp.float32).astype(jnp.bfloat16)
-    far = lax.ppermute(far, "core", SWAP)
-    near = jnp.dot(a, b[:, :512], preferred_element_type=jnp.float32)
-    part = near + far.astype(jnp.float32)
-    away = lax.ppermute(part[:, 256:].astype(jnp.bfloat16), "yhi", SWAP)
-    return part[:, :256] + away.astype(jnp.float32)
+        source = (ylo ^ flip) * 4 + ((x + dx) & 3)
+        out = lax.dynamic_update_index_in_dim(out, piece, place_in_ring(source - z), 0)
+    return out
+
+
+def dot(a, b):
+    return jnp.einsum("dmk,dkn->mn", a, b, preferred_element_type=jnp.float32)
+
+
+def product(a, b, chunks):
+    far = lax.ppermute(dot(a, b[:, :, 512:]).astype(jnp.bfloat16), "core", SWAP)
+    part = dot(a, b[:, :, 256:512]) + far[:, 256:].astype(jnp.float32)
+    rest = dot(a, b[:, :, :256]) + far[:, :256].astype(jnp.float32)
+    step = part.shape[0] // chunks
+    out = []
+    for m in range(chunks):
+        rows = slice(step * m, step * m + step)
+        away = lax.ppermute(part[rows].astype(jnp.bfloat16), "yhi", SWAP)
+        out.append((rest[rows], away))
+    return out
 
 
 def local(basis_left, basis_right, grid_weight, task_owner, task_block, core_matrix, block_mask):
@@ -231,28 +243,40 @@
     arrived = lax.all_to_all(
         outgoing.reshape(tasks, 3, 8, 128), AXES[:4], split_axis=0, concat_axis=0, tiled=True
     )
-    tag = arrived[:, 2, :2, :2].astype(jnp.float32)
-    labels = jnp.minimum(tag[:, :, 0] * 16 + tag[:, :, 1], 512.0).astype(jnp.int32).reshape(-1)
-    labels_far = lax.ppermute(labels, "yhi", SWAP)
-    arrived_far = lax.ppermute(arrived[:, :2].reshape(2 * tasks, 8, 128), "yhi", SWAP)
+    slots = arrived[:, :2].reshape(2 * tasks, 8, 128)
+    tag = arrived[:, 2, :2, :2]
+    tag_tile = jnp.pad(tag.reshape(4, 128), ((0, 4), (0, 0)))[None]
+    far = lax.ppermute(jnp.concatenate([slots, tag_tile], axis=0), "yhi", SWAP)
+
+    def label_of(tag):
+        tag = tag.astype(jnp.float32)
+        return jnp.minimum(tag[:, 0] * 16 + tag[:, 1], 512.0).astype(jnp.int32)
+
+    labels = label_of(tag.reshape(2 * tasks, 2))
+    labels_far = label_of(far[2 * tasks, :4].reshape(2 * tasks, 2))
     collected = collect(labels, arrived.reshape(3 * tasks, 8, 128))
     block_rows = row * 32 + jnp.arange(32, dtype=jnp.int32)
     block_cols = col * 16 + jnp.arange(16, dtype=jnp.int32)
     mask = (block_mask != 0) | (block_rows[:, None] == block_cols[None, :])
     place = jnp.stack([row, col, yhi]).astype(jnp.int32)
     ks_out, own, panel, pattern = assemble(
-        place, mask.astype(jnp.float32).reshape(-1), labels_far, arrived_far, collected, core_matrix
+        place, mask.astype(jnp.float32).reshape(-1), labels_far, far, collected, core_matrix
     )
 
     keep = lax.dynamic_index_in_dim(panel, 2 * core + yhi, 0, keepdims=False)
     give = lax.dynamic_index_in_dim(panel, 2 * (1 - core) + yhi, 0, keepdims=False)
     unit = jnp.concatenate([keep, lax.ppermute(give, "core", SWAP)], axis=1)
     b = gather_rows(unit, ylo, x, z)
-    pattern = pattern.astype(jnp.float32)
-    square = pattern * product(gather_z(own), b)
-    cube_term = pattern * product(gather_z(square.astype(jnp.bfloat16)), b)
-    density = 3.0 * square - 2.0 * cube_term
-    return (ks_out, density)
+    squares = []
+    for m, (rest, away) in enumerate(product(gather_z(own, True), b, 2)):
+        if m > 0:
+            away, _ = lax.optimization_barrier((away, squares[0]))
+        mask = pattern[512 * m : 512 * m + 512].astype(jnp.float32)
+        squares.append(mask * (rest + away.astype(jnp.float32)))
+    a2 = [gather_z(square.astype(jnp.bfloat16), m == 0) for m, square in enumerate(squares)]
+    ((rest, away),) = product(jnp.concatenate(a2, axis=1), b, 1)
+    cube_term = pattern.astype(jnp.float32) * (rest + away.astype(jnp.float32))
+    return (ks_out, 3.0 * jnp.concatenate(squares, axis=0) - 2.0 * cube_term)
 
 
 def solution(mesh):

time: 227 us -> 214 us (0.943)
  waiting for transfers between devices: 125 us -> 108 us
  starting transfers between devices: 55.6 us -> 64.7 us
  other arithmetic: 7.05 us -> 4.69 us
    ppermute x6 -> x11, waiting for transfers between devices: 0.02 us -> 40.5 us  [gather_z(): up = lax.ppermute(up, 'z', ring_of(8, 1))]
    ppermute x6 -> x10, waiting for transfers between devices: 44.7 us -> 4.38 us  [gather_z(): down = lax.ppermute(down, 'z', ring_of(8, -1))]
    ppermute x12 -> x7, waiting for transfers between devices: 58.2 us -> 34 us  [the longest x3 19.8 us: product(): away = lax.ppermute(part[rows].astype(jnp.bfloat16), 'yhi', SWAP)]
    ppermute x6 -> x10, starting transfers between devices: 11.8 us -> 31.3 us  [gather_z(): down = lax.ppermute(down, 'z', ring_of(8, -1))]
    ppermute x12 -> x7, starting transfers between devices: 19.3 us -> 11.1 us  [the longest x3 6.57 us: product(): away = lax.ppermute(part[rows].astype(jnp.bfloat16), 'yhi', SWAP)]
    dot_general x4 -> x6, matrix products: 9.31 us -> 10.7 us  [dot(): return jnp.einsum('dmk,dkn->mn', a, b, preferred_element_type=jnp.float32)]
  transfers between devices with their start and end apart: 31 -> 35, of which waited for: 17 -> 24; matrix products, arithmetic and copies ran while one was open for 3% -> 3% of each run, Pallas kernels for 2% -> 2%
where the time goes in v3:
time: 214 us; the launch traced here: 213 us
  waiting for transfers between devices  108 us (50%)
  starting transfers between devices  64.7 us (30%)
  Pallas kernels  19.9 us (9%)
  matrix products  10.7 us (5%)
  other arithmetic  4.69 us (2%)
  local copies, waits for them, and re-layouts  4.6 us (2%)
    ppermute x11, waiting for transfers between devices, gather_z(): up = lax.ppermute(up, 'z', ring_of(8, 1))  40.5 us
    ppermute x10, starting transfers between devices, gather_z(): down = lax.ppermute(down, 'z', ring_of(8, -1))  31.3 us
    all_to_all x1, waiting for transfers between devices, local(): lax.all_to_all(outgoing.reshape(tasks, 3, 8, 128), AXES[:4], split_axis=0...  22.2 us
    ppermute x3, waiting for transfers between devices, product(): away = lax.ppermute(part[rows].astype(jnp.bfloat16), 'yhi', SWAP)  19.8 us
    all_to_all x1, starting transfers between devices, local(): lax.all_to_all(outgoing.reshape(tasks, 3, 8, 128), AXES[:4], split_axis=0...  13.8 us
    dot_general x6, matrix products, dot(): return jnp.einsum('dmk,dkn->mn', a, b, preferred_element_type=jnp.float32)  10.7 us
    pallas_call x1, Pallas kernels, assemble(): pl.pallas_call(functools.partial(assemble_kernel, scale=COUPLING / math.s...  9.26 us
    ppermute x1, waiting for transfers between devices, local(): far = lax.ppermute(jnp.concatenate([slots, tag_tile], axis=0), 'yhi', SWAP)  7.02 us
  transfers between devices with their start and end apart: 35, of which 24 were waited for; matrix products, arithmetic and copies ran while one was open for 3% of the time, Pallas kernels for 2%

profile of v3, /device:TPU:2, one launch (start us, length us, event | category | flops | bytes accessed | tf_op | source)
XLA Modules:
  0.0 213.5 jit_solution(11663086923543367883)
XLA Ops:
  2.7 7.0 %contribute.1 = bf16[384,8,128]{2,1,0:T(8,128)(2,1)} custom-call(s32[128]{0:T(128)} %multiply_add_fusion.pos_ref, s32[128]{0:T(128)} %block_ref.1, bf16[128,32,128]{2,1,0:T(8,128)(2,1)} %left_ref.1, bf16[128,32,128]{2,1,0:T(8,128)(2,1)} %right_ref.1, f32[128,128]{1,0:T(8,128)} %weight_ref.1), custom_call_target="tpu_custom_call" | custom-call | tf_op jit(solution)/shard_map/contribute/pallas_call | solution.py:139
  9.7 13.8 %all-to-all-start = ((bf16[128,3,8,128]{3,2,1,0:T(8,128)(2,1)}), bf16[128,3,8,128]{3,2,1,0:T(8,128)(2,1)S(1)}, u32[]{:S(2)}, u32[]{:S(2)}) async-start(bf16[128,3,8,128]{3,2,1,0:T(8,128)(2,1)} %bitcast.108), calls=%async_computation | async-start | bytes 1572864 | tf_op jit(solution)/shard_map/all_to_all | solution.py:243
  23.6 22.2 %all-to-all-done = bf16[128,3,8,128]{3,2,1,0:T(8,128)(2,1)S(1)} async-done(((bf16[128,3,8,128]{3,2,1,0:T(8,128)(2,1)}), bf16[128,3,8,128]{3,2,1,0:T(8,128)(2,1)S(1)}, u32[]{:S(2)}, u32[]{:S(2)}) %all-to-all-start) | async-done | bytes 786464 | tf_op jit(solution)/shard_map/all_to_all | solution.py:243
  46.1 3.0 %collective-permute-start = (bf16[257,8,128]{2,1,0:T(8,128)(2,1)S(1)}, bf16[257,8,128]{2,1,0:T(8,128)(2,1)S(1)}, u32[]{:S(2)}, u32[]{:S(2)}) collective-permute-start(bf16[257,8,128]{2,1,0:T(8,128)(2,1)S(1)} %pad_maximum_fusion.7), channel_id=1, source_target_pairs={{0,1},{1,0},{2,3},{3,2},{4,5},{5,4},{6,7},{7,6},{8,9},{9,8},{10,11... | collective-permute-start | bytes 1579016 | tf_op jit(solution)/shard_map/ppermute | solution.py:249
  51.2 3.6 %collect.1.first_ref = f32[520,8,128]{2,1,0:T(8,128)} custom-call(s32[256]{0:T(256)} %fusion.26.label_ref, bf16[384,8,128]{2,1,0:T(8,128)(2,1)} %bitcast.107), custom_call_target="tpu_custom_call" | custom-call | flops 1048576 | bytes 8388608 | tf_op jit(solution)/shard_map/collect/pallas_call | solution.py:149
  54.9 7.0 %collective-permute-done.slot_ref = bf16[257,8,128]{2,1,0:T(8,128)(2,1)S(1)} collective-permute-done((bf16[257,8,128]{2,1,0:T(8,128)(2,1)S(1)}, bf16[257,8,128]{2,1,0:T(8,128)(2,1)S(1)}, u32[]{:S(2)}, u32[]{:S(2)}) %collective-permute-start) | collective-permute-done | bytes 526368 | tf_op jit(solution)/shard_map/ppermute | solution.py:249
  62.8 9.3 %assemble.1 = (f32[1024,256]{1,0:T(8,128)}, bf16[1024,256]{1,0:T(8,128)(2,1)}, bf16[4,256,512]{2,1,0:T(8,128)(2,1)}, bf16[1024,256]{1,0:T(8,128)(2,1)}) custom-call(s32[3]{0:T(128)} %pad_add_fusion.place_ref, f32[512]{0:T(512)} %reshape.49.mask_ref, s32[256]{0:T(256)} %fusion.29.label_ref, bf16[257,8,128]{2,1,0:T(8,128)(2,1)} %copy-done.1, ...), custom_call_target="tpu_custom_call" | custom-call | tf_op jit(solution)/shard_map/assemble/pallas_call | solution.py:160
  82.9 4.9 %collective-permute-done.1 = bf16[1024,256]{1,0:T(8,128)(2,1)S(1)} collective-permute-done((bf16[1024,256]{1,0:T(8,128)(2,1)}, bf16[1024,256]{1,0:T(8,128)(2,1)S(1)}, u32[]{:S(2)}, u32[]{:S(2)}) %collective-permute-start.1) | collective-permute-done | bytes 524320 | tf_op jit(solution)/shard_map/ppermute | solution.py:184
  87.7 3.2 %collective-permute-start.4 = (bf16[1024,256]{1,0:T(8,128)(2,1)S(1)}, bf16[1024,256]{1,0:T(8,128)(2,1)S(1)}, u32[]{:S(2)}, u32[]{:S(2)}) collective-permute-start(bf16[1024,256]{1,0:T(8,128)(2,1)S(1)} %collective-permute-done.2), channel_id=1, source_target_pairs={{0,28},{4,0},{8,4},{12,8},{16,12},{20,16},{24,20},{28,24},{1,29},{... | collective-permute-start | bytes 1572872 | tf_op jit(solution)/shard_map/ppermute | solution.py:187
  96.2 6.2 %collective-permute-done.3 = bf16[1024,256]{1,0:T(8,128)(2,1)S(1)} collective-permute-done((bf16[1024,256]{1,0:T(8,128)(2,1)S(1)}, bf16[1024,256]{1,0:T(8,128)(2,1)S(1)}, u32[]{:S(2)}, u32[]{:S(2)}) %collective-permute-start.3) | collective-permute-done | bytes 524320 | tf_op jit(solution)/shard_map/ppermute | solution.py:184
  102.5 3.3 %collective-permute-start.6 = (bf16[1024,256]{1,0:T(8,128)(2,1)S(1)}, bf16[1024,256]{1,0:T(8,128)(2,1)S(1)}, u32[]{:S(2)}, u32[]{:S(2)}) collective-permute-start(bf16[1024,256]{1,0:T(8,128)(2,1)S(1)} %collective-permute-done.4), channel_id=1, source_target_pairs={{0,28},{4,0},{8,4},{12,8},{16,12},{20,16},{24,20},{28,24},{1,29},{... | collective-permute-start | bytes 1572872 | tf_op jit(solution)/shard_map/ppermute | solution.py:187
  109.1 7.1 %collective-permute-done.5 = bf16[1024,256]{1,0:T(8,128)(2,1)S(1)} collective-permute-done((bf16[1024,256]{1,0:T(8,128)(2,1)S(1)}, bf16[1024,256]{1,0:T(8,128)(2,1)S(1)}, u32[]{:S(2)}, u32[]{:S(2)}) %collective-permute-start.5) | collective-permute-done | bytes 524320 | tf_op jit(solution)/shard_map/ppermute | solution.py:184
  119.6 9.5 %collective-permute-done.7 = bf16[1024,256]{1,0:T(8,128)(2,1)S(1)} collective-permute-done((bf16[1024,256]{1,0:T(8,128)(2,1)S(1)}, bf16[1024,256]{1,0:T(8,128)(2,1)S(1)}, u32[]{:S(2)}, u32[]{:S(2)}) %collective-permute-start.7) | collective-permute-done | bytes 524320 | tf_op jit(solution)/shard_map/ppermute | solution.py:184
  140.3 5.9 %collective-permute-done.16 = bf16[512,256]{1,0:T(8,128)(2,1)S(1)} collective-permute-done((bf16[512,256]{1,0:T(8,128)(2,1)S(1)}, bf16[512,256]{1,0:T(8,128)(2,1)S(1)}, u32[]{:S(2)}, u32[]{:S(2)}) %collective-permute-start.16) | collective-permute-done | bytes 262176 | tf_op jit(solution)/shard_map/ppermute | solution.py:227
  146.4 3.2 %collective-permute-start.19 = (bf16[512,256]{1,0:T(8,128)(2,1)S(1)}, bf16[512,256]{1,0:T(8,128)(2,1)S(1)}, u32[]{:S(2)}, u32[]{:S(2)}) collective-permute-start(bf16[512,256]{1,0:T(8,128)(2,1)S(1)} %get-tuple-element.13), channel_id=1, source_target_pairs={{0,28},{4,0},{8,4},{12,8},{16,12},{20,16},{24,20},{28,24},{1,29},{... | collective-permute-start | bytes 786440 | tf_op jit(solution)/shard_map/ppermute | solution.py:187
  151.2 3.2 %collective-permute-start.26 = (bf16[512,256]{1,0:T(8,128)(2,1)S(1)}, bf16[512,256]{1,0:T(8,128)(2,1)S(1)}, u32[]{:S(2)}, u32[]{:S(2)}) collective-permute-start(bf16[512,256]{1,0:T(8,128)(2,1)S(1)} %get-tuple-element.16), channel_id=1, source_target_pairs={{0,28},{4,0},{8,4},{12,8},{16,12},{20,16},{24,20},{28,24},{1,29},{... | collective-permute-start | bytes 786440 | tf_op jit(solution)/shard_map/ppermute | solution.py:187
  154.5 3.5 %collective-permute-start.21 = (bf16[512,256]{1,0:T(8,128)(2,1)S(1)}, bf16[512,256]{1,0:T(8,128)(2,1)S(1)}, u32[]{:S(2)}, u32[]{:S(2)}) collective-permute-start(bf16[512,256]{1,0:T(8,128)(2,1)S(1)} %collective-permute-done.19), channel_id=1, source_target_pairs={{0,28},{4,0},{8,4},{12,8},{16,12},{20,16},{24,20},{28,24},{1,29},{... | collective-permute-start | bytes 786440 | tf_op jit(solution)/shard_map/ppermute | solution.py:187
  158.0 3.6 %collective-permute-done.25 = bf16[512,256]{1,0:T(8,128)(2,1)S(1)} collective-permute-done((bf16[512,256]{1,0:T(8,128)(2,1)S(1)}, bf16[512,256]{1,0:T(8,128)(2,1)S(1)}, u32[]{:S(2)}, u32[]{:S(2)}) %collective-permute-start.25) | collective-permute-done | bytes 262176 | tf_op jit(solution)/shard_map/ppermute | solution.py:184
  161.7 3.3 %collective-permute-start.28 = (bf16[512,256]{1,0:T(8,128)(2,1)S(1)}, bf16[512,256]{1,0:T(8,128)(2,1)S(1)}, u32[]{:S(2)}, u32[]{:S(2)}) collective-permute-start(bf16[512,256]{1,0:T(8,128)(2,1)S(1)} %collective-permute-done.26), channel_id=1, source_target_pairs={{0,28},{4,0},{8,4},{12,8},{16,12},{20,16},{24,20},{28,24},{1,29},{... | collective-permute-start | bytes 786440 | tf_op jit(solution)/shard_map/ppermute | solution.py:187
  167.3 3.3 %collective-permute-start.23 = (bf16[512,256]{1,0:T(8,128)(2,1)S(1)}, bf16[512,256]{1,0:T(8,128)(2,1)S(1)}, u32[]{:S(2)}, u32[]{:S(2)}) collective-permute-start(bf16[512,256]{1,0:T(8,128)(2,1)S(1)} %collective-permute-done.21), channel_id=1, source_target_pairs={{0,28},{4,0},{8,4},{12,8},{16,12},{20,16},{24,20},{28,24},{1,29},{... | collective-permute-start | bytes 786440 | tf_op jit(solution)/shard_map/ppermute | solution.py:187
  172.9 3.3 %collective-permute-start.30 = (bf16[512,256]{1,0:T(8,128)(2,1)S(1)}, bf16[512,256]{1,0:T(8,128)(2,1)S(1)}, u32[]{:S(2)}, u32[]{:S(2)}) collective-permute-start(bf16[512,256]{1,0:T(8,128)(2,1)S(1)} %collective-permute-done.28), channel_id=1, source_target_pairs={{0,28},{4,0},{8,4},{12,8},{16,12},{20,16},{24,20},{28,24},{1,29},{... | collective-permute-start | bytes 786440 | tf_op jit(solution)/shard_map/ppermute | solution.py:187
  178.5 3.2 %collective-permute-done.30 = bf16[512,256]{1,0:T(8,128)(2,1)S(1)} collective-permute-done((bf16[512,256]{1,0:T(8,128)(2,1)S(1)}, bf16[512,256]{1,0:T(8,128)(2,1)S(1)}, u32[]{:S(2)}, u32[]{:S(2)}) %collective-permute-start.30) | collective-permute-done | bytes 262176 | tf_op jit(solution)/shard_map/ppermute | solution.py:187
  181.7 3.7 %collective-permute-start.31 = (bf16[512,256]{1,0:T(8,128)(2,1)S(1)}, bf16[512,256]{1,0:T(8,128)(2,1)S(1)}, u32[]{:S(2)}, u32[]{:S(2)}) collective-permute-start(bf16[512,256]{1,0:T(8,128)(2,1)S(1)} %collective-permute-done.30), channel_id=1, source_target_pairs={{0,28},{4,0},{8,4},{12,8},{16,12},{20,16},{24,20},{28,24},{1,29},{... | collective-permute-start | bytes 786440 | tf_op jit(solution)/shard_map/ppermute | solution.py:187
  198.6 12.6 %collective-permute-done.33 = bf16[1024,256]{1,0:T(8,128)(2,1)S(1)} collective-permute-done((bf16[1024,256]{1,0:T(8,128)(2,1)S(1)}, bf16[1024,256]{1,0:T(8,128)(2,1)S(1)}, u32[]{:S(2)}, u32[]{:S(2)}) %collective-permute-start.33) | collective-permute-done | bytes 524320 | tf_op jit(solution)/shard_map/ppermute | solution.py:227
  (118 shorter events, 63.4 us)
Async XLA Ops:
  9.7 36.1 %all-to-all-start = ((bf16[128,3,8,128]{3,2,1,0:T(8,128)(2,1)}), bf16[128,3,8,128]{3,2,1,0:T(8,128)(2,1)S(1)}, u32[]{:S(2)}, u32[]{:S(2)}) async-start(bf16[128,3,8,128]{3,2,1,0:T(8,128)(2,1)} %bitcast.108), calls=%async_computation | async-start | bytes 1572864 | tf_op jit(solution)/shard_map/all_to_all | solution.py:243
  46.1 15.8 %collective-permute-start = (bf16[257,8,128]{2,1,0:T(8,128)(2,1)S(1)}, bf16[257,8,128]{2,1,0:T(8,128)(2,1)S(1)}, u32[]{:S(2)}, u32[]{:S(2)}) collective-permute-start(bf16[257,8,128]{2,1,0:T(8,128)(2,1)S(1)} %pad_maximum_fusion.7), channel_id=1, source_target_pairs={{0,1},{1,0},{2,3},{3,2},{4,5},{5,4},{6,7},{7,6},{8,9},{9,8},{10,11... | collective-permute-start | bytes 1579016 | tf_op jit(solution)/shard_map/ppermute | solution.py:249
  72.0 15.7 %collective-permute-start.1 = (bf16[1024,256]{1,0:T(8,128)(2,1)}, bf16[1024,256]{1,0:T(8,128)(2,1)S(1)}, u32[]{:S(2)}, u32[]{:S(2)}) collective-permute-start(bf16[1024,256]{1,0:T(8,128)(2,1)} %get-tuple-element.9), channel_id=1, source_target_pairs={{0,4},{4,8},{8,12},{12,16},{16,20},{20,24},{24,28},{28,0},{1,5},{5... | collective-permute-start | bytes 1572872 | tf_op jit(solution)/shard_map/ppermute | solution.py:184
  74.2 13.6 %collective-permute-start.2 = (bf16[1024,256]{1,0:T(8,128)(2,1)}, bf16[1024,256]{1,0:T(8,128)(2,1)S(1)}, u32[]{:S(2)}, u32[]{:S(2)}) collective-permute-start(bf16[1024,256]{1,0:T(8,128)(2,1)} %get-tuple-element.9), channel_id=1, source_target_pairs={{0,28},{4,0},{8,4},{12,8},{16,12},{20,16},{24,20},{28,24},{1,29},{... | collective-permute-start | bytes 1572872 | tf_op jit(solution)/shard_map/ppermute | solution.py:187
  78.0 14.4 %collective-permute-start.9 = (bf16[256,1024]{1,0:T(8,128)(2,1)S(1)}, bf16[256,1024]{1,0:T(8,128)(2,1)S(1)}, u32[]{:S(2)}, u32[]{:S(2)}) collective-permute-start(bf16[256,1024]{1,0:T(8,128)(2,1)S(1)} %pad_maximum_fusion.8), channel_id=1, source_target_pairs={{0,128},{128,0},{1,129},{129,1},{2,130},{130,2},{3,131},{131,3},{4... | collective-permute-start | bytes 1572872 | tf_op jit(solution)/shard_map/ppermute | solution.py:199
  80.2 13.7 %collective-permute-start.10 = (bf16[256,1024]{1,0:T(8,128)(2,1)S(1)}, bf16[256,1024]{1,0:T(8,128)(2,1)S(1)}, u32[]{:S(2)}, u32[]{:S(2)}) collective-permute-start(bf16[256,1024]{1,0:T(8,128)(2,1)S(1)} %pad_maximum_fusion.8), channel_id=1, source_target_pairs={{0,32},{32,64},{64,96},{96,0},{1,33},{33,65},{65,97},{97,1},{2,34}... | collective-permute-start | bytes 1572872 | tf_op jit(solution)/shard_map/ppermute | solution.py:200
  81.5 20.9 %collective-permute-start.11 = (bf16[256,1024]{1,0:T(8,128)(2,1)S(1)}, bf16[256,1024]{1,0:T(8,128)(2,1)S(1)}, u32[]{:S(2)}, u32[]{:S(2)}) collective-permute-start(bf16[256,1024]{1,0:T(8,128)(2,1)S(1)} %pad_maximum_fusion.8), channel_id=1, source_target_pairs={{0,96},{32,0},{64,32},{96,64},{1,97},{33,1},{65,33},{97,65},{2,98}... | collective-permute-start | bytes 1572872 | tf_op jit(solution)/shard_map/ppermute | solution.py:201
  87.7 14.7 %collective-permute-start.3 = (bf16[1024,256]{1,0:T(8,128)(2,1)S(1)}, bf16[1024,256]{1,0:T(8,128)(2,1)S(1)}, u32[]{:S(2)}, u32[]{:S(2)}) collective-permute-start(bf16[1024,256]{1,0:T(8,128)(2,1)S(1)} %collective-permute-done.1), channel_id=1, source_target_pairs={{0,4},{4,8},{8,12},{12,16},{16,20},{20,24},{24,28},{28,0},{1,5},{5... | collective-permute-start | bytes 1572872 | tf_op jit(solution)/shard_map/ppermute | solution.py:184
  87.7 14.7 %collective-permute-start.4 = (bf16[1024,256]{1,0:T(8,128)(2,1)S(1)}, bf16[1024,256]{1,0:T(8,128)(2,1)S(1)}, u32[]{:S(2)}, u32[]{:S(2)}) collective-permute-start(bf16[1024,256]{1,0:T(8,128)(2,1)S(1)} %collective-permute-done.2), channel_id=1, source_target_pairs={{0,28},{4,0},{8,4},{12,8},{16,12},{20,16},{24,20},{28,24},{1,29},{... | collective-permute-start | bytes 1572872 | tf_op jit(solution)/shard_map/ppermute | solution.py:187
  94.0 24.1 %collective-permute-start.12 = (bf16[2,256,1024]{2,1,0:T(8,128)(2,1)S(1)}, bf16[2,256,1024]{2,1,0:T(8,128)(2,1)S(1)}, u32[]{:S(2)}, u32[]{:S(2)}) collective-permute-start(bf16[2,256,1024]{2,1,0:T(8,128)(2,1)S(1)} %pad_maximum_fusion.4), channel_id=1, source_target_pairs={{0,32},{32,64},{64,96},{96,0},{1,33},{33,65},{65,97},{97,1},{2,34}... | collective-permute-start | bytes 3145736 | tf_op jit(solution)/shard_map/ppermute | solution.py:202
  95.4 12.5 %collective-permute-start.13 = (bf16[256,1024]{1,0:T(8,128)(2,1)S(1)}, bf16[256,1024]{1,0:T(8,128)(2,1)S(1)}, u32[]{:S(2)}, u32[]{:S(2)}) collective-permute-start(bf16[256,1024]{1,0:T(8,128)(2,1)S(1)} %collective-permute-done.9), channel_id=1, source_target_pairs={{0,96},{32,0},{64,32},{96,64},{1,97},{33,1},{65,33},{97,65},{2,98}... | collective-permute-start | bytes 1572872 | tf_op jit(solution)/shard_map/ppermute | solution.py:203
  102.4 13.8 %collective-permute-start.5 = (bf16[1024,256]{1,0:T(8,128)(2,1)S(1)}, bf16[1024,256]{1,0:T(8,128)(2,1)S(1)}, u32[]{:S(2)}, u32[]{:S(2)}) collective-permute-start(bf16[1024,256]{1,0:T(8,128)(2,1)S(1)} %collective-permute-done.3), channel_id=1, source_target_pairs={{0,4},{4,8},{8,12},{12,16},{16,20},{20,24},{24,28},{28,0},{1,5},{5... | collective-permute-start | bytes 1572872 | tf_op jit(solution)/shard_map/ppermute | solution.py:184
  102.5 13.8 %collective-permute-start.6 = (bf16[1024,256]{1,0:T(8,128)(2,1)S(1)}, bf16[1024,256]{1,0:T(8,128)(2,1)S(1)}, u32[]{:S(2)}, u32[]{:S(2)}) collective-permute-start(bf16[1024,256]{1,0:T(8,128)(2,1)S(1)} %collective-permute-done.4), channel_id=1, source_target_pairs={{0,28},{4,0},{8,4},{12,8},{16,12},{20,16},{24,20},{28,24},{1,29},{... | collective-permute-start | bytes 1572872 | tf_op jit(solution)/shard_map/ppermute | solution.py:187
  107.9 11.6 %collective-permute-start.14 = (bf16[256,1024]{1,0:T(8,128)(2,1)S(1)}, bf16[256,1024]{1,0:T(8,128)(2,1)S(1)}, u32[]{:S(2)}, u32[]{:S(2)}) collective-permute-start(bf16[256,1024]{1,0:T(8,128)(2,1)S(1)} %collective-permute-done.13), channel_id=1, source_target_pairs={{0,96},{32,0},{64,32},{96,64},{1,97},{33,1},{65,33},{97,65},{2,98}... | collective-permute-start | bytes 1572872 | tf_op jit(solution)/shard_map/ppermute | solution.py:204
  116.2 12.9 %collective-permute-start.7 = (bf16[1024,256]{1,0:T(8,128)(2,1)S(1)}, bf16[1024,256]{1,0:T(8,128)(2,1)S(1)}, u32[]{:S(2)}, u32[]{:S(2)}) collective-permute-start(bf16[1024,256]{1,0:T(8,128)(2,1)S(1)} %collective-permute-done.5), channel_id=1, source_target_pairs={{0,4},{4,8},{8,12},{12,16},{16,20},{20,24},{24,28},{28,0},{1,5},{5... | collective-permute-start | bytes 1572872 | tf_op jit(solution)/shard_map/ppermute | solution.py:184
  138.4 12.6 %collective-permute-start.17 = (bf16[512,256]{1,0:T(8,128)(2,1)S(1)}, bf16[512,256]{1,0:T(8,128)(2,1)S(1)}, u32[]{:S(2)}, u32[]{:S(2)}) collective-permute-start(bf16[512,256]{1,0:T(8,128)(2,1)S(1)} %get-tuple-element.21), channel_id=1, source_target_pairs={{0,1},{1,0},{2,3},{3,2},{4,5},{5,4},{6,7},{7,6},{8,9},{9,8},{10,11... | collective-permute-start | bytes 786440 | tf_op jit(solution)/shard_map/ppermute | solution.py:227
  154.4 12.8 %collective-permute-start.20 = (bf16[512,256]{1,0:T(8,128)(2,1)S(1)}, bf16[512,256]{1,0:T(8,128)(2,1)S(1)}, u32[]{:S(2)}, u32[]{:S(2)}) collective-permute-start(bf16[512,256]{1,0:T(8,128)(2,1)S(1)} %collective-permute-done.18), channel_id=1, source_target_pairs={{0,4},{4,8},{8,12},{12,16},{16,20},{20,24},{24,28},{28,0},{1,5},{5... | collective-permute-start | bytes 786440 | tf_op jit(solution)/shard_map/ppermute | solution.py:184
  154.5 12.8 %collective-permute-start.21 = (bf16[512,256]{1,0:T(8,128)(2,1)S(1)}, bf16[512,256]{1,0:T(8,128)(2,1)S(1)}, u32[]{:S(2)}, u32[]{:S(2)}) collective-permute-start(bf16[512,256]{1,0:T(8,128)(2,1)S(1)} %collective-permute-done.19), channel_id=1, source_target_pairs={{0,28},{4,0},{8,4},{12,8},{16,12},{20,16},{24,20},{28,24},{1,29},{... | collective-permute-start | bytes 786440 | tf_op jit(solution)/shard_map/ppermute | solution.py:187
  161.7 11.2 %collective-permute-start.27 = (bf16[512,256]{1,0:T(8,128)(2,1)S(1)}, bf16[512,256]{1,0:T(8,128)(2,1)S(1)}, u32[]{:S(2)}, u32[]{:S(2)}) collective-permute-start(bf16[512,256]{1,0:T(8,128)(2,1)S(1)} %collective-permute-done.25), channel_id=1, source_target_pairs={{0,4},{4,8},{8,12},{12,16},{16,20},{20,24},{24,28},{28,0},{1,5},{5... | collective-permute-start | bytes 786440 | tf_op jit(solution)/shard_map/ppermute | solution.py:184
  161.7 11.2 %collective-permute-start.28 = (bf16[512,256]{1,0:T(8,128)(2,1)S(1)}, bf16[512,256]{1,0:T(8,128)(2,1)S(1)}, u32[]{:S(2)}, u32[]{:S(2)}) collective-permute-start(bf16[512,256]{1,0:T(8,128)(2,1)S(1)} %collective-permute-done.26), channel_id=1, source_target_pairs={{0,28},{4,0},{8,4},{12,8},{16,12},{20,16},{24,20},{28,24},{1,29},{... | collective-permute-start | bytes 786440 | tf_op jit(solution)/shard_map/ppermute | solution.py:187
  167.3 11.2 %collective-permute-start.22 = (bf16[512,256]{1,0:T(8,128)(2,1)S(1)}, bf16[512,256]{1,0:T(8,128)(2,1)S(1)}, u32[]{:S(2)}, u32[]{:S(2)}) collective-permute-start(bf16[512,256]{1,0:T(8,128)(2,1)S(1)} %collective-permute-done.20), channel_id=1, source_target_pairs={{0,4},{4,8},{8,12},{12,16},{16,20},{20,24},{24,28},{28,0},{1,5},{5... | collective-permute-start | bytes 786440 | tf_op jit(solution)/shard_map/ppermute | solution.py:184
  167.3 18.1 %collective-permute-start.23 = (bf16[512,256]{1,0:T(8,128)(2,1)S(1)}, bf16[512,256]{1,0:T(8,128)(2,1)S(1)}, u32[]{:S(2)}, u32[]{:S(2)}) collective-permute-start(bf16[512,256]{1,0:T(8,128)(2,1)S(1)} %collective-permute-done.21), channel_id=1, source_target_pairs={{0,28},{4,0},{8,4},{12,8},{16,12},{20,16},{24,20},{28,24},{1,29},{... | collective-permute-start | bytes 786440 | tf_op jit(solution)/shard_map/ppermute | solution.py:187
  172.9 12.5 %collective-permute-start.29 = (bf16[512,256]{1,0:T(8,128)(2,1)S(1)}, bf16[512,256]{1,0:T(8,128)(2,1)S(1)}, u32[]{:S(2)}, u32[]{:S(2)}) collective-permute-start(bf16[512,256]{1,0:T(8,128)(2,1)S(1)} %collective-permute-done.27), channel_id=1, source_target_pairs={{0,4},{4,8},{8,12},{12,16},{16,20},{20,24},{24,28},{28,0},{1,5},{5... | collective-permute-start | bytes 786440 | tf_op jit(solution)/shard_map/ppermute | solution.py:184
  195.6 15.6 %collective-permute-start.33 = (bf16[1024,256]{1,0:T(8,128)(2,1)S(1)}, bf16[1024,256]{1,0:T(8,128)(2,1)S(1)}, u32[]{:S(2)}, u32[]{:S(2)}) collective-permute-start(bf16[1024,256]{1,0:T(8,128)(2,1)S(1)} %fusion.13), channel_id=1, source_target_pairs={{0,1},{1,0},{2,3},{3,2},{4,5},{5,4},{6,7},{7,6},{8,9},{9,8},{10,11... | collective-permute-start | bytes 1572872 | tf_op jit(solution)/shard_map/ppermute | solution.py:227
  (15 other events, 143.4 us)

commit v4 on v3

--- a/solution.py
+++ b/solution.py
@@ -27,22 +27,34 @@
     return out
 
 
-def contribute_kernel(pos_ref, block_ref, left_ref, right_ref, weight_ref, out_ref):
-    out_ref[...] = jnp.full(out_ref.shape, 32.0, out_ref.dtype)
+def contribute_kernel(owner_ref, block_ref, left_ref, right_ref, weight_ref, out_ref, count_ref, tag_ref):
+    owners = count_ref.shape[0]
     group = lanes_group((8, 128))
     sub = lax.broadcasted_iota(jnp.int32, (8, 128), 0)
     lane = lax.broadcasted_iota(jnp.int32, (8, 128), 1)
 
+    def clear(o, carry):
+        for u in range(8):
+            count_ref[o * 8 + u] = 0
+            tag_ref[o * 16 + 2 * u] = 512
+            tag_ref[o * 16 + 2 * u + 1] = 512
+            for slot in range(2):
+                out_ref[(o * 8 + u) * 3 + slot] = jnp.zeros((8, 128), jnp.bfloat16)
+        return carry
+
+    lax.fori_loop(0, owners // 8, clear, 0)
+
     def body(g, carry):
-        base = pl.multiple_of(g * 8, 8)
-        w = weight_ref[pl.ds(base, 8), :]
-        left = left_ref[pl.ds(base, 8)].astype(jnp.float32) * w[:, None, :]
-        left = left.astype(jnp.bfloat16).reshape(256, 128)
-        right = right_ref[pl.ds(base, 8)].reshape(256, 128)
-        for half in range(2):
+        base = pl.multiple_of(g * 16, 16)
+        w = weight_ref[pl.ds(base, 16), :]
+        left = left_ref[pl.ds(base, 16)].astype(jnp.float32) * w[:, None, :]
+        left = left.astype(jnp.bfloat16).reshape(512, 128)
+        right = right_ref[pl.ds(base, 16)].reshape(512, 128)
+        tiles = []
+        for part in range(4):
             c = lax.dot_general(
-                left[half * 128 : half * 128 + 128],
-                right[half * 128 : half * 128 + 128],
+                left[part * 128 : part * 128 + 128],
+                right[part * 128 : part * 128 + 128],
                 (((1,), (1,)), ((), ())),
                 preferred_element_type=jnp.float32,
             )
@@ -52,26 +64,34 @@
                     rows[k] if k == t else pltpu.roll(rows[k], (32 * (k - t)) % 128, 1)
                     for k in range(4)
                 ]
-                task = base + half * 4 + t
-                owner, slot = pos_ref[task] >> 1, pos_ref[task] & 1
-                out_ref[owner * 3 + slot] = pick(rows, group).astype(jnp.bfloat16)
-                block = block_ref[task]
-                high = (block >> 4).astype(jnp.float32)
-                low = (block & 15).astype(jnp.float32)
-                tag = out_ref[owner * 3 + 2].astype(jnp.float32)
-                tag = jnp.where(sub == slot, jnp.where(lane == 0, high, low), tag)
-                out_ref[owner * 3 + 2] = tag.astype(jnp.bfloat16)
-        return carry
-
-    lax.fori_loop(0, 16, body, 0)
-
-
-def accumulate(acc_ref, label_ref, slot_ref, stride):
+                tiles.append(pick(rows, group).astype(jnp.bfloat16))
+        for t, tile in enumerate(tiles):
+            owner = owner_ref[base + t]
+            slot = count_ref[owner]
+            count_ref[owner] = slot + 1
+            tag_ref[owner * 2 + slot] = block_ref[base + t]
+            out_ref[owner * 3 + slot] = tile
+        return carry
+
+    lax.fori_loop(0, left_ref.shape[0] // 16, body, 0)
+
+    def label(o, carry):
+        for u in range(8):
+            tags = [tag_ref[o * 16 + 2 * u + slot] for slot in range(2)]
+            high = jnp.where(sub == 0, tags[0] >> 4, tags[1] >> 4)
+            low = jnp.where(sub == 0, tags[0] & 15, tags[1] & 15)
+            tile = jnp.where(lane == 0, high, low).astype(jnp.float32)
+            out_ref[(o * 8 + u) * 3 + 2] = tile.astype(jnp.bfloat16)
+        return carry
+
+    lax.fori_loop(0, owners // 8, label, 0)
+
+
+def accumulate(acc_ref, label_ref, slot_ref):
     def body(s, carry):
         for u in range(8):
             n = label_ref[s * 8 + u]
-            at = (s * 4 + u // 2) * stride + u % 2
-            acc_ref[n] = acc_ref[n] + slot_ref[at].astype(jnp.float32)
+            acc_ref[n] = acc_ref[n] + slot_ref[(s * 4 + u // 2) * 3 + u % 2].astype(jnp.float32)
         return carry
 
     lax.fori_loop(0, label_ref.shape[0] // 8, body, 0)
@@ -79,15 +99,30 @@
 
 def collect_kernel(label_ref, slot_ref, acc_ref):
     acc_ref[...] = jnp.zeros_like(acc_ref)
-    accumulate(acc_ref, label_ref, slot_ref, 3)
+    accumulate(acc_ref, label_ref, slot_ref)
 
 
 def assemble_kernel(
     place_ref, mask_ref, label_ref, slot_ref, first_ref, core_ref,
-    ks_ref, own_ref, panel_ref, pattern_ref, acc_ref, *, scale,
+    ks_ref, own_ref, panel_ref, pattern_ref, even_ref, odd_ref, *, scale,
 ):
-    acc_ref[...] = first_ref[...]
-    accumulate(acc_ref, label_ref, slot_ref, 2)
+    step = pl.program_id(0)
+
+    @pl.when(step == 0)
+    def _():
+        even_ref[...] = jnp.zeros_like(even_ref)
+        odd_ref[...] = jnp.zeros_like(odd_ref)
+
+        def add(s, carry):
+            for u in range(4):
+                at = s * 8 + 2 * u
+                n, m = label_ref[at], label_ref[at + 1]
+                even_ref[n] = even_ref[n] + slot_ref[at].astype(jnp.float32)
+                odd_ref[m] = odd_ref[m] + slot_ref[at + 1].astype(jnp.float32)
+            return carry
+
+        lax.fori_loop(0, label_ref.shape[0] // 8, add, 0)
+
     row, col, half_own = place_ref[0], place_ref[1], place_ref[2]
     group = lanes_group((8, 128))
     sub = lax.broadcasted_iota(jnp.int32, (8, 128), 0)
@@ -96,16 +131,15 @@
 
     def body(i, carry):
         r0 = pl.multiple_of(i * 32, 32)
-        quarter = i // 8
-        q0 = pl.multiple_of((i % 8) * 32, 32)
         for side in range(2):
             half = half_own if side == 0 else 1 - half_own
             for jt in range(2):
-                n = i * 16 + half * 8 + jt * 4
-                blocks = [acc_ref[n + j] for j in range(4)]
+                near = i * 16 + half * 8 + jt * 4
+                n = step * 128 + near
+                blocks = [first_ref[near + j] + (even_ref[n + j] + odd_ref[n + j]) for j in range(4)]
                 pat = pick([jnp.full((8, 128), mask_ref[n + j]) for j in range(4)], group)
                 c0 = pl.multiple_of(half * 256 + jt * 128, 128)
-                gap = col * 512 + c0 - row * 1024 - r0
+                gap = col * 512 + c0 - row * 1024 - step * 256 - r0
                 ks_rows, x_rows = [], []
                 for t in range(4):
                     turned = [
@@ -117,7 +151,7 @@
                     ks_rows.append(ks)
                     x_rows.append(pat * (identity - scale * ks))
                 x = jnp.concatenate(x_rows, axis=0).astype(jnp.bfloat16)
-                panel_ref[quarter, pl.ds(q0, 32), side * 256 + jt * 128 : side * 256 + jt * 128 + 128] = x
+                panel_ref[0, pl.ds(r0, 32), side * 256 + jt * 128 : side * 256 + jt * 128 + 128] = x
                 if side == 0:
                     at = slice(jt * 128, jt * 128 + 128)
                     ks_ref[pl.ds(r0, 32), at] = jnp.concatenate(ks_rows, axis=0)
@@ -127,22 +161,23 @@
                     )
         return carry
 
-    lax.fori_loop(0, 32, body, 0)
+    lax.fori_loop(0, 8, body, 0, unroll=2)
 
 
 VMEM = pl.BlockSpec(memory_space=pltpu.VMEM)
 SMEM = pl.BlockSpec(memory_space=pltpu.SMEM)
 
 
-def contribute(pos, block, left, right, weight):
+def contribute(owner, block, left, right, weight):
     tasks = left.shape[0]
     return pl.pallas_call(
         contribute_kernel,
         out_shape=jax.ShapeDtypeStruct((3 * tasks, 8, 128), jnp.bfloat16),
         in_specs=[SMEM, SMEM, VMEM, VMEM, VMEM],
         out_specs=VMEM,
+        scratch_shapes=[pltpu.SMEM((tasks,), jnp.int32), pltpu.SMEM((2 * tasks,), jnp.int32)],
         name="contribute",
-    )(pos, block, left, right, weight)
+    )(owner, block, left, right, weight)
 
 
 def collect(labels, slots):
@@ -157,6 +192,9 @@
 
 
 def assemble(place, mask, labels, slots, first, core):
+    def quarter(i):
+        return (i, 0)
+
     return pl.pallas_call(
         functools.partial(assemble_kernel, scale=COUPLING / math.sqrt(NBLK * BS)),
         out_shape=(
@@ -165,9 +203,19 @@
             jax.ShapeDtypeStruct((4, 256, 512), jnp.bfloat16),
             jax.ShapeDtypeStruct((1024, 256), jnp.bfloat16),
         ),
-        in_specs=[SMEM, SMEM, SMEM, VMEM, VMEM, VMEM],
-        out_specs=(VMEM, VMEM, VMEM, VMEM),
-        scratch_shapes=[pltpu.VMEM((520, 8, 128), jnp.float32)],
+        grid=(4,),
+        in_specs=[
+            SMEM, SMEM, SMEM, VMEM,
+            pl.BlockSpec((128, 8, 128), lambda i: (i, 0, 0)),
+            pl.BlockSpec((256, 512), quarter),
+        ],
+        out_specs=(
+            pl.BlockSpec((256, 256), quarter),
+            pl.BlockSpec((256, 256), quarter),
+            pl.BlockSpec((1, 256, 512), lambda i: (i, 0, 0)),
+            pl.BlockSpec((256, 256), quarter),
+        ),
+        scratch_shapes=[pltpu.VMEM((520, 8, 128), jnp.float32)] * 2,
         name="assemble",
     )(place, mask, labels, slots, first, core)
 
@@ -218,14 +266,17 @@
 
 def product(a, b, chunks):
     far = lax.ppermute(dot(a, b[:, :, 512:]).astype(jnp.bfloat16), "core", SWAP)
-    part = dot(a, b[:, :, 256:512]) + far[:, 256:].astype(jnp.float32)
-    rest = dot(a, b[:, :, :256]) + far[:, :256].astype(jnp.float32)
-    step = part.shape[0] // chunks
+    near = lax.optimization_barrier(dot(a, b[:, :, :512]))
+    step = a.shape[1] // chunks
     out = []
     for m in range(chunks):
         rows = slice(step * m, step * m + step)
-        away = lax.ppermute(part[rows].astype(jnp.bfloat16), "yhi", SWAP)
-        out.append((rest[rows], away))
+        part = near[rows, 256:] + far[rows, 256:].astype(jnp.float32)
+        part = part.astype(jnp.bfloat16)
+        if m > 0:
+            part, _ = lax.optimization_barrier((part, out[-1][2]))
+        away = lax.ppermute(part, "yhi", SWAP)
+        out.append((near[rows, :256], far[rows, :256], away))
     return out
 
 
@@ -234,12 +285,7 @@
     row, col = ylo * 4 + x, z * 2 + core
     tasks = basis_left.shape[0]
 
-    target = task_owner[:, 0]
-    order = jnp.arange(tasks, dtype=jnp.int32)
-    earlier = (target[:, None] == target[None, :]) & (order[None, :] < order[:, None])
-    pos = target * 2 + jnp.sum(earlier.astype(jnp.int32), axis=1)
-
-    outgoing = contribute(pos, task_block, basis_left, basis_right, grid_weight)
+    outgoing = contribute(task_owner[:, 0], task_block, basis_left, basis_right, grid_weight)
     arrived = lax.all_to_all(
         outgoing.reshape(tasks, 3, 8, 128), AXES[:4], split_axis=0, concat_axis=0, tiled=True
     )
@@ -268,14 +314,14 @@
     unit = jnp.concatenate([keep, lax.ppermute(give, "core", SWAP)], axis=1)
     b = gather_rows(unit, ylo, x, z)
     squares = []
-    for m, (rest, away) in enumerate(product(gather_z(own, True), b, 2)):
+    for m, (near, far, away) in enumerate(product(gather_z(own, True), b, 2)):
         if m > 0:
             away, _ = lax.optimization_barrier((away, squares[0]))
         mask = pattern[512 * m : 512 * m + 512].astype(jnp.float32)
-        squares.append(mask * (rest + away.astype(jnp.float32)))
+        squares.append(mask * (near + far.astype(jnp.float32) + away.astype(jnp.float32)))
     a2 = [gather_z(square.astype(jnp.bfloat16), m == 0) for m, square in enumerate(squares)]
-    ((rest, away),) = product(jnp.concatenate(a2, axis=1), b, 1)
-    cube_term = pattern.astype(jnp.float32) * (rest + away.astype(jnp.float32))
+    ((near, far, away),) = product(jnp.concatenate(a2, axis=1), b, 1)
+    cube_term = pattern.astype(jnp.float32) * (near + far.astype(jnp.float32) + away.astype(jnp.float32))
     return (ks_out, 3.0 * jnp.concatenate(squares, axis=0) - 2.0 * cube_term)
 
 

time: 214 us -> 208 us (0.972)
  Pallas kernels: 19.9 us -> 15.9 us
  waiting for transfers between devices: 108 us -> 105 us
  starting transfers between devices: 64.7 us -> 67.4 us
    ppermute x2, waiting for transfers between devices: 5.29 us -> 0.64 us  [product(): far = lax.ppermute(dot(a, b[:, :, 512:]).astype(jnp.bfloat16), 'core', SWAP)]
    ppermute x3, waiting for transfers between devices: 19.8 us -> 22.4 us  [product(): away = lax.ppermute(part, 'yhi', SWAP)]
    ppermute x3, starting transfers between devices: 6.57 us -> 8.79 us  [product(): away = lax.ppermute(part, 'yhi', SWAP)]
    pallas_call x1, Pallas kernels: 9.26 us -> 7.05 us  [assemble(): pl.pallas_call(functools.partial(assemble_kernel, scale=COUPLING / math.s...]
    dot_general x6 -> x4, matrix products: 10.7 us -> 9.3 us  [dot(): return jnp.einsum('dmk,dkn->mn', a, b, preferred_element_type=jnp.float32)]
  transfers between devices with their start and end apart: 35 -> 35, of which waited for: 24 -> 24; matrix products, arithmetic and copies ran while one was open for 3% -> 5% of each run, Pallas kernels for 2% -> 2%
where the time goes in v4:
time: 208 us
  waiting for transfers between devices  105 us (50%)
  starting transfers between devices  67.4 us (32%)
  Pallas kernels  15.9 us (8%)
  matrix products  9.3 us (4%)
  local copies, waits for them, and re-layouts  4.57 us (2%)
  other arithmetic  4.49 us (2%)
    ppermute x11, waiting for transfers between devices, gather_z(): up = lax.ppermute(up, 'z', ring_of(8, 1))  41.7 us
    ppermute x10, starting transfers between devices, gather_z(): down = lax.ppermute(down, 'z', ring_of(8, -1))  31 us
    ppermute x3, waiting for transfers between devices, product(): away = lax.ppermute(part, 'yhi', SWAP)  22.4 us
    all_to_all x1, waiting for transfers between devices, local(): lax.all_to_all(outgoing.reshape(tasks, 3, 8, 128), AXES[:4], split_axis=0...  22.2 us
    all_to_all x1, starting transfers between devices, local(): lax.all_to_all(outgoing.reshape(tasks, 3, 8, 128), AXES[:4], split_axis=0...  13.8 us
    dot_general x4, matrix products, dot(): return jnp.einsum('dmk,dkn->mn', a, b, preferred_element_type=jnp.float32)  9.3 us
    ppermute x3, starting transfers between devices, product(): away = lax.ppermute(part, 'yhi', SWAP)  8.79 us
    ppermute x1, waiting for transfers between devices, local(): far = lax.ppermute(jnp.concatenate([slots, tag_tile], axis=0), 'yhi', SWAP)  7.15 us
  transfers between devices with their start and end apart: 35, of which 24 were waited for; matrix products, arithmetic and copies ran while one was open for 5% of the time, Pallas kernels for 2%

profile of v4, /device:TPU:2, one launch (start us, length us, event | category | flops | bytes accessed | tf_op | source)
XLA Modules:
  0.0 208.2 jit_solution(6059878904816468723)
XLA Ops:
  0.6 5.4 %contribute.1 = bf16[384,8,128]{2,1,0:T(8,128)(2,1)} custom-call(s32[128]{0:T(128)} %bitcast.91, s32[128]{0:T(128)} %block_ref.1, bf16[128,32,128]{2,1,0:T(8,128)(2,1)} %left_ref.1, bf16[128,32,128]{2,1,0:T(8,128)(2,1)} %right_ref.1, f32[128,128]{1,0:T(8,128)} %weight_ref.1), custom_call_target="tpu_custom_call" | custom-call | tf_op jit(solution)/shard_map/contribute/pallas_call | solution.py:173
  6.1 13.8 %all-to-all-start = ((bf16[128,3,8,128]{3,2,1,0:T(8,128)(2,1)}), bf16[128,3,8,128]{3,2,1,0:T(8,128)(2,1)S(1)}, u32[]{:S(2)}, u32[]{:S(2)}) async-start(bf16[128,3,8,128]{3,2,1,0:T(8,128)(2,1)} %bitcast.86), calls=%async_computation | async-start | bytes 1572864 | tf_op jit(solution)/shard_map/all_to_all | solution.py:289
  19.9 22.2 %all-to-all-done = bf16[128,3,8,128]{3,2,1,0:T(8,128)(2,1)S(1)} async-done(((bf16[128,3,8,128]{3,2,1,0:T(8,128)(2,1)}), bf16[128,3,8,128]{3,2,1,0:T(8,128)(2,1)S(1)}, u32[]{:S(2)}, u32[]{:S(2)}) %all-to-all-start) | async-done | bytes 786464 | tf_op jit(solution)/shard_map/all_to_all | solution.py:289
  42.4 3.0 %collective-permute-start = (bf16[257,8,128]{2,1,0:T(8,128)(2,1)S(1)}, bf16[257,8,128]{2,1,0:T(8,128)(2,1)S(1)}, u32[]{:S(2)}, u32[]{:S(2)}) collective-permute-start(bf16[257,8,128]{2,1,0:T(8,128)(2,1)S(1)} %pad_maximum_fusion.8), channel_id=1, source_target_pairs={{0,1},{1,0},{2,3},{3,2},{4,5},{5,4},{6,7},{7,6},{8,9},{9,8},{10,11... | collective-permute-start | bytes 1579016 | tf_op jit(solution)/shard_map/ppermute | solution.py:295
  47.7 3.4 %collect.1.first_ref = f32[520,8,128]{2,1,0:T(8,128)} custom-call(s32[256]{0:T(256)} %fusion.31.label_ref, bf16[384,8,128]{2,1,0:T(8,128)(2,1)} %bitcast.85), custom_call_target="tpu_custom_call" | custom-call | flops 1048576 | bytes 8388608 | tf_op jit(solution)/shard_map/collect/pallas_call | solution.py:184
  51.1 7.1 %collective-permute-done.slot_ref = bf16[257,8,128]{2,1,0:T(8,128)(2,1)S(1)} collective-permute-done((bf16[257,8,128]{2,1,0:T(8,128)(2,1)S(1)}, bf16[257,8,128]{2,1,0:T(8,128)(2,1)S(1)}, u32[]{:S(2)}, u32[]{:S(2)}) %collective-permute-start) | collective-permute-done | bytes 526368 | tf_op jit(solution)/shard_map/ppermute | solution.py:295
  59.2 7.0 %assemble.1 = (f32[1024,256]{1,0:T(8,128)}, bf16[1024,256]{1,0:T(8,128)(2,1)}, bf16[4,256,512]{2,1,0:T(8,128)(2,1)}, bf16[1024,256]{1,0:T(8,128)(2,1)}) custom-call(s32[3]{0:T(128)} %pad_add_fusion.place_ref, f32[512]{0:T(512)} %reshape.48.mask_ref, s32[256]{0:T(256)} %fusion.34.label_ref, bf16[257,8,128]{2,1,0:T(8,128)(2,1)} %copy-done.2, ...), custom_call_target="tpu_custom_call" | custom-call | tf_op jit(solution)/shard_map/assemble/pallas_call | solution.py:198
  77.4 4.8 %collective-permute-done.1 = bf16[1024,256]{1,0:T(8,128)(2,1)S(1)} collective-permute-done((bf16[1024,256]{1,0:T(8,128)(2,1)}, bf16[1024,256]{1,0:T(8,128)(2,1)S(1)}, u32[]{:S(2)}, u32[]{:S(2)}) %collective-permute-start.1) | collective-permute-done | bytes 524320 | tf_op jit(solution)/shard_map/ppermute | solution.py:232
  82.2 3.2 %collective-permute-start.4 = (bf16[1024,256]{1,0:T(8,128)(2,1)S(1)}, bf16[1024,256]{1,0:T(8,128)(2,1)S(1)}, u32[]{:S(2)}, u32[]{:S(2)}) collective-permute-start(bf16[1024,256]{1,0:T(8,128)(2,1)S(1)} %collective-permute-done.2), channel_id=1, source_target_pairs={{0,28},{4,0},{8,4},{12,8},{16,12},{20,16},{24,20},{28,24},{1,29},{... | collective-permute-start | bytes 1572872 | tf_op jit(solution)/shard_map/ppermute | solution.py:235
  90.7 6.3 %collective-permute-done.3 = bf16[1024,256]{1,0:T(8,128)(2,1)S(1)} collective-permute-done((bf16[1024,256]{1,0:T(8,128)(2,1)S(1)}, bf16[1024,256]{1,0:T(8,128)(2,1)S(1)}, u32[]{:S(2)}, u32[]{:S(2)}) %collective-permute-start.3) | collective-permute-done | bytes 524320 | tf_op jit(solution)/shard_map/ppermute | solution.py:232
  97.1 3.3 %collective-permute-start.6 = (bf16[1024,256]{1,0:T(8,128)(2,1)S(1)}, bf16[1024,256]{1,0:T(8,128)(2,1)S(1)}, u32[]{:S(2)}, u32[]{:S(2)}) collective-permute-start(bf16[1024,256]{1,0:T(8,128)(2,1)S(1)} %collective-permute-done.4), channel_id=1, source_target_pairs={{0,28},{4,0},{8,4},{12,8},{16,12},{20,16},{24,20},{28,24},{1,29},{... | collective-permute-start | bytes 1572872 | tf_op jit(solution)/shard_map/ppermute | solution.py:235
  103.6 7.5 %collective-permute-done.5 = bf16[1024,256]{1,0:T(8,128)(2,1)S(1)} collective-permute-done((bf16[1024,256]{1,0:T(8,128)(2,1)S(1)}, bf16[1024,256]{1,0:T(8,128)(2,1)S(1)}, u32[]{:S(2)}, u32[]{:S(2)}) %collective-permute-start.5) | collective-permute-done | bytes 524320 | tf_op jit(solution)/shard_map/ppermute | solution.py:232
  114.1 10.1 %collective-permute-done.7 = bf16[1024,256]{1,0:T(8,128)(2,1)S(1)} collective-permute-done((bf16[1024,256]{1,0:T(8,128)(2,1)S(1)}, bf16[1024,256]{1,0:T(8,128)(2,1)S(1)}, u32[]{:S(2)}, u32[]{:S(2)}) %collective-permute-start.7) | collective-permute-done | bytes 524320 | tf_op jit(solution)/shard_map/ppermute | solution.py:232
  129.5 3.0 %collective-permute-start.16 = (bf16[512,256]{1,0:T(8,128)(2,1)S(1)}, bf16[512,256]{1,0:T(8,128)(2,1)S(1)}, u32[]{:S(2)}, u32[]{:S(2)}) collective-permute-start(bf16[512,256]{1,0:T(8,128)(2,1)S(1)} %get-tuple-element.20), channel_id=1, source_target_pairs={{0,1},{1,0},{2,3},{3,2},{4,5},{5,4},{6,7},{7,6},{8,9},{9,8},{10,11... | collective-permute-start | bytes 786440 | tf_op jit(solution)/shard_map/ppermute | solution.py:278
  132.5 7.0 %collective-permute-done.16 = bf16[512,256]{1,0:T(8,128)(2,1)S(1)} collective-permute-done((bf16[512,256]{1,0:T(8,128)(2,1)S(1)}, bf16[512,256]{1,0:T(8,128)(2,1)S(1)}, u32[]{:S(2)}, u32[]{:S(2)}) %collective-permute-start.16) | collective-permute-done | bytes 262176 | tf_op jit(solution)/shard_map/ppermute | solution.py:278
  142.6 3.2 %collective-permute-start.19 = (bf16[512,256]{1,0:T(8,128)(2,1)S(1)}, bf16[512,256]{1,0:T(8,128)(2,1)S(1)}, u32[]{:S(2)}, u32[]{:S(2)}) collective-permute-start(bf16[512,256]{1,0:T(8,128)(2,1)S(1)} %get-tuple-element.15), channel_id=1, source_target_pairs={{0,28},{4,0},{8,4},{12,8},{16,12},{20,16},{24,20},{28,24},{1,29},{... | collective-permute-start | bytes 786440 | tf_op jit(solution)/shard_map/ppermute | solution.py:235
  148.8 3.2 %collective-permute-start.26 = (bf16[512,256]{1,0:T(8,128)(2,1)S(1)}, bf16[512,256]{1,0:T(8,128)(2,1)S(1)}, u32[]{:S(2)}, u32[]{:S(2)}) collective-permute-start(bf16[512,256]{1,0:T(8,128)(2,1)S(1)} %get-tuple-element.18), channel_id=1, source_target_pairs={{0,28},{4,0},{8,4},{12,8},{16,12},{20,16},{24,20},{28,24},{1,29},{... | collective-permute-start | bytes 786440 | tf_op jit(solution)/shard_map/ppermute | solution.py:235
  152.0 3.5 %collective-permute-start.21 = (bf16[512,256]{1,0:T(8,128)(2,1)S(1)}, bf16[512,256]{1,0:T(8,128)(2,1)S(1)}, u32[]{:S(2)}, u32[]{:S(2)}) collective-permute-start(bf16[512,256]{1,0:T(8,128)(2,1)S(1)} %collective-permute-done.19), channel_id=1, source_target_pairs={{0,28},{4,0},{8,4},{12,8},{16,12},{20,16},{24,20},{28,24},{1,29},{... | collective-permute-start | bytes 786440 | tf_op jit(solution)/shard_map/ppermute | solution.py:235
  155.6 3.6 %collective-permute-done.25 = bf16[512,256]{1,0:T(8,128)(2,1)S(1)} collective-permute-done((bf16[512,256]{1,0:T(8,128)(2,1)S(1)}, bf16[512,256]{1,0:T(8,128)(2,1)S(1)}, u32[]{:S(2)}, u32[]{:S(2)}) %collective-permute-start.25) | collective-permute-done | bytes 262176 | tf_op jit(solution)/shard_map/ppermute | solution.py:232
  159.3 3.3 %collective-permute-start.28 = (bf16[512,256]{1,0:T(8,128)(2,1)S(1)}, bf16[512,256]{1,0:T(8,128)(2,1)S(1)}, u32[]{:S(2)}, u32[]{:S(2)}) collective-permute-start(bf16[512,256]{1,0:T(8,128)(2,1)S(1)} %collective-permute-done.26), channel_id=1, source_target_pairs={{0,28},{4,0},{8,4},{12,8},{16,12},{20,16},{24,20},{28,24},{1,29},{... | collective-permute-start | bytes 786440 | tf_op jit(solution)/shard_map/ppermute | solution.py:235
  164.9 3.3 %collective-permute-start.23 = (bf16[512,256]{1,0:T(8,128)(2,1)S(1)}, bf16[512,256]{1,0:T(8,128)(2,1)S(1)}, u32[]{:S(2)}, u32[]{:S(2)}) collective-permute-start(bf16[512,256]{1,0:T(8,128)(2,1)S(1)} %collective-permute-done.21), channel_id=1, source_target_pairs={{0,28},{4,0},{8,4},{12,8},{16,12},{20,16},{24,20},{28,24},{1,29},{... | collective-permute-start | bytes 786440 | tf_op jit(solution)/shard_map/ppermute | solution.py:235
  170.5 3.3 %collective-permute-start.30 = (bf16[512,256]{1,0:T(8,128)(2,1)S(1)}, bf16[512,256]{1,0:T(8,128)(2,1)S(1)}, u32[]{:S(2)}, u32[]{:S(2)}) collective-permute-start(bf16[512,256]{1,0:T(8,128)(2,1)S(1)} %collective-permute-done.28), channel_id=1, source_target_pairs={{0,28},{4,0},{8,4},{12,8},{16,12},{20,16},{24,20},{28,24},{1,29},{... | collective-permute-start | bytes 786440 | tf_op jit(solution)/shard_map/ppermute | solution.py:235
  178.5 3.7 %collective-permute-start.31 = (bf16[512,256]{1,0:T(8,128)(2,1)S(1)}, bf16[512,256]{1,0:T(8,128)(2,1)S(1)}, u32[]{:S(2)}, u32[]{:S(2)}) collective-permute-start(bf16[512,256]{1,0:T(8,128)(2,1)S(1)} %collective-permute-done.30), channel_id=1, source_target_pairs={{0,28},{4,0},{8,4},{12,8},{16,12},{20,16},{24,20},{28,24},{1,29},{... | collective-permute-start | bytes 786440 | tf_op jit(solution)/shard_map/ppermute | solution.py:235
  194.2 12.7 %collective-permute-done.33 = bf16[1024,256]{1,0:T(8,128)(2,1)S(1)} collective-permute-done((bf16[1024,256]{1,0:T(8,128)(2,1)S(1)}, bf16[1024,256]{1,0:T(8,128)(2,1)S(1)}, u32[]{:S(2)}, u32[]{:S(2)}) %collective-permute-start.33) | collective-permute-done | bytes 524320 | tf_op jit(solution)/shard_map/ppermute | solution.py:278
  (116 shorter events, 60.0 us)
Async XLA Ops:
  6.1 36.1 %all-to-all-start = ((bf16[128,3,8,128]{3,2,1,0:T(8,128)(2,1)}), bf16[128,3,8,128]{3,2,1,0:T(8,128)(2,1)S(1)}, u32[]{:S(2)}, u32[]{:S(2)}) async-start(bf16[128,3,8,128]{3,2,1,0:T(8,128)(2,1)} %bitcast.86), calls=%async_computation | async-start | bytes 1572864 | tf_op jit(solution)/shard_map/all_to_all | solution.py:289
  42.4 15.8 %collective-permute-start = (bf16[257,8,128]{2,1,0:T(8,128)(2,1)S(1)}, bf16[257,8,128]{2,1,0:T(8,128)(2,1)S(1)}, u32[]{:S(2)}, u32[]{:S(2)}) collective-permute-start(bf16[257,8,128]{2,1,0:T(8,128)(2,1)S(1)} %pad_maximum_fusion.8), channel_id=1, source_target_pairs={{0,1},{1,0},{2,3},{3,2},{4,5},{5,4},{6,7},{7,6},{8,9},{9,8},{10,11... | collective-permute-start | bytes 1579016 | tf_op jit(solution)/shard_map/ppermute | solution.py:295
  66.2 16.0 %collective-permute-start.1 = (bf16[1024,256]{1,0:T(8,128)(2,1)}, bf16[1024,256]{1,0:T(8,128)(2,1)S(1)}, u32[]{:S(2)}, u32[]{:S(2)}) collective-permute-start(bf16[1024,256]{1,0:T(8,128)(2,1)} %get-tuple-element.10), channel_id=1, source_target_pairs={{0,4},{4,8},{8,12},{12,16},{16,20},{20,24},{24,28},{28,0},{1,5},{5... | collective-permute-start | bytes 1572872 | tf_op jit(solution)/shard_map/ppermute | solution.py:232
  68.7 13.5 %collective-permute-start.2 = (bf16[1024,256]{1,0:T(8,128)(2,1)}, bf16[1024,256]{1,0:T(8,128)(2,1)S(1)}, u32[]{:S(2)}, u32[]{:S(2)}) collective-permute-start(bf16[1024,256]{1,0:T(8,128)(2,1)} %get-tuple-element.10), channel_id=1, source_target_pairs={{0,28},{4,0},{8,4},{12,8},{16,12},{20,16},{24,20},{28,24},{1,29},{... | collective-permute-start | bytes 1572872 | tf_op jit(solution)/shard_map/ppermute | solution.py:235
  72.2 14.7 %collective-permute-start.9 = (bf16[256,1024]{1,0:T(8,128)(2,1)S(1)}, bf16[256,1024]{1,0:T(8,128)(2,1)S(1)}, u32[]{:S(2)}, u32[]{:S(2)}) collective-permute-start(bf16[256,1024]{1,0:T(8,128)(2,1)S(1)} %pad_maximum_fusion.9), channel_id=1, source_target_pairs={{0,128},{128,0},{1,129},{129,1},{2,130},{130,2},{3,131},{131,3},{4... | collective-permute-start | bytes 1572872 | tf_op jit(solution)/shard_map/ppermute | solution.py:247
  74.8 13.7 %collective-permute-start.10 = (bf16[256,1024]{1,0:T(8,128)(2,1)S(1)}, bf16[256,1024]{1,0:T(8,128)(2,1)S(1)}, u32[]{:S(2)}, u32[]{:S(2)}) collective-permute-start(bf16[256,1024]{1,0:T(8,128)(2,1)S(1)} %pad_maximum_fusion.9), channel_id=1, source_target_pairs={{0,32},{32,64},{64,96},{96,0},{1,33},{33,65},{65,97},{97,1},{2,34}... | collective-permute-start | bytes 1572872 | tf_op jit(solution)/shard_map/ppermute | solution.py:248
  76.0 21.0 %collective-permute-start.11 = (bf16[256,1024]{1,0:T(8,128)(2,1)S(1)}, bf16[256,1024]{1,0:T(8,128)(2,1)S(1)}, u32[]{:S(2)}, u32[]{:S(2)}) collective-permute-start(bf16[256,1024]{1,0:T(8,128)(2,1)S(1)} %pad_maximum_fusion.9), channel_id=1, source_target_pairs={{0,96},{32,0},{64,32},{96,64},{1,97},{33,1},{65,33},{97,65},{2,98}... | collective-permute-start | bytes 1572872 | tf_op jit(solution)/shard_map/ppermute | solution.py:249
  82.2 14.9 %collective-permute-start.3 = (bf16[1024,256]{1,0:T(8,128)(2,1)S(1)}, bf16[1024,256]{1,0:T(8,128)(2,1)S(1)}, u32[]{:S(2)}, u32[]{:S(2)}) collective-permute-start(bf16[1024,256]{1,0:T(8,128)(2,1)S(1)} %collective-permute-done.1), channel_id=1, source_target_pairs={{0,4},{4,8},{8,12},{12,16},{16,20},{20,24},{24,28},{28,0},{1,5},{5... | collective-permute-start | bytes 1572872 | tf_op jit(solution)/shard_map/ppermute | solution.py:232
  82.2 14.9 %collective-permute-start.4 = (bf16[1024,256]{1,0:T(8,128)(2,1)S(1)}, bf16[1024,256]{1,0:T(8,128)(2,1)S(1)}, u32[]{:S(2)}, u32[]{:S(2)}) collective-permute-start(bf16[1024,256]{1,0:T(8,128)(2,1)S(1)} %collective-permute-done.2), channel_id=1, source_target_pairs={{0,28},{4,0},{8,4},{12,8},{16,12},{20,16},{24,20},{28,24},{1,29},{... | collective-permute-start | bytes 1572872 | tf_op jit(solution)/shard_map/ppermute | solution.py:235
  88.5 24.1 %collective-permute-start.12 = (bf16[2,256,1024]{2,1,0:T(8,128)(2,1)S(1)}, bf16[2,256,1024]{2,1,0:T(8,128)(2,1)S(1)}, u32[]{:S(2)}, u32[]{:S(2)}) collective-permute-start(bf16[2,256,1024]{2,1,0:T(8,128)(2,1)S(1)} %pad_maximum_fusion.7), channel_id=1, source_target_pairs={{0,32},{32,64},{64,96},{96,0},{1,33},{33,65},{65,97},{97,1},{2,34}... | collective-permute-start | bytes 3145736 | tf_op jit(solution)/shard_map/ppermute | solution.py:250
  89.9 12.5 %collective-permute-start.13 = (bf16[256,1024]{1,0:T(8,128)(2,1)S(1)}, bf16[256,1024]{1,0:T(8,128)(2,1)S(1)}, u32[]{:S(2)}, u32[]{:S(2)}) collective-permute-start(bf16[256,1024]{1,0:T(8,128)(2,1)S(1)} %collective-permute-done.9), channel_id=1, source_target_pairs={{0,96},{32,0},{64,32},{96,64},{1,97},{33,1},{65,33},{97,65},{2,98}... | collective-permute-start | bytes 1572872 | tf_op jit(solution)/shard_map/ppermute | solution.py:251
  97.1 14.0 %collective-permute-start.5 = (bf16[1024,256]{1,0:T(8,128)(2,1)S(1)}, bf16[1024,256]{1,0:T(8,128)(2,1)S(1)}, u32[]{:S(2)}, u32[]{:S(2)}) collective-permute-start(bf16[1024,256]{1,0:T(8,128)(2,1)S(1)} %collective-permute-done.3), channel_id=1, source_target_pairs={{0,4},{4,8},{8,12},{12,16},{16,20},{20,24},{24,28},{28,0},{1,5},{5... | collective-permute-start | bytes 1572872 | tf_op jit(solution)/shard_map/ppermute | solution.py:232
  97.1 14.0 %collective-permute-start.6 = (bf16[1024,256]{1,0:T(8,128)(2,1)S(1)}, bf16[1024,256]{1,0:T(8,128)(2,1)S(1)}, u32[]{:S(2)}, u32[]{:S(2)}) collective-permute-start(bf16[1024,256]{1,0:T(8,128)(2,1)S(1)} %collective-permute-done.4), channel_id=1, source_target_pairs={{0,28},{4,0},{8,4},{12,8},{16,12},{20,16},{24,20},{28,24},{1,29},{... | collective-permute-start | bytes 1572872 | tf_op jit(solution)/shard_map/ppermute | solution.py:235
  102.4 11.6 %collective-permute-start.14 = (bf16[256,1024]{1,0:T(8,128)(2,1)S(1)}, bf16[256,1024]{1,0:T(8,128)(2,1)S(1)}, u32[]{:S(2)}, u32[]{:S(2)}) collective-permute-start(bf16[256,1024]{1,0:T(8,128)(2,1)S(1)} %collective-permute-done.13), channel_id=1, source_target_pairs={{0,96},{32,0},{64,32},{96,64},{1,97},{33,1},{65,33},{97,65},{2,98}... | collective-permute-start | bytes 1572872 | tf_op jit(solution)/shard_map/ppermute | solution.py:252
  111.1 13.1 %collective-permute-start.7 = (bf16[1024,256]{1,0:T(8,128)(2,1)S(1)}, bf16[1024,256]{1,0:T(8,128)(2,1)S(1)}, u32[]{:S(2)}, u32[]{:S(2)}) collective-permute-start(bf16[1024,256]{1,0:T(8,128)(2,1)S(1)} %collective-permute-done.5), channel_id=1, source_target_pairs={{0,4},{4,8},{8,12},{12,16},{16,20},{20,24},{24,28},{28,0},{1,5},{5... | collective-permute-start | bytes 1572872 | tf_op jit(solution)/shard_map/ppermute | solution.py:232
  148.7 10.5 %collective-permute-start.25 = (bf16[512,256]{1,0:T(8,128)(2,1)S(1)}, bf16[512,256]{1,0:T(8,128)(2,1)S(1)}, u32[]{:S(2)}, u32[]{:S(2)}) collective-permute-start(bf16[512,256]{1,0:T(8,128)(2,1)S(1)} %get-tuple-element.18), channel_id=1, source_target_pairs={{0,4},{4,8},{8,12},{12,16},{16,20},{20,24},{24,28},{28,0},{1,5},{5... | collective-permute-start | bytes 786440 | tf_op jit(solution)/shard_map/ppermute | solution.py:232
  152.0 12.8 %collective-permute-start.20 = (bf16[512,256]{1,0:T(8,128)(2,1)S(1)}, bf16[512,256]{1,0:T(8,128)(2,1)S(1)}, u32[]{:S(2)}, u32[]{:S(2)}) collective-permute-start(bf16[512,256]{1,0:T(8,128)(2,1)S(1)} %collective-permute-done.18), channel_id=1, source_target_pairs={{0,4},{4,8},{8,12},{12,16},{16,20},{20,24},{24,28},{28,0},{1,5},{5... | collective-permute-start | bytes 786440 | tf_op jit(solution)/shard_map/ppermute | solution.py:232
  152.0 12.8 %collective-permute-start.21 = (bf16[512,256]{1,0:T(8,128)(2,1)S(1)}, bf16[512,256]{1,0:T(8,128)(2,1)S(1)}, u32[]{:S(2)}, u32[]{:S(2)}) collective-permute-start(bf16[512,256]{1,0:T(8,128)(2,1)S(1)} %collective-permute-done.19), channel_id=1, source_target_pairs={{0,28},{4,0},{8,4},{12,8},{16,12},{20,16},{24,20},{28,24},{1,29},{... | collective-permute-start | bytes 786440 | tf_op jit(solution)/shard_map/ppermute | solution.py:235
  159.2 11.2 %collective-permute-start.27 = (bf16[512,256]{1,0:T(8,128)(2,1)S(1)}, bf16[512,256]{1,0:T(8,128)(2,1)S(1)}, u32[]{:S(2)}, u32[]{:S(2)}) collective-permute-start(bf16[512,256]{1,0:T(8,128)(2,1)S(1)} %collective-permute-done.25), channel_id=1, source_target_pairs={{0,4},{4,8},{8,12},{12,16},{16,20},{20,24},{24,28},{28,0},{1,5},{5... | collective-permute-start | bytes 786440 | tf_op jit(solution)/shard_map/ppermute | solution.py:232
  159.3 11.2 %collective-permute-start.28 = (bf16[512,256]{1,0:T(8,128)(2,1)S(1)}, bf16[512,256]{1,0:T(8,128)(2,1)S(1)}, u32[]{:S(2)}, u32[]{:S(2)}) collective-permute-start(bf16[512,256]{1,0:T(8,128)(2,1)S(1)} %collective-permute-done.26), channel_id=1, source_target_pairs={{0,28},{4,0},{8,4},{12,8},{16,12},{20,16},{24,20},{28,24},{1,29},{... | collective-permute-start | bytes 786440 | tf_op jit(solution)/shard_map/ppermute | solution.py:235
  164.8 11.2 %collective-permute-start.22 = (bf16[512,256]{1,0:T(8,128)(2,1)S(1)}, bf16[512,256]{1,0:T(8,128)(2,1)S(1)}, u32[]{:S(2)}, u32[]{:S(2)}) collective-permute-start(bf16[512,256]{1,0:T(8,128)(2,1)S(1)} %collective-permute-done.20), channel_id=1, source_target_pairs={{0,4},{4,8},{8,12},{12,16},{16,20},{20,24},{24,28},{28,0},{1,5},{5... | collective-permute-start | bytes 786440 | tf_op jit(solution)/shard_map/ppermute | solution.py:232
  164.9 11.2 %collective-permute-start.23 = (bf16[512,256]{1,0:T(8,128)(2,1)S(1)}, bf16[512,256]{1,0:T(8,128)(2,1)S(1)}, u32[]{:S(2)}, u32[]{:S(2)}) collective-permute-start(bf16[512,256]{1,0:T(8,128)(2,1)S(1)} %collective-permute-done.21), channel_id=1, source_target_pairs={{0,28},{4,0},{8,4},{12,8},{16,12},{20,16},{24,20},{28,24},{1,29},{... | collective-permute-start | bytes 786440 | tf_op jit(solution)/shard_map/ppermute | solution.py:235
  170.5 11.7 %collective-permute-start.29 = (bf16[512,256]{1,0:T(8,128)(2,1)S(1)}, bf16[512,256]{1,0:T(8,128)(2,1)S(1)}, u32[]{:S(2)}, u32[]{:S(2)}) collective-permute-start(bf16[512,256]{1,0:T(8,128)(2,1)S(1)} %collective-permute-done.27), channel_id=1, source_target_pairs={{0,4},{4,8},{8,12},{12,16},{16,20},{20,24},{24,28},{28,0},{1,5},{5... | collective-permute-start | bytes 786440 | tf_op jit(solution)/shard_map/ppermute | solution.py:232
  191.3 15.6 %collective-permute-start.33 = (bf16[1024,256]{1,0:T(8,128)(2,1)S(1)}, bf16[1024,256]{1,0:T(8,128)(2,1)S(1)}, u32[]{:S(2)}, u32[]{:S(2)}) collective-permute-start(bf16[1024,256]{1,0:T(8,128)(2,1)S(1)} %fusion.18), channel_id=1, source_target_pairs={{0,1},{1,0},{2,3},{3,2},{4,5},{5,4},{6,7},{7,6},{8,9},{9,8},{10,11... | collective-permute-start | bytes 1572872 | tf_op jit(solution)/shard_map/ppermute | solution.py:278
  (15 other events, 146.9 us)

commit v5 on v4

--- a/solution.py
+++ b/solution.py
@@ -30,16 +30,15 @@
 def contribute_kernel(owner_ref, block_ref, left_ref, right_ref, weight_ref, out_ref, count_ref, tag_ref):
     owners = count_ref.shape[0]
     group = lanes_group((8, 128))
-    sub = lax.broadcasted_iota(jnp.int32, (8, 128), 0)
-    lane = lax.broadcasted_iota(jnp.int32, (8, 128), 1)
+    sub = lax.broadcasted_iota(jnp.int32, (2, 128), 0)
+    lane = lax.broadcasted_iota(jnp.int32, (2, 128), 1)
 
     def clear(o, carry):
         for u in range(8):
             count_ref[o * 8 + u] = 0
             tag_ref[o * 16 + 2 * u] = 512
             tag_ref[o * 16 + 2 * u + 1] = 512
-            for slot in range(2):
-                out_ref[(o * 8 + u) * 3 + slot] = jnp.zeros((8, 128), jnp.bfloat16)
+            out_ref[o * 8 + u] = jnp.zeros((9, 2, 128), jnp.bfloat16)
         return carry
 
     lax.fori_loop(0, owners // 8, clear, 0)
@@ -64,13 +63,13 @@
                     rows[k] if k == t else pltpu.roll(rows[k], (32 * (k - t)) % 128, 1)
                     for k in range(4)
                 ]
-                tiles.append(pick(rows, group).astype(jnp.bfloat16))
+                tiles.append(pick(rows, group).reshape(4, 2, 128).astype(jnp.bfloat16))
         for t, tile in enumerate(tiles):
             owner = owner_ref[base + t]
             slot = count_ref[owner]
             count_ref[owner] = slot + 1
             tag_ref[owner * 2 + slot] = block_ref[base + t]
-            out_ref[owner * 3 + slot] = tile
+            out_ref[owner, pl.ds(slot * 4, 4)] = tile
         return carry
 
     lax.fori_loop(0, left_ref.shape[0] // 16, body, 0)
@@ -81,7 +80,7 @@
             high = jnp.where(sub == 0, tags[0] >> 4, tags[1] >> 4)
             low = jnp.where(sub == 0, tags[0] & 15, tags[1] & 15)
             tile = jnp.where(lane == 0, high, low).astype(jnp.float32)
-            out_ref[(o * 8 + u) * 3 + 2] = tile.astype(jnp.bfloat16)
+            out_ref[o * 8 + u, 8] = tile.astype(jnp.bfloat16)
         return carry
 
     lax.fori_loop(0, owners // 8, label, 0)
@@ -91,7 +90,7 @@
     def body(s, carry):
         for u in range(8):
             n = label_ref[s * 8 + u]
-            acc_ref[n] = acc_ref[n] + slot_ref[(s * 4 + u // 2) * 3 + u % 2].astype(jnp.float32)
+            acc_ref[n] = acc_ref[n] + slot_ref[s * 8 + u].astype(jnp.float32)
         return carry
 
     lax.fori_loop(0, label_ref.shape[0] // 8, body, 0)
@@ -124,6 +123,8 @@
         lax.fori_loop(0, label_ref.shape[0] // 8, add, 0)
 
     row, col, half_own = place_ref[0], place_ref[1], place_ref[2]
+    apart = step ^ (2 * (col & 1) + half_own)
+    kept = jnp.where(apart == 0, 0, jnp.where(apart == 2, 1, 2))
     group = lanes_group((8, 128))
     sub = lax.broadcasted_iota(jnp.int32, (8, 128), 0)
     lane = lax.broadcasted_iota(jnp.int32, (8, 128), 1)
@@ -151,7 +152,7 @@
                     ks_rows.append(ks)
                     x_rows.append(pat * (identity - scale * ks))
                 x = jnp.concatenate(x_rows, axis=0).astype(jnp.bfloat16)
-                panel_ref[0, pl.ds(r0, 32), side * 256 + jt * 128 : side * 256 + jt * 128 + 128] = x
+                panel_ref[kept, pl.ds(r0, 32), side * 256 + jt * 128 : side * 256 + jt * 128 + 128] = x
                 if side == 0:
                     at = slice(jt * 128, jt * 128 + 128)
                     ks_ref[pl.ds(r0, 32), at] = jnp.concatenate(ks_rows, axis=0)
@@ -172,7 +173,7 @@
     tasks = left.shape[0]
     return pl.pallas_call(
         contribute_kernel,
-        out_shape=jax.ShapeDtypeStruct((3 * tasks, 8, 128), jnp.bfloat16),
+        out_shape=jax.ShapeDtypeStruct((tasks, 9, 2, 128), jnp.bfloat16),
         in_specs=[SMEM, SMEM, VMEM, VMEM, VMEM],
         out_specs=VMEM,
         scratch_shapes=[pltpu.SMEM((tasks,), jnp.int32), pltpu.SMEM((2 * tasks,), jnp.int32)],
@@ -200,7 +201,7 @@
         out_shape=(
             jax.ShapeDtypeStruct((1024, 256), jnp.float32),
             jax.ShapeDtypeStruct((1024, 256), jnp.bfloat16),
-            jax.ShapeDtypeStruct((4, 256, 512), jnp.bfloat16),
+            jax.ShapeDtypeStruct((3, 256, 512), jnp.bfloat16),
             jax.ShapeDtypeStruct((1024, 256), jnp.bfloat16),
         ),
         grid=(4,),
@@ -212,7 +213,7 @@
         out_specs=(
             pl.BlockSpec((256, 256), quarter),
             pl.BlockSpec((256, 256), quarter),
-            pl.BlockSpec((1, 256, 512), lambda i: (i, 0, 0)),
+            pl.BlockSpec((3, 256, 512), lambda i: (0, 0, 0)),
             pl.BlockSpec((256, 256), quarter),
         ),
         scratch_shapes=[pltpu.VMEM((520, 8, 128), jnp.float32)] * 2,
@@ -287,12 +288,13 @@
 
     outgoing = contribute(task_owner[:, 0], task_block, basis_left, basis_right, grid_weight)
     arrived = lax.all_to_all(
-        outgoing.reshape(tasks, 3, 8, 128), AXES[:4], split_axis=0, concat_axis=0, tiled=True
+        outgoing, AXES[:4], split_axis=0, concat_axis=0, tiled=True
     )
-    slots = arrived[:, :2].reshape(2 * tasks, 8, 128)
-    tag = arrived[:, 2, :2, :2]
+    slots = arrived[:, :8].reshape(2 * tasks, 8, 128)
+    tag = arrived[:, 8, :, :2]
     tag_tile = jnp.pad(tag.reshape(4, 128), ((0, 4), (0, 0)))[None]
-    far = lax.ppermute(jnp.concatenate([slots, tag_tile], axis=0), "yhi", SWAP)
+    slots = jnp.concatenate([slots, tag_tile], axis=0)
+    far = lax.ppermute(slots, "yhi", SWAP)
 
     def label_of(tag):
         tag = tag.astype(jnp.float32)
@@ -300,7 +302,7 @@
 
     labels = label_of(tag.reshape(2 * tasks, 2))
     labels_far = label_of(far[2 * tasks, :4].reshape(2 * tasks, 2))
-    collected = collect(labels, arrived.reshape(3 * tasks, 8, 128))
+    collected = collect(labels, slots)
     block_rows = row * 32 + jnp.arange(32, dtype=jnp.int32)
     block_cols = col * 16 + jnp.arange(16, dtype=jnp.int32)
     mask = (block_mask != 0) | (block_rows[:, None] == block_cols[None, :])
@@ -309,8 +311,7 @@
         place, mask.astype(jnp.float32).reshape(-1), labels_far, far, collected, core_matrix
     )
 
-    keep = lax.dynamic_index_in_dim(panel, 2 * core + yhi, 0, keepdims=False)
-    give = lax.dynamic_index_in_dim(panel, 2 * (1 - core) + yhi, 0, keepdims=False)
+    keep, give = panel[0], panel[1]
     unit = jnp.concatenate([keep, lax.ppermute(give, "core", SWAP)], axis=1)
     b = gather_rows(unit, ylo, x, z)
     squares = []

time: 208 us -> 204 us (0.981)
  waiting for transfers between devices: 105 us -> 102 us
    all_to_all x1, waiting for transfers between devices: 22.2 us -> 18.8 us  [local(): lax.all_to_all(outgoing, AXES[:4], split_axis=0, concat_axis=0, tiled=True)]
where the time goes in v5:
time: 204 us
  waiting for transfers between devices  102 us (50%)
  starting transfers between devices  65.9 us (32%)
  Pallas kernels  16.5 us (8%)
  matrix products  9.3 us (5%)
  local copies, waits for them, and re-layouts  4.91 us (2%)
  other arithmetic  4.49 us (2%)
    ppermute x11, waiting for transfers between devices, gather_z(): up = lax.ppermute(up, 'z', ring_of(8, 1))  41.5 us
    ppermute x10, starting transfers between devices, gather_z(): down = lax.ppermute(down, 'z', ring_of(8, -1))  32.2 us
    ppermute x3, waiting for transfers between devices, product(): away = lax.ppermute(part, 'yhi', SWAP)  22.4 us
    all_to_all x1, waiting for transfers between devices, local(): lax.all_to_all(outgoing, AXES[:4], split_axis=0, concat_axis=0, tiled=True)  18.8 us
    all_to_all x1, starting transfers between devices, local(): lax.all_to_all(outgoing, AXES[:4], split_axis=0, concat_axis=0, tiled=True)  13.8 us
    dot_general x4, matrix products, dot(): return jnp.einsum('dmk,dkn->mn', a, b, preferred_element_type=jnp.float32)  9.3 us
    ppermute x3, starting transfers between devices, product(): away = lax.ppermute(part, 'yhi', SWAP)  8.79 us
    ppermute x1, waiting for transfers between devices, local(): far = lax.ppermute(slots, 'yhi', SWAP)  7.48 us
  transfers between devices with their start and end apart: 35, of which 24 were waited for; matrix products, arithmetic and copies ran while one was open for 5% of the time, Pallas kernels for 2%

profile of v5, /device:TPU:2, one launch (start us, length us, event | category | flops | bytes accessed | tf_op | source)
XLA Modules:
  0.0 203.8 jit_solution(16442162597941354550)
XLA Ops:
  0.6 5.5 %contribute.1 = bf16[128,9,2,128]{3,2,1,0:T(2,128)(2,1)} custom-call(s32[128]{0:T(128)} %bitcast.87, s32[128]{0:T(128)} %block_ref.1, bf16[128,32,128]{2,1,0:T(8,128)(2,1)} %left_ref.1, bf16[128,32,128]{2,1,0:T(8,128)(2,1)} %right_ref.1, f32[128,128]{1,0:T(8,128)} %weight_ref.1), custom_call_target="tpu_custom_call" | custom-call | tf_op jit(solution)/shard_map/contribute/pallas_call | solution.py:174
  6.1 13.8 %all-to-all-start = ((bf16[128,9,2,128]{3,2,1,0:T(2,128)(2,1)}), bf16[128,9,2,128]{3,2,1,0:T(2,128)(2,1)S(1)}, u32[]{:S(2)}, u32[]{:S(2)}) async-start(bf16[128,9,2,128]{3,2,1,0:T(2,128)(2,1)} %contribute.1), calls=%async_computation | async-start | bytes 1179648 | tf_op jit(solution)/shard_map/all_to_all | solution.py:290
  20.0 18.8 %all-to-all-done = bf16[128,9,2,128]{3,2,1,0:T(2,128)(2,1)S(1)} async-done(((bf16[128,9,2,128]{3,2,1,0:T(2,128)(2,1)}), bf16[128,9,2,128]{3,2,1,0:T(2,128)(2,1)S(1)}, u32[]{:S(2)}, u32[]{:S(2)}) %all-to-all-start) | async-done | bytes 589856 | tf_op jit(solution)/shard_map/all_to_all | solution.py:290
  39.4 3.0 %collective-permute-start = (bf16[257,8,128]{2,1,0:T(8,128)(2,1)S(1)}, bf16[257,8,128]{2,1,0:T(8,128)(2,1)S(1)}, u32[]{:S(2)}, u32[]{:S(2)}) collective-permute-start(bf16[257,8,128]{2,1,0:T(8,128)(2,1)S(1)} %pad_maximum_fusion.8.slot_ref), channel_id=1, source_target_pairs={{0,1},{1,0},{2,3},{3,2},{4,5},{5,4},{6,7},{7,6},{8,9},{9,8},{10,11... | collective-permute-start | bytes 1579016 | tf_op jit(solution)/shard_map/ppermute | solution.py:297
  44.7 3.6 %collect.1.first_ref = f32[520,8,128]{2,1,0:T(8,128)} custom-call(s32[256]{0:T(256)} %fusion.31.label_ref, bf16[257,8,128]{2,1,0:T(8,128)(2,1)} %copy-done), custom_call_target="tpu_custom_call" | custom-call | flops 1048576 | bytes 8388608 | tf_op jit(solution)/shard_map/collect/pallas_call | solution.py:185
  48.2 7.5 %collective-permute-done.slot_ref = bf16[257,8,128]{2,1,0:T(8,128)(2,1)S(1)} collective-permute-done((bf16[257,8,128]{2,1,0:T(8,128)(2,1)S(1)}, bf16[257,8,128]{2,1,0:T(8,128)(2,1)S(1)}, u32[]{:S(2)}, u32[]{:S(2)}) %collective-permute-start) | collective-permute-done | bytes 526368 | tf_op jit(solution)/shard_map/ppermute | solution.py:297
  56.6 7.4 %assemble.1 = (f32[1024,256]{1,0:T(8,128)}, bf16[1024,256]{1,0:T(8,128)(2,1)}, bf16[3,256,512]{2,1,0:T(8,128)(2,1)}, bf16[1024,256]{1,0:T(8,128)(2,1)}) custom-call(s32[3]{0:T(128)} %pad_add_fusion.place_ref, f32[512]{0:T(512)} %reshape.40.mask_ref, s32[256]{0:T(256)} %fusion.34.label_ref, bf16[257,8,128]{2,1,0:T(8,128)(2,1)} %copy-done.2, ...), custom_call_target="tpu_custom_call" | custom-call | tf_op jit(solution)/shard_map/assemble/pallas_call | solution.py:199
  73.9 5.6 %collective-permute-done.1 = bf16[1024,256]{1,0:T(8,128)(2,1)S(1)} collective-permute-done((bf16[1024,256]{1,0:T(8,128)(2,1)}, bf16[1024,256]{1,0:T(8,128)(2,1)S(1)}, u32[]{:S(2)}, u32[]{:S(2)}) %collective-permute-start.1) | collective-permute-done | bytes 524320 | tf_op jit(solution)/shard_map/ppermute | solution.py:233
  79.5 3.2 %collective-permute-start.4 = (bf16[1024,256]{1,0:T(8,128)(2,1)S(1)}, bf16[1024,256]{1,0:T(8,128)(2,1)S(1)}, u32[]{:S(2)}, u32[]{:S(2)}) collective-permute-start(bf16[1024,256]{1,0:T(8,128)(2,1)S(1)} %collective-permute-done.2), channel_id=1, source_target_pairs={{0,28},{4,0},{8,4},{12,8},{16,12},{20,16},{24,20},{28,24},{1,29},{... | collective-permute-start | bytes 1572872 | tf_op jit(solution)/shard_map/ppermute | solution.py:236
  87.3 6.6 %collective-permute-done.3 = bf16[1024,256]{1,0:T(8,128)(2,1)S(1)} collective-permute-done((bf16[1024,256]{1,0:T(8,128)(2,1)S(1)}, bf16[1024,256]{1,0:T(8,128)(2,1)S(1)}, u32[]{:S(2)}, u32[]{:S(2)}) %collective-permute-start.3) | collective-permute-done | bytes 524320 | tf_op jit(solution)/shard_map/ppermute | solution.py:233
  93.9 3.3 %collective-permute-start.6 = (bf16[1024,256]{1,0:T(8,128)(2,1)S(1)}, bf16[1024,256]{1,0:T(8,128)(2,1)S(1)}, u32[]{:S(2)}, u32[]{:S(2)}) collective-permute-start(bf16[1024,256]{1,0:T(8,128)(2,1)S(1)} %collective-permute-done.4), channel_id=1, source_target_pairs={{0,28},{4,0},{8,4},{12,8},{16,12},{20,16},{24,20},{28,24},{1,29},{... | collective-permute-start | bytes 1572872 | tf_op jit(solution)/shard_map/ppermute | solution.py:236
  100.1 7.2 %collective-permute-done.5 = bf16[1024,256]{1,0:T(8,128)(2,1)S(1)} collective-permute-done((bf16[1024,256]{1,0:T(8,128)(2,1)S(1)}, bf16[1024,256]{1,0:T(8,128)(2,1)S(1)}, u32[]{:S(2)}, u32[]{:S(2)}) %collective-permute-start.5) | collective-permute-done | bytes 524320 | tf_op jit(solution)/shard_map/ppermute | solution.py:233
  110.6 9.1 %collective-permute-done.7 = bf16[1024,256]{1,0:T(8,128)(2,1)S(1)} collective-permute-done((bf16[1024,256]{1,0:T(8,128)(2,1)S(1)}, bf16[1024,256]{1,0:T(8,128)(2,1)S(1)}, u32[]{:S(2)}, u32[]{:S(2)}) %collective-permute-start.7) | collective-permute-done | bytes 524320 | tf_op jit(solution)/shard_map/ppermute | solution.py:233
  125.0 3.0 %collective-permute-start.16 = (bf16[512,256]{1,0:T(8,128)(2,1)S(1)}, bf16[512,256]{1,0:T(8,128)(2,1)S(1)}, u32[]{:S(2)}, u32[]{:S(2)}) collective-permute-start(bf16[512,256]{1,0:T(8,128)(2,1)S(1)} %get-tuple-element.20), channel_id=1, source_target_pairs={{0,1},{1,0},{2,3},{3,2},{4,5},{5,4},{6,7},{7,6},{8,9},{9,8},{10,11... | collective-permute-start | bytes 786440 | tf_op jit(solution)/shard_map/ppermute | solution.py:279
  128.0 7.0 %collective-permute-done.16 = bf16[512,256]{1,0:T(8,128)(2,1)S(1)} collective-permute-done((bf16[512,256]{1,0:T(8,128)(2,1)S(1)}, bf16[512,256]{1,0:T(8,128)(2,1)S(1)}, u32[]{:S(2)}, u32[]{:S(2)}) %collective-permute-start.16) | collective-permute-done | bytes 262176 | tf_op jit(solution)/shard_map/ppermute | solution.py:279
  138.2 3.2 %collective-permute-start.19 = (bf16[512,256]{1,0:T(8,128)(2,1)S(1)}, bf16[512,256]{1,0:T(8,128)(2,1)S(1)}, u32[]{:S(2)}, u32[]{:S(2)}) collective-permute-start(bf16[512,256]{1,0:T(8,128)(2,1)S(1)} %get-tuple-element.15), channel_id=1, source_target_pairs={{0,28},{4,0},{8,4},{12,8},{16,12},{20,16},{24,20},{28,24},{1,29},{... | collective-permute-start | bytes 786440 | tf_op jit(solution)/shard_map/ppermute | solution.py:236
  144.4 3.2 %collective-permute-start.26 = (bf16[512,256]{1,0:T(8,128)(2,1)S(1)}, bf16[512,256]{1,0:T(8,128)(2,1)S(1)}, u32[]{:S(2)}, u32[]{:S(2)}) collective-permute-start(bf16[512,256]{1,0:T(8,128)(2,1)S(1)} %get-tuple-element.18), channel_id=1, source_target_pairs={{0,28},{4,0},{8,4},{12,8},{16,12},{20,16},{24,20},{28,24},{1,29},{... | collective-permute-start | bytes 786440 | tf_op jit(solution)/shard_map/ppermute | solution.py:236
  147.6 3.5 %collective-permute-start.21 = (bf16[512,256]{1,0:T(8,128)(2,1)S(1)}, bf16[512,256]{1,0:T(8,128)(2,1)S(1)}, u32[]{:S(2)}, u32[]{:S(2)}) collective-permute-start(bf16[512,256]{1,0:T(8,128)(2,1)S(1)} %collective-permute-done.19), channel_id=1, source_target_pairs={{0,28},{4,0},{8,4},{12,8},{16,12},{20,16},{24,20},{28,24},{1,29},{... | collective-permute-start | bytes 786440 | tf_op jit(solution)/shard_map/ppermute | solution.py:236
  151.2 3.6 %collective-permute-done.25 = bf16[512,256]{1,0:T(8,128)(2,1)S(1)} collective-permute-done((bf16[512,256]{1,0:T(8,128)(2,1)S(1)}, bf16[512,256]{1,0:T(8,128)(2,1)S(1)}, u32[]{:S(2)}, u32[]{:S(2)}) %collective-permute-start.25) | collective-permute-done | bytes 262176 | tf_op jit(solution)/shard_map/ppermute | solution.py:233
  154.8 3.3 %collective-permute-start.28 = (bf16[512,256]{1,0:T(8,128)(2,1)S(1)}, bf16[512,256]{1,0:T(8,128)(2,1)S(1)}, u32[]{:S(2)}, u32[]{:S(2)}) collective-permute-start(bf16[512,256]{1,0:T(8,128)(2,1)S(1)} %collective-permute-done.26), channel_id=1, source_target_pairs={{0,28},{4,0},{8,4},{12,8},{16,12},{20,16},{24,20},{28,24},{1,29},{... | collective-permute-start | bytes 786440 | tf_op jit(solution)/shard_map/ppermute | solution.py:236
  160.5 3.3 %collective-permute-start.23 = (bf16[512,256]{1,0:T(8,128)(2,1)S(1)}, bf16[512,256]{1,0:T(8,128)(2,1)S(1)}, u32[]{:S(2)}, u32[]{:S(2)}) collective-permute-start(bf16[512,256]{1,0:T(8,128)(2,1)S(1)} %collective-permute-done.21), channel_id=1, source_target_pairs={{0,28},{4,0},{8,4},{12,8},{16,12},{20,16},{24,20},{28,24},{1,29},{... | collective-permute-start | bytes 786440 | tf_op jit(solution)/shard_map/ppermute | solution.py:236
  166.1 3.3 %collective-permute-start.30 = (bf16[512,256]{1,0:T(8,128)(2,1)S(1)}, bf16[512,256]{1,0:T(8,128)(2,1)S(1)}, u32[]{:S(2)}, u32[]{:S(2)}) collective-permute-start(bf16[512,256]{1,0:T(8,128)(2,1)S(1)} %collective-permute-done.28), channel_id=1, source_target_pairs={{0,28},{4,0},{8,4},{12,8},{16,12},{20,16},{24,20},{28,24},{1,29},{... | collective-permute-start | bytes 786440 | tf_op jit(solution)/shard_map/ppermute | solution.py:236
  174.0 3.7 %collective-permute-start.31 = (bf16[512,256]{1,0:T(8,128)(2,1)S(1)}, bf16[512,256]{1,0:T(8,128)(2,1)S(1)}, u32[]{:S(2)}, u32[]{:S(2)}) collective-permute-start(bf16[512,256]{1,0:T(8,128)(2,1)S(1)} %collective-permute-done.30), channel_id=1, source_target_pairs={{0,28},{4,0},{8,4},{12,8},{16,12},{20,16},{24,20},{28,24},{1,29},{... | collective-permute-start | bytes 786440 | tf_op jit(solution)/shard_map/ppermute | solution.py:236
  189.8 12.7 %collective-permute-done.33 = bf16[1024,256]{1,0:T(8,128)(2,1)S(1)} collective-permute-done((bf16[1024,256]{1,0:T(8,128)(2,1)S(1)}, bf16[1024,256]{1,0:T(8,128)(2,1)S(1)}, u32[]{:S(2)}, u32[]{:S(2)}) %collective-permute-start.33) | collective-permute-done | bytes 524320 | tf_op jit(solution)/shard_map/ppermute | solution.py:279
  (116 shorter events, 58.1 us)
Async XLA Ops:
  6.1 32.6 %all-to-all-start = ((bf16[128,9,2,128]{3,2,1,0:T(2,128)(2,1)}), bf16[128,9,2,128]{3,2,1,0:T(2,128)(2,1)S(1)}, u32[]{:S(2)}, u32[]{:S(2)}) async-start(bf16[128,9,2,128]{3,2,1,0:T(2,128)(2,1)} %contribute.1), calls=%async_computation | async-start | bytes 1179648 | tf_op jit(solution)/shard_map/all_to_all | solution.py:290
  39.4 16.3 %collective-permute-start = (bf16[257,8,128]{2,1,0:T(8,128)(2,1)S(1)}, bf16[257,8,128]{2,1,0:T(8,128)(2,1)S(1)}, u32[]{:S(2)}, u32[]{:S(2)}) collective-permute-start(bf16[257,8,128]{2,1,0:T(8,128)(2,1)S(1)} %pad_maximum_fusion.8.slot_ref), channel_id=1, source_target_pairs={{0,1},{1,0},{2,3},{3,2},{4,5},{5,4},{6,7},{7,6},{8,9},{9,8},{10,11... | collective-permute-start | bytes 1579016 | tf_op jit(solution)/shard_map/ppermute | solution.py:297
  64.1 15.4 %collective-permute-start.1 = (bf16[1024,256]{1,0:T(8,128)(2,1)}, bf16[1024,256]{1,0:T(8,128)(2,1)S(1)}, u32[]{:S(2)}, u32[]{:S(2)}) collective-permute-start(bf16[1024,256]{1,0:T(8,128)(2,1)} %get-tuple-element.10), channel_id=1, source_target_pairs={{0,4},{4,8},{8,12},{12,16},{16,20},{20,24},{24,28},{28,0},{1,5},{5... | collective-permute-start | bytes 1572872 | tf_op jit(solution)/shard_map/ppermute | solution.py:233
  65.4 14.2 %collective-permute-start.2 = (bf16[1024,256]{1,0:T(8,128)(2,1)}, bf16[1024,256]{1,0:T(8,128)(2,1)S(1)}, u32[]{:S(2)}, u32[]{:S(2)}) collective-permute-start(bf16[1024,256]{1,0:T(8,128)(2,1)} %get-tuple-element.10), channel_id=1, source_target_pairs={{0,28},{4,0},{8,4},{12,8},{16,12},{20,16},{24,20},{28,24},{1,29},{... | collective-permute-start | bytes 1572872 | tf_op jit(solution)/shard_map/ppermute | solution.py:236
  70.2 14.1 %collective-permute-start.9 = (bf16[256,1024]{1,0:T(8,128)(2,1)S(1)}, bf16[256,1024]{1,0:T(8,128)(2,1)S(1)}, u32[]{:S(2)}, u32[]{:S(2)}) collective-permute-start(bf16[256,1024]{1,0:T(8,128)(2,1)S(1)} %pad_maximum_fusion.9), channel_id=1, source_target_pairs={{0,128},{128,0},{1,129},{129,1},{2,130},{130,2},{3,131},{131,3},{4... | collective-permute-start | bytes 1572872 | tf_op jit(solution)/shard_map/ppermute | solution.py:248
  71.3 13.7 %collective-permute-start.10 = (bf16[256,1024]{1,0:T(8,128)(2,1)S(1)}, bf16[256,1024]{1,0:T(8,128)(2,1)S(1)}, u32[]{:S(2)}, u32[]{:S(2)}) collective-permute-start(bf16[256,1024]{1,0:T(8,128)(2,1)S(1)} %pad_maximum_fusion.9), channel_id=1, source_target_pairs={{0,32},{32,64},{64,96},{96,0},{1,33},{33,65},{65,97},{97,1},{2,34}... | collective-permute-start | bytes 1572872 | tf_op jit(solution)/shard_map/ppermute | solution.py:249
  72.5 21.3 %collective-permute-start.11 = (bf16[256,1024]{1,0:T(8,128)(2,1)S(1)}, bf16[256,1024]{1,0:T(8,128)(2,1)S(1)}, u32[]{:S(2)}, u32[]{:S(2)}) collective-permute-start(bf16[256,1024]{1,0:T(8,128)(2,1)S(1)} %pad_maximum_fusion.9), channel_id=1, source_target_pairs={{0,96},{32,0},{64,32},{96,64},{1,97},{33,1},{65,33},{97,65},{2,98}... | collective-permute-start | bytes 1572872 | tf_op jit(solution)/shard_map/ppermute | solution.py:250
  79.5 14.3 %collective-permute-start.3 = (bf16[1024,256]{1,0:T(8,128)(2,1)S(1)}, bf16[1024,256]{1,0:T(8,128)(2,1)S(1)}, u32[]{:S(2)}, u32[]{:S(2)}) collective-permute-start(bf16[1024,256]{1,0:T(8,128)(2,1)S(1)} %collective-permute-done.1), channel_id=1, source_target_pairs={{0,4},{4,8},{8,12},{12,16},{16,20},{20,24},{24,28},{28,0},{1,5},{5... | collective-permute-start | bytes 1572872 | tf_op jit(solution)/shard_map/ppermute | solution.py:233
  79.5 14.4 %collective-permute-start.4 = (bf16[1024,256]{1,0:T(8,128)(2,1)S(1)}, bf16[1024,256]{1,0:T(8,128)(2,1)S(1)}, u32[]{:S(2)}, u32[]{:S(2)}) collective-permute-start(bf16[1024,256]{1,0:T(8,128)(2,1)S(1)} %collective-permute-done.2), channel_id=1, source_target_pairs={{0,28},{4,0},{8,4},{12,8},{16,12},{20,16},{24,20},{28,24},{1,29},{... | collective-permute-start | bytes 1572872 | tf_op jit(solution)/shard_map/ppermute | solution.py:236
  85.1 24.1 %collective-permute-start.12 = (bf16[2,256,1024]{2,1,0:T(8,128)(2,1)S(1)}, bf16[2,256,1024]{2,1,0:T(8,128)(2,1)S(1)}, u32[]{:S(2)}, u32[]{:S(2)}) collective-permute-start(bf16[2,256,1024]{2,1,0:T(8,128)(2,1)S(1)} %pad_maximum_fusion.7), channel_id=1, source_target_pairs={{0,32},{32,64},{64,96},{96,0},{1,33},{33,65},{65,97},{97,1},{2,34}... | collective-permute-start | bytes 3145736 | tf_op jit(solution)/shard_map/ppermute | solution.py:251
  86.4 12.5 %collective-permute-start.13 = (bf16[256,1024]{1,0:T(8,128)(2,1)S(1)}, bf16[256,1024]{1,0:T(8,128)(2,1)S(1)}, u32[]{:S(2)}, u32[]{:S(2)}) collective-permute-start(bf16[256,1024]{1,0:T(8,128)(2,1)S(1)} %collective-permute-done.9), channel_id=1, source_target_pairs={{0,96},{32,0},{64,32},{96,64},{1,97},{33,1},{65,33},{97,65},{2,98}... | collective-permute-start | bytes 1572872 | tf_op jit(solution)/shard_map/ppermute | solution.py:252
  93.9 13.4 %collective-permute-start.5 = (bf16[1024,256]{1,0:T(8,128)(2,1)S(1)}, bf16[1024,256]{1,0:T(8,128)(2,1)S(1)}, u32[]{:S(2)}, u32[]{:S(2)}) collective-permute-start(bf16[1024,256]{1,0:T(8,128)(2,1)S(1)} %collective-permute-done.3), channel_id=1, source_target_pairs={{0,4},{4,8},{8,12},{12,16},{16,20},{20,24},{24,28},{28,0},{1,5},{5... | collective-permute-start | bytes 1572872 | tf_op jit(solution)/shard_map/ppermute | solution.py:233
  93.9 13.4 %collective-permute-start.6 = (bf16[1024,256]{1,0:T(8,128)(2,1)S(1)}, bf16[1024,256]{1,0:T(8,128)(2,1)S(1)}, u32[]{:S(2)}, u32[]{:S(2)}) collective-permute-start(bf16[1024,256]{1,0:T(8,128)(2,1)S(1)} %collective-permute-done.4), channel_id=1, source_target_pairs={{0,28},{4,0},{8,4},{12,8},{16,12},{20,16},{24,20},{28,24},{1,29},{... | collective-permute-start | bytes 1572872 | tf_op jit(solution)/shard_map/ppermute | solution.py:236
  98.9 11.6 %collective-permute-start.14 = (bf16[256,1024]{1,0:T(8,128)(2,1)S(1)}, bf16[256,1024]{1,0:T(8,128)(2,1)S(1)}, u32[]{:S(2)}, u32[]{:S(2)}) collective-permute-start(bf16[256,1024]{1,0:T(8,128)(2,1)S(1)} %collective-permute-done.13), channel_id=1, source_target_pairs={{0,96},{32,0},{64,32},{96,64},{1,97},{33,1},{65,33},{97,65},{2,98}... | collective-permute-start | bytes 1572872 | tf_op jit(solution)/shard_map/ppermute | solution.py:253
  107.3 12.5 %collective-permute-start.7 = (bf16[1024,256]{1,0:T(8,128)(2,1)S(1)}, bf16[1024,256]{1,0:T(8,128)(2,1)S(1)}, u32[]{:S(2)}, u32[]{:S(2)}) collective-permute-start(bf16[1024,256]{1,0:T(8,128)(2,1)S(1)} %collective-permute-done.5), channel_id=1, source_target_pairs={{0,4},{4,8},{8,12},{12,16},{16,20},{20,24},{24,28},{28,0},{1,5},{5... | collective-permute-start | bytes 1572872 | tf_op jit(solution)/shard_map/ppermute | solution.py:233
  144.3 10.5 %collective-permute-start.25 = (bf16[512,256]{1,0:T(8,128)(2,1)S(1)}, bf16[512,256]{1,0:T(8,128)(2,1)S(1)}, u32[]{:S(2)}, u32[]{:S(2)}) collective-permute-start(bf16[512,256]{1,0:T(8,128)(2,1)S(1)} %get-tuple-element.18), channel_id=1, source_target_pairs={{0,4},{4,8},{8,12},{12,16},{16,20},{20,24},{24,28},{28,0},{1,5},{5... | collective-permute-start | bytes 786440 | tf_op jit(solution)/shard_map/ppermute | solution.py:233
  147.6 12.8 %collective-permute-start.20 = (bf16[512,256]{1,0:T(8,128)(2,1)S(1)}, bf16[512,256]{1,0:T(8,128)(2,1)S(1)}, u32[]{:S(2)}, u32[]{:S(2)}) collective-permute-start(bf16[512,256]{1,0:T(8,128)(2,1)S(1)} %collective-permute-done.18), channel_id=1, source_target_pairs={{0,4},{4,8},{8,12},{12,16},{16,20},{20,24},{24,28},{28,0},{1,5},{5... | collective-permute-start | bytes 786440 | tf_op jit(solution)/shard_map/ppermute | solution.py:233
  147.6 12.8 %collective-permute-start.21 = (bf16[512,256]{1,0:T(8,128)(2,1)S(1)}, bf16[512,256]{1,0:T(8,128)(2,1)S(1)}, u32[]{:S(2)}, u32[]{:S(2)}) collective-permute-start(bf16[512,256]{1,0:T(8,128)(2,1)S(1)} %collective-permute-done.19), channel_id=1, source_target_pairs={{0,28},{4,0},{8,4},{12,8},{16,12},{20,16},{24,20},{28,24},{1,29},{... | collective-permute-start | bytes 786440 | tf_op jit(solution)/shard_map/ppermute | solution.py:236
  154.8 11.2 %collective-permute-start.27 = (bf16[512,256]{1,0:T(8,128)(2,1)S(1)}, bf16[512,256]{1,0:T(8,128)(2,1)S(1)}, u32[]{:S(2)}, u32[]{:S(2)}) collective-permute-start(bf16[512,256]{1,0:T(8,128)(2,1)S(1)} %collective-permute-done.25), channel_id=1, source_target_pairs={{0,4},{4,8},{8,12},{12,16},{16,20},{20,24},{24,28},{28,0},{1,5},{5... | collective-permute-start | bytes 786440 | tf_op jit(solution)/shard_map/ppermute | solution.py:233
  154.8 11.2 %collective-permute-start.28 = (bf16[512,256]{1,0:T(8,128)(2,1)S(1)}, bf16[512,256]{1,0:T(8,128)(2,1)S(1)}, u32[]{:S(2)}, u32[]{:S(2)}) collective-permute-start(bf16[512,256]{1,0:T(8,128)(2,1)S(1)} %collective-permute-done.26), channel_id=1, source_target_pairs={{0,28},{4,0},{8,4},{12,8},{16,12},{20,16},{24,20},{28,24},{1,29},{... | collective-permute-start | bytes 786440 | tf_op jit(solution)/shard_map/ppermute | solution.py:236
  160.4 11.2 %collective-permute-start.22 = (bf16[512,256]{1,0:T(8,128)(2,1)S(1)}, bf16[512,256]{1,0:T(8,128)(2,1)S(1)}, u32[]{:S(2)}, u32[]{:S(2)}) collective-permute-start(bf16[512,256]{1,0:T(8,128)(2,1)S(1)} %collective-permute-done.20), channel_id=1, source_target_pairs={{0,4},{4,8},{8,12},{12,16},{16,20},{20,24},{24,28},{28,0},{1,5},{5... | collective-permute-start | bytes 786440 | tf_op jit(solution)/shard_map/ppermute | solution.py:233
  160.5 11.2 %collective-permute-start.23 = (bf16[512,256]{1,0:T(8,128)(2,1)S(1)}, bf16[512,256]{1,0:T(8,128)(2,1)S(1)}, u32[]{:S(2)}, u32[]{:S(2)}) collective-permute-start(bf16[512,256]{1,0:T(8,128)(2,1)S(1)} %collective-permute-done.21), channel_id=1, source_target_pairs={{0,28},{4,0},{8,4},{12,8},{16,12},{20,16},{24,20},{28,24},{1,29},{... | collective-permute-start | bytes 786440 | tf_op jit(solution)/shard_map/ppermute | solution.py:236
  166.0 11.7 %collective-permute-start.29 = (bf16[512,256]{1,0:T(8,128)(2,1)S(1)}, bf16[512,256]{1,0:T(8,128)(2,1)S(1)}, u32[]{:S(2)}, u32[]{:S(2)}) collective-permute-start(bf16[512,256]{1,0:T(8,128)(2,1)S(1)} %collective-permute-done.27), channel_id=1, source_target_pairs={{0,4},{4,8},{8,12},{12,16},{16,20},{20,24},{24,28},{28,0},{1,5},{5... | collective-permute-start | bytes 786440 | tf_op jit(solution)/shard_map/ppermute | solution.py:233
  186.9 15.6 %collective-permute-start.33 = (bf16[1024,256]{1,0:T(8,128)(2,1)S(1)}, bf16[1024,256]{1,0:T(8,128)(2,1)S(1)}, u32[]{:S(2)}, u32[]{:S(2)}) collective-permute-start(bf16[1024,256]{1,0:T(8,128)(2,1)S(1)} %fusion.18), channel_id=1, source_target_pairs={{0,1},{1,0},{2,3},{3,2},{4,5},{5,4},{6,7},{7,6},{8,9},{9,8},{10,11... | collective-permute-start | bytes 1572872 | tf_op jit(solution)/shard_map/ppermute | solution.py:279
  (15 other events, 143.6 us)

commit v6 on v5

--- a/solution.py
+++ b/solution.py
@@ -86,80 +86,110 @@
     lax.fori_loop(0, owners // 8, label, 0)
 
 
-def accumulate(acc_ref, label_ref, slot_ref):
-    def body(s, carry):
-        for u in range(8):
-            n = label_ref[s * 8 + u]
-            acc_ref[n] = acc_ref[n] + slot_ref[s * 8 + u].astype(jnp.float32)
-        return carry
-
-    lax.fori_loop(0, label_ref.shape[0] // 8, body, 0)
-
-
-def collect_kernel(label_ref, slot_ref, acc_ref):
-    acc_ref[...] = jnp.zeros_like(acc_ref)
-    accumulate(acc_ref, label_ref, slot_ref)
-
-
-def assemble_kernel(
-    place_ref, mask_ref, label_ref, slot_ref, first_ref, core_ref,
-    ks_ref, own_ref, panel_ref, pattern_ref, even_ref, odd_ref, *, scale,
+def read_labels(slot_ref, vector_ref, label_ref):
+    pairs = slot_ref[slot_ref.shape[0] - 1].astype(jnp.float32)
+    labels = jnp.minimum(pairs * 16.0 + pltpu.roll(pairs, 127, 1), 512.0)
+    vector_ref[...] = labels.astype(jnp.int32)
+    pltpu.sync_copy(vector_ref, label_ref)
+
+
+def add_slots(even_ref, odd_ref, label_ref, slot_ref):
+    even_ref[...] = jnp.zeros_like(even_ref)
+    odd_ref[...] = jnp.zeros_like(odd_ref)
+
+    def add(s, carry):
+        for u in range(4):
+            at = s * 8 + 2 * u
+            place = (s % 8) * 16 + 4 * u
+            n, m = label_ref[s // 8, place], label_ref[s // 8, place + 2]
+            even_ref[n] = even_ref[n] + slot_ref[at].astype(jnp.float32)
+            odd_ref[m] = odd_ref[m] + slot_ref[at + 1].astype(jnp.float32)
+        return carry
+
+    lax.fori_loop(0, slot_ref.shape[0] // 8, add, 0)
+
+
+def spread(blocks, group):
+    rows = []
+    for t in range(4):
+        turned = [
+            blocks[j] if j == t else pltpu.roll(blocks[j], (32 * (j - t)) % 128, 1) for j in range(4)
+        ]
+        rows.append(pick(turned, group))
+    return rows
+
+
+def where_am_i():
+    ylo, x, z, core, yhi = (lax.axis_index(a) for a in AXES)
+    return ylo * 4 + x, z * 2 + core, yhi
+
+
+def collect_kernel(
+    mask_ref, slot_ref, core_ref, base_ref, pattern_ref, even_ref, odd_ref, vector_ref, label_ref
 ):
-    step = pl.program_id(0)
-
-    @pl.when(step == 0)
-    def _():
-        even_ref[...] = jnp.zeros_like(even_ref)
-        odd_ref[...] = jnp.zeros_like(odd_ref)
-
-        def add(s, carry):
-            for u in range(4):
-                at = s * 8 + 2 * u
-                n, m = label_ref[at], label_ref[at + 1]
-                even_ref[n] = even_ref[n] + slot_ref[at].astype(jnp.float32)
-                odd_ref[m] = odd_ref[m] + slot_ref[at + 1].astype(jnp.float32)
-            return carry
-
-        lax.fori_loop(0, label_ref.shape[0] // 8, add, 0)
-
-    row, col, half_own = place_ref[0], place_ref[1], place_ref[2]
-    apart = step ^ (2 * (col & 1) + half_own)
-    kept = jnp.where(apart == 0, 0, jnp.where(apart == 2, 1, 2))
+    read_labels(slot_ref, vector_ref, label_ref)
+    add_slots(even_ref, odd_ref, label_ref, slot_ref)
+    row, col, half_own = where_am_i()
     group = lanes_group((8, 128))
-    sub = lax.broadcasted_iota(jnp.int32, (8, 128), 0)
-    lane = lax.broadcasted_iota(jnp.int32, (8, 128), 1)
-    slant = sub - lane
 
     def body(i, carry):
         r0 = pl.multiple_of(i * 32, 32)
         for side in range(2):
             half = half_own if side == 0 else 1 - half_own
             for jt in range(2):
-                near = i * 16 + half * 8 + jt * 4
-                n = step * 128 + near
-                blocks = [first_ref[near + j] + (even_ref[n + j] + odd_ref[n + j]) for j in range(4)]
-                pat = pick([jnp.full((8, 128), mask_ref[n + j]) for j in range(4)], group)
+                j0 = half * 8 + jt * 4
+                n = i * 16 + j0
+                blocks = [even_ref[n + j] + odd_ref[n + j] for j in range(4)]
+                marks = []
+                for j in range(4):
+                    on = (mask_ref[i, j0 + j] != 0) | (row * 32 + i == col * 16 + j0 + j)
+                    marks.append(jnp.full((8, 128), jnp.where(on, 1.0, 0.0)))
+                pat = pick(marks, group)
                 c0 = pl.multiple_of(half * 256 + jt * 128, 128)
-                gap = col * 512 + c0 - row * 1024 - step * 256 - r0
-                ks_rows, x_rows = [], []
-                for t in range(4):
-                    turned = [
-                        blocks[j] if j == t else pltpu.roll(blocks[j], (32 * (j - t)) % 128, 1)
-                        for j in range(4)
-                    ]
-                    ks = core_ref[pl.ds(r0 + 8 * t, 8), pl.ds(c0, 128)] + pick(turned, group)
-                    identity = jnp.where(slant == gap - 8 * t, 0.5, 0.0)
-                    ks_rows.append(ks)
-                    x_rows.append(pat * (identity - scale * ks))
-                x = jnp.concatenate(x_rows, axis=0).astype(jnp.bfloat16)
-                panel_ref[kept, pl.ds(r0, 32), side * 256 + jt * 128 : side * 256 + jt * 128 + 128] = x
+                at = slice(side * 256 + jt * 128, side * 256 + jt * 128 + 128)
+                base_ref[pl.ds(r0, 32), at] = core_ref[pl.ds(r0, 32), pl.ds(c0, 128)] + (
+                    jnp.concatenate(spread(blocks, group), axis=0)
+                )
+                pattern_ref[pl.ds(r0, 32), at] = jnp.concatenate([pat] * 4, axis=0).astype(jnp.bfloat16)
+        return carry
+
+    lax.fori_loop(0, 32, body, 0)
+
+
+def assemble_kernel(
+    slot_ref, base_ref, pattern_ref, ks_ref, own_ref, panel_ref,
+    even_ref, odd_ref, vector_ref, label_ref, *, scale,
+):
+    step = pl.program_id(0)
+
+    @pl.when(step == 0)
+    def _():
+        read_labels(slot_ref, vector_ref, label_ref)
+        add_slots(even_ref, odd_ref, label_ref, slot_ref)
+
+    row, col, half_own = where_am_i()
+    apart = step ^ (2 * (col & 1) + half_own)
+    kept = jnp.where(apart == 0, 0, jnp.where(apart == 2, 1, 2))
+    group = lanes_group((8, 128))
+    slant = lax.broadcasted_iota(jnp.int32, (32, 128), 0) - lax.broadcasted_iota(jnp.int32, (32, 128), 1)
+
+    def body(i, carry):
+        r0 = pl.multiple_of(i * 32, 32)
+        for side in range(2):
+            half = half_own if side == 0 else 1 - half_own
+            for jt in range(2):
+                n = step * 128 + i * 16 + half * 8 + jt * 4
+                blocks = [even_ref[n + j] + odd_ref[n + j] for j in range(4)]
+                at = slice(side * 256 + jt * 128, side * 256 + jt * 128 + 128)
+                ks = base_ref[pl.ds(r0, 32), at] + jnp.concatenate(spread(blocks, group), axis=0)
+                gap = col * 512 + half * 256 + jt * 128 - row * 1024 - step * 256 - r0
+                identity = jnp.where(slant == gap, 0.5, 0.0)
+                pat = pattern_ref[pl.ds(r0, 32), at].astype(jnp.float32)
+                x = (pat * (identity - scale * ks)).astype(jnp.bfloat16)
+                panel_ref[kept, pl.ds(r0, 32), at] = x
                 if side == 0:
-                    at = slice(jt * 128, jt * 128 + 128)
-                    ks_ref[pl.ds(r0, 32), at] = jnp.concatenate(ks_rows, axis=0)
+                    ks_ref[pl.ds(r0, 32), at] = ks
                     own_ref[pl.ds(r0, 32), at] = x
-                    pattern_ref[pl.ds(r0, 32), at] = jnp.concatenate([pat] * 4, axis=0).astype(
-                        jnp.bfloat16
-                    )
         return carry
 
     lax.fori_loop(0, 8, body, 0, unroll=2)
@@ -181,18 +211,30 @@
     )(owner, block, left, right, weight)
 
 
-def collect(labels, slots):
+ADDERS = [
+    pltpu.VMEM((520, 8, 128), jnp.float32),
+    pltpu.VMEM((520, 8, 128), jnp.float32),
+    pltpu.VMEM((8, 128), jnp.int32),
+    pltpu.SMEM((8, 128), jnp.int32),
+]
+
+
+def collect(mask, slots, core):
     return pl.pallas_call(
         collect_kernel,
-        out_shape=jax.ShapeDtypeStruct((520, 8, 128), jnp.float32),
-        in_specs=[SMEM, VMEM],
-        out_specs=VMEM,
+        out_shape=(
+            jax.ShapeDtypeStruct((1024, 512), jnp.float32),
+            jax.ShapeDtypeStruct((1024, 512), jnp.bfloat16),
+        ),
+        in_specs=[SMEM, VMEM, VMEM],
+        out_specs=(VMEM, VMEM),
+        scratch_shapes=ADDERS,
         cost_estimate=pl.CostEstimate(flops=1 << 20, bytes_accessed=1 << 23, transcendentals=0),
         name="collect",
-    )(labels, slots)
-
-
-def assemble(place, mask, labels, slots, first, core):
+    )(mask, slots, core)
+
+
+def assemble(slots, base, pattern):
     def quarter(i):
         return (i, 0)
 
@@ -202,23 +244,17 @@
             jax.ShapeDtypeStruct((1024, 256), jnp.float32),
             jax.ShapeDtypeStruct((1024, 256), jnp.bfloat16),
             jax.ShapeDtypeStruct((3, 256, 512), jnp.bfloat16),
-            jax.ShapeDtypeStruct((1024, 256), jnp.bfloat16),
         ),
         grid=(4,),
-        in_specs=[
-            SMEM, SMEM, SMEM, VMEM,
-            pl.BlockSpec((128, 8, 128), lambda i: (i, 0, 0)),
-            pl.BlockSpec((256, 512), quarter),
-        ],
+        in_specs=[VMEM, pl.BlockSpec((256, 512), quarter), pl.BlockSpec((256, 512), quarter)],
         out_specs=(
             pl.BlockSpec((256, 256), quarter),
             pl.BlockSpec((256, 256), quarter),
             pl.BlockSpec((3, 256, 512), lambda i: (0, 0, 0)),
-            pl.BlockSpec((256, 256), quarter),
         ),
-        scratch_shapes=[pltpu.VMEM((520, 8, 128), jnp.float32)] * 2,
+        scratch_shapes=ADDERS,
         name="assemble",
-    )(place, mask, labels, slots, first, core)
+    )(slots, base, pattern)
 
 
 def ring_of(n, step):
@@ -282,8 +318,7 @@
 
 
 def local(basis_left, basis_right, grid_weight, task_owner, task_block, core_matrix, block_mask):
-    ylo, x, z, core, yhi = (lax.axis_index(a) for a in AXES)
-    row, col = ylo * 4 + x, z * 2 + core
+    ylo, x, z = (lax.axis_index(a) for a in AXES[:3])
     tasks = basis_left.shape[0]
 
     outgoing = contribute(task_owner[:, 0], task_block, basis_left, basis_right, grid_weight)
@@ -296,33 +331,21 @@
     slots = jnp.concatenate([slots, tag_tile], axis=0)
     far = lax.ppermute(slots, "yhi", SWAP)
 
-    def label_of(tag):
-        tag = tag.astype(jnp.float32)
-        return jnp.minimum(tag[:, 0] * 16 + tag[:, 1], 512.0).astype(jnp.int32)
-
-    labels = label_of(tag.reshape(2 * tasks, 2))
-    labels_far = label_of(far[2 * tasks, :4].reshape(2 * tasks, 2))
-    collected = collect(labels, slots)
-    block_rows = row * 32 + jnp.arange(32, dtype=jnp.int32)
-    block_cols = col * 16 + jnp.arange(16, dtype=jnp.int32)
-    mask = (block_mask != 0) | (block_rows[:, None] == block_cols[None, :])
-    place = jnp.stack([row, col, yhi]).astype(jnp.int32)
-    ks_out, own, panel, pattern = assemble(
-        place, mask.astype(jnp.float32).reshape(-1), labels_far, far, collected, core_matrix
-    )
-
-    keep, give = panel[0], panel[1]
-    unit = jnp.concatenate([keep, lax.ppermute(give, "core", SWAP)], axis=1)
+    base, pattern = collect(block_mask, slots, core_matrix)
+    ks_out, own, panel = assemble(far, base, pattern)
+
+    keep, give = panel[0], lax.ppermute(panel[1], "core", SWAP)
+    unit = jnp.concatenate([keep, give], axis=1)
     b = gather_rows(unit, ylo, x, z)
     squares = []
     for m, (near, far, away) in enumerate(product(gather_z(own, True), b, 2)):
         if m > 0:
             away, _ = lax.optimization_barrier((away, squares[0]))
-        mask = pattern[512 * m : 512 * m + 512].astype(jnp.float32)
+        mask = pattern[512 * m : 512 * m + 512, :256].astype(jnp.float32)
         squares.append(mask * (near + far.astype(jnp.float32) + away.astype(jnp.float32)))
     a2 = [gather_z(square.astype(jnp.bfloat16), m == 0) for m, square in enumerate(squares)]
     ((near, far, away),) = product(jnp.concatenate(a2, axis=1), b, 1)
-    cube_term = pattern.astype(jnp.float32) * (near + far.astype(jnp.float32) + away.astype(jnp.float32))
+    cube_term = pattern[:, :256].astype(jnp.float32) * (near + far.astype(jnp.float32) + away.astype(jnp.float32))
     return (ks_out, 3.0 * jnp.concatenate(squares, axis=0) - 2.0 * cube_term)
 
 

time: 204 us -> 204 us (level)
  blocking collectives: 0 us -> 32.6 us
  waiting for transfers between devices: 102 us -> 78.1 us
  starting transfers between devices: 65.9 us -> 52.1 us
  Pallas kernels: 16.5 us -> 23.2 us
  other arithmetic: 4.49 us -> 2.2 us
    all_to_all x0 -> x1, blocking collectives: none -> 32.6 us  [local(): lax.all_to_all(outgoing, AXES[:4], split_axis=0, concat_axis=0, tiled=True)]
    all_to_all x1 -> x0, waiting for transfers between devices: 18.8 us -> none  [local(): lax.all_to_all(outgoing, AXES[:4], split_axis=0, concat_axis=0, tiled=True)]
    all_to_all x1 -> x0, starting transfers between devices: 13.8 us -> none  [local(): lax.all_to_all(outgoing, AXES[:4], split_axis=0, concat_axis=0, tiled=True)]
    pallas_call x1, Pallas kernels: 3.57 us -> 9.89 us  [collect(): pl.pallas_call(collect_kernel, out_shape=(jax.ShapeDtypeStruct((1024, 512...]
    ppermute x1, waiting for transfers between devices: 7.48 us -> 2.76 us  [local(): far = lax.ppermute(slots, 'yhi', SWAP)]
  transfers between devices with their start and end apart: 35 -> 34, of which waited for: 24 -> 23; matrix products, arithmetic and copies ran while one was open for 5% -> 5% of each run, Pallas kernels for 2% -> 5%
where the time goes in v6:
time: 204 us
  waiting for transfers between devices  78.1 us (38%)
  starting transfers between devices  52.1 us (26%)
  blocking collectives  32.6 us (16%)
  Pallas kernels  23.2 us (11%)
  matrix products  9.3 us (5%)
  local copies, waits for them, and re-layouts  5.51 us (3%)
  other arithmetic  2.2 us (1%)
    ppermute x11, waiting for transfers between devices, gather_z(): up = lax.ppermute(up, 'z', ring_of(8, 1))  41.5 us
    all_to_all x1, blocking collectives, local(): lax.all_to_all(outgoing, AXES[:4], split_axis=0, concat_axis=0, tiled=True)  32.6 us
    ppermute x10, starting transfers between devices, gather_z(): down = lax.ppermute(down, 'z', ring_of(8, -1))  32.2 us
    ppermute x3, waiting for transfers between devices, product(): away = lax.ppermute(part, 'yhi', SWAP)  22.4 us
    pallas_call x1, Pallas kernels, collect(): pl.pallas_call(collect_kernel, out_shape=(jax.ShapeDtypeStruct((1024, 512...  9.89 us
    dot_general x4, matrix products, dot(): return jnp.einsum('dmk,dkn->mn', a, b, preferred_element_type=jnp.float32)  9.3 us
    ppermute x3, starting transfers between devices, product(): away = lax.ppermute(part, 'yhi', SWAP)  8.79 us
    pallas_call x1, Pallas kernels, assemble(): pl.pallas_call(functools.partial(assemble_kernel, scale=COUPLING / math.s...  7.79 us
  transfers between devices with their start and end apart: 34, of which 23 were waited for; matrix products, arithmetic and copies ran while one was open for 5% of the time, Pallas kernels for 5%

profile of v6, /device:TPU:2, one launch (start us, length us, event | category | flops | bytes accessed | tf_op | source)
XLA Modules:
  0.0 204.0 jit_solution(1115893275240023127)
XLA Ops:
  0.6 5.5 %contribute.1 = bf16[128,9,2,128]{3,2,1,0:T(2,128)(2,1)} custom-call(s32[128]{0:T(128)} %bitcast.81, s32[128]{0:T(128)} %block_ref.1, bf16[128,32,128]{2,1,0:T(8,128)(2,1)} %left_ref.1, bf16[128,32,128]{2,1,0:T(8,128)(2,1)} %right_ref.1, f32[128,128]{1,0:T(8,128)} %weight_ref.1), custom_call_target="tpu_custom_call" | custom-call | tf_op jit(solution)/shard_map/contribute/pallas_call | solution.py:204
  6.1 32.6 %all_to_all.5 = bf16[128,9,2,128]{3,2,1,0:T(2,128)(2,1)S(1)} all-to-all(bf16[128,9,2,128]{3,2,1,0:T(2,128)(2,1)} %contribute.1), channel_id=1, replica_groups=mesh['ylo'=2,'x'=4,'z'=8,'core'=2,'yhi'=2] {'ylo','x','z','core'}, dimensions={0} | all-to-all | bytes 1179648 | tf_op jit(solution)/shard_map/all_to_all | solution.py:325
  39.4 3.0 %collective-permute-start = (bf16[257,8,128]{2,1,0:T(8,128)(2,1)S(1)}, bf16[257,8,128]{2,1,0:T(8,128)(2,1)S(1)}, u32[]{:S(2)}, u32[]{:S(2)}) collective-permute-start(bf16[257,8,128]{2,1,0:T(8,128)(2,1)S(1)} %pad_maximum_fusion.8.slot_ref), channel_id=1, source_target_pairs={{0,1},{1,0},{2,3},{3,2},{4,5},{5,4},{6,7},{7,6},{8,9},{9,8},{10,11... | collective-permute-start | bytes 1579016 | tf_op jit(solution)/shard_map/ppermute | solution.py:332
  43.0 9.9 %collect.1 = (f32[1024,512]{1,0:T(8,128)}, bf16[1024,512]{1,0:T(8,128)(2,1)}) custom-call(s32[32,16]{1,0:T(8,128)} %copy.10.mask_ref, bf16[257,8,128]{2,1,0:T(8,128)(2,1)} %copy-done.1, f32[1024,512]{1,0:T(8,128)} %core_ref.1), custom_call_target="tpu_custom_call" | custom-call | flops 1048576 | bytes 8388608 | tf_op jit(solution)/shard_map/collect/pallas_call | solution.py:223
  56.5 7.8 %assemble.1 = (f32[1024,256]{1,0:T(8,128)}, bf16[1024,256]{1,0:T(8,128)(2,1)}, bf16[3,256,512]{2,1,0:T(8,128)(2,1)}) custom-call(bf16[257,8,128]{2,1,0:T(8,128)(2,1)} %copy-done.2, f32[1024,512]{1,0:T(8,128)} %get-tuple-element.9.base_ref, bf16[1024,512]{1,0:T(8,128)(2,1)} %get-tuple-element.10.pattern_ref), custom_call_target="tpu_custom_call" | custom-call | tf_op jit(solution)/shard_map/assemble/pallas_call | solution.py:241
  74.1 5.6 %collective-permute-done.1 = bf16[1024,256]{1,0:T(8,128)(2,1)S(1)} collective-permute-done((bf16[1024,256]{1,0:T(8,128)(2,1)}, bf16[1024,256]{1,0:T(8,128)(2,1)S(1)}, u32[]{:S(2)}, u32[]{:S(2)}) %collective-permute-start.1) | collective-permute-done | bytes 524320 | tf_op jit(solution)/shard_map/ppermute | solution.py:269
  79.8 3.2 %collective-permute-start.4 = (bf16[1024,256]{1,0:T(8,128)(2,1)S(1)}, bf16[1024,256]{1,0:T(8,128)(2,1)S(1)}, u32[]{:S(2)}, u32[]{:S(2)}) collective-permute-start(bf16[1024,256]{1,0:T(8,128)(2,1)S(1)} %collective-permute-done.2), channel_id=1, source_target_pairs={{0,28},{4,0},{8,4},{12,8},{16,12},{20,16},{24,20},{28,24},{1,29},{... | collective-permute-start | bytes 1572872 | tf_op jit(solution)/shard_map/ppermute | solution.py:272
  87.5 6.6 %collective-permute-done.3 = bf16[1024,256]{1,0:T(8,128)(2,1)S(1)} collective-permute-done((bf16[1024,256]{1,0:T(8,128)(2,1)S(1)}, bf16[1024,256]{1,0:T(8,128)(2,1)S(1)}, u32[]{:S(2)}, u32[]{:S(2)}) %collective-permute-start.3) | collective-permute-done | bytes 524320 | tf_op jit(solution)/shard_map/ppermute | solution.py:269
  94.1 3.3 %collective-permute-start.6 = (bf16[1024,256]{1,0:T(8,128)(2,1)S(1)}, bf16[1024,256]{1,0:T(8,128)(2,1)S(1)}, u32[]{:S(2)}, u32[]{:S(2)}) collective-permute-start(bf16[1024,256]{1,0:T(8,128)(2,1)S(1)} %collective-permute-done.4), channel_id=1, source_target_pairs={{0,28},{4,0},{8,4},{12,8},{16,12},{20,16},{24,20},{28,24},{1,29},{... | collective-permute-start | bytes 1572872 | tf_op jit(solution)/shard_map/ppermute | solution.py:272
  100.3 7.2 %collective-permute-done.5 = bf16[1024,256]{1,0:T(8,128)(2,1)S(1)} collective-permute-done((bf16[1024,256]{1,0:T(8,128)(2,1)S(1)}, bf16[1024,256]{1,0:T(8,128)(2,1)S(1)}, u32[]{:S(2)}, u32[]{:S(2)}) %collective-permute-start.5) | collective-permute-done | bytes 524320 | tf_op jit(solution)/shard_map/ppermute | solution.py:269
  110.8 9.1 %collective-permute-done.7 = bf16[1024,256]{1,0:T(8,128)(2,1)S(1)} collective-permute-done((bf16[1024,256]{1,0:T(8,128)(2,1)S(1)}, bf16[1024,256]{1,0:T(8,128)(2,1)S(1)}, u32[]{:S(2)}, u32[]{:S(2)}) %collective-permute-start.7) | collective-permute-done | bytes 524320 | tf_op jit(solution)/shard_map/ppermute | solution.py:269
  125.3 3.0 %collective-permute-start.16 = (bf16[512,256]{1,0:T(8,128)(2,1)S(1)}, bf16[512,256]{1,0:T(8,128)(2,1)S(1)}, u32[]{:S(2)}, u32[]{:S(2)}) collective-permute-start(bf16[512,256]{1,0:T(8,128)(2,1)S(1)} %get-tuple-element.22), channel_id=1, source_target_pairs={{0,1},{1,0},{2,3},{3,2},{4,5},{5,4},{6,7},{7,6},{8,9},{9,8},{10,11... | collective-permute-start | bytes 786440 | tf_op jit(solution)/shard_map/ppermute | solution.py:315
  128.3 7.0 %collective-permute-done.16 = bf16[512,256]{1,0:T(8,128)(2,1)S(1)} collective-permute-done((bf16[512,256]{1,0:T(8,128)(2,1)S(1)}, bf16[512,256]{1,0:T(8,128)(2,1)S(1)}, u32[]{:S(2)}, u32[]{:S(2)}) %collective-permute-start.16) | collective-permute-done | bytes 262176 | tf_op jit(solution)/shard_map/ppermute | solution.py:315
  135.3 2.9 %collective-permute-start.17 = (bf16[512,256]{1,0:T(8,128)(2,1)S(1)}, bf16[512,256]{1,0:T(8,128)(2,1)S(1)}, u32[]{:S(2)}, u32[]{:S(2)}) collective-permute-start(bf16[512,256]{1,0:T(8,128)(2,1)S(1)} %get-tuple-element.14), channel_id=1, source_target_pairs={{0,1},{1,0},{2,3},{3,2},{4,5},{5,4},{6,7},{7,6},{8,9},{9,8},{10,11... | collective-permute-start | bytes 786440 | tf_op jit(solution)/shard_map/ppermute | solution.py:315
  138.4 3.2 %collective-permute-start.19 = (bf16[512,256]{1,0:T(8,128)(2,1)S(1)}, bf16[512,256]{1,0:T(8,128)(2,1)S(1)}, u32[]{:S(2)}, u32[]{:S(2)}) collective-permute-start(bf16[512,256]{1,0:T(8,128)(2,1)S(1)} %get-tuple-element.17), channel_id=1, source_target_pairs={{0,28},{4,0},{8,4},{12,8},{16,12},{20,16},{24,20},{28,24},{1,29},{... | collective-permute-start | bytes 786440 | tf_op jit(solution)/shard_map/ppermute | solution.py:272
  144.6 3.2 %collective-permute-start.26 = (bf16[512,256]{1,0:T(8,128)(2,1)S(1)}, bf16[512,256]{1,0:T(8,128)(2,1)S(1)}, u32[]{:S(2)}, u32[]{:S(2)}) collective-permute-start(bf16[512,256]{1,0:T(8,128)(2,1)S(1)} %get-tuple-element.20), channel_id=1, source_target_pairs={{0,28},{4,0},{8,4},{12,8},{16,12},{20,16},{24,20},{28,24},{1,29},{... | collective-permute-start | bytes 786440 | tf_op jit(solution)/shard_map/ppermute | solution.py:272
  147.8 3.5 %collective-permute-start.21 = (bf16[512,256]{1,0:T(8,128)(2,1)S(1)}, bf16[512,256]{1,0:T(8,128)(2,1)S(1)}, u32[]{:S(2)}, u32[]{:S(2)}) collective-permute-start(bf16[512,256]{1,0:T(8,128)(2,1)S(1)} %collective-permute-done.19), channel_id=1, source_target_pairs={{0,28},{4,0},{8,4},{12,8},{16,12},{20,16},{24,20},{28,24},{1,29},{... | collective-permute-start | bytes 786440 | tf_op jit(solution)/shard_map/ppermute | solution.py:272
  151.4 3.6 %collective-permute-done.25 = bf16[512,256]{1,0:T(8,128)(2,1)S(1)} collective-permute-done((bf16[512,256]{1,0:T(8,128)(2,1)S(1)}, bf16[512,256]{1,0:T(8,128)(2,1)S(1)}, u32[]{:S(2)}, u32[]{:S(2)}) %collective-permute-start.25) | collective-permute-done | bytes 262176 | tf_op jit(solution)/shard_map/ppermute | solution.py:269
  155.1 3.3 %collective-permute-start.28 = (bf16[512,256]{1,0:T(8,128)(2,1)S(1)}, bf16[512,256]{1,0:T(8,128)(2,1)S(1)}, u32[]{:S(2)}, u32[]{:S(2)}) collective-permute-start(bf16[512,256]{1,0:T(8,128)(2,1)S(1)} %collective-permute-done.26), channel_id=1, source_target_pairs={{0,28},{4,0},{8,4},{12,8},{16,12},{20,16},{24,20},{28,24},{1,29},{... | collective-permute-start | bytes 786440 | tf_op jit(solution)/shard_map/ppermute | solution.py:272
  160.7 3.3 %collective-permute-start.23 = (bf16[512,256]{1,0:T(8,128)(2,1)S(1)}, bf16[512,256]{1,0:T(8,128)(2,1)S(1)}, u32[]{:S(2)}, u32[]{:S(2)}) collective-permute-start(bf16[512,256]{1,0:T(8,128)(2,1)S(1)} %collective-permute-done.21), channel_id=1, source_target_pairs={{0,28},{4,0},{8,4},{12,8},{16,12},{20,16},{24,20},{28,24},{1,29},{... | collective-permute-start | bytes 786440 | tf_op jit(solution)/shard_map/ppermute | solution.py:272
  166.3 3.3 %collective-permute-start.30 = (bf16[512,256]{1,0:T(8,128)(2,1)S(1)}, bf16[512,256]{1,0:T(8,128)(2,1)S(1)}, u32[]{:S(2)}, u32[]{:S(2)}) collective-permute-start(bf16[512,256]{1,0:T(8,128)(2,1)S(1)} %collective-permute-done.28), channel_id=1, source_target_pairs={{0,28},{4,0},{8,4},{12,8},{16,12},{20,16},{24,20},{28,24},{1,29},{... | collective-permute-start | bytes 786440 | tf_op jit(solution)/shard_map/ppermute | solution.py:272
  174.2 3.7 %collective-permute-start.31 = (bf16[512,256]{1,0:T(8,128)(2,1)S(1)}, bf16[512,256]{1,0:T(8,128)(2,1)S(1)}, u32[]{:S(2)}, u32[]{:S(2)}) collective-permute-start(bf16[512,256]{1,0:T(8,128)(2,1)S(1)} %collective-permute-done.30), channel_id=1, source_target_pairs={{0,28},{4,0},{8,4},{12,8},{16,12},{20,16},{24,20},{28,24},{1,29},{... | collective-permute-start | bytes 786440 | tf_op jit(solution)/shard_map/ppermute | solution.py:272
  187.1 2.9 %collective-permute-start.33 = (bf16[1024,256]{1,0:T(8,128)(2,1)S(1)}, bf16[1024,256]{1,0:T(8,128)(2,1)S(1)}, u32[]{:S(2)}, u32[]{:S(2)}) collective-permute-start(bf16[1024,256]{1,0:T(8,128)(2,1)S(1)} %fusion.18), channel_id=1, source_target_pairs={{0,1},{1,0},{2,3},{3,2},{4,5},{5,4},{6,7},{7,6},{8,9},{9,8},{10,11... | collective-permute-start | bytes 1572872 | tf_op jit(solution)/shard_map/ppermute | solution.py:315
  190.0 12.7 %collective-permute-done.33 = bf16[1024,256]{1,0:T(8,128)(2,1)S(1)} collective-permute-done((bf16[1024,256]{1,0:T(8,128)(2,1)S(1)}, bf16[1024,256]{1,0:T(8,128)(2,1)S(1)}, u32[]{:S(2)}, u32[]{:S(2)}) %collective-permute-start.33) | collective-permute-done | bytes 524320 | tf_op jit(solution)/shard_map/ppermute | solution.py:315
  (105 shorter events, 53.4 us)
Async XLA Ops:
  39.4 16.3 %collective-permute-start = (bf16[257,8,128]{2,1,0:T(8,128)(2,1)S(1)}, bf16[257,8,128]{2,1,0:T(8,128)(2,1)S(1)}, u32[]{:S(2)}, u32[]{:S(2)}) collective-permute-start(bf16[257,8,128]{2,1,0:T(8,128)(2,1)S(1)} %pad_maximum_fusion.8.slot_ref), channel_id=1, source_target_pairs={{0,1},{1,0},{2,3},{3,2},{4,5},{5,4},{6,7},{7,6},{8,9},{9,8},{10,11... | collective-permute-start | bytes 1579016 | tf_op jit(solution)/shard_map/ppermute | solution.py:332
  64.3 15.4 %collective-permute-start.1 = (bf16[1024,256]{1,0:T(8,128)(2,1)}, bf16[1024,256]{1,0:T(8,128)(2,1)S(1)}, u32[]{:S(2)}, u32[]{:S(2)}) collective-permute-start(bf16[1024,256]{1,0:T(8,128)(2,1)} %get-tuple-element.12), channel_id=1, source_target_pairs={{0,4},{4,8},{8,12},{12,16},{16,20},{20,24},{24,28},{28,0},{1,5},{5... | collective-permute-start | bytes 1572872 | tf_op jit(solution)/shard_map/ppermute | solution.py:269
  65.6 14.2 %collective-permute-start.2 = (bf16[1024,256]{1,0:T(8,128)(2,1)}, bf16[1024,256]{1,0:T(8,128)(2,1)S(1)}, u32[]{:S(2)}, u32[]{:S(2)}) collective-permute-start(bf16[1024,256]{1,0:T(8,128)(2,1)} %get-tuple-element.12), channel_id=1, source_target_pairs={{0,28},{4,0},{8,4},{12,8},{16,12},{20,16},{24,20},{28,24},{1,29},{... | collective-permute-start | bytes 1572872 | tf_op jit(solution)/shard_map/ppermute | solution.py:272
  70.4 14.1 %collective-permute-start.9 = (bf16[256,1024]{1,0:T(8,128)(2,1)S(1)}, bf16[256,1024]{1,0:T(8,128)(2,1)S(1)}, u32[]{:S(2)}, u32[]{:S(2)}) collective-permute-start(bf16[256,1024]{1,0:T(8,128)(2,1)S(1)} %pad_maximum_fusion.9), channel_id=1, source_target_pairs={{0,128},{128,0},{1,129},{129,1},{2,130},{130,2},{3,131},{131,3},{4... | collective-permute-start | bytes 1572872 | tf_op jit(solution)/shard_map/ppermute | solution.py:284
  71.5 13.7 %collective-permute-start.10 = (bf16[256,1024]{1,0:T(8,128)(2,1)S(1)}, bf16[256,1024]{1,0:T(8,128)(2,1)S(1)}, u32[]{:S(2)}, u32[]{:S(2)}) collective-permute-start(bf16[256,1024]{1,0:T(8,128)(2,1)S(1)} %pad_maximum_fusion.9), channel_id=1, source_target_pairs={{0,32},{32,64},{64,96},{96,0},{1,33},{33,65},{65,97},{97,1},{2,34}... | collective-permute-start | bytes 1572872 | tf_op jit(solution)/shard_map/ppermute | solution.py:285
  72.8 21.3 %collective-permute-start.11 = (bf16[256,1024]{1,0:T(8,128)(2,1)S(1)}, bf16[256,1024]{1,0:T(8,128)(2,1)S(1)}, u32[]{:S(2)}, u32[]{:S(2)}) collective-permute-start(bf16[256,1024]{1,0:T(8,128)(2,1)S(1)} %pad_maximum_fusion.9), channel_id=1, source_target_pairs={{0,96},{32,0},{64,32},{96,64},{1,97},{33,1},{65,33},{97,65},{2,98}... | collective-permute-start | bytes 1572872 | tf_op jit(solution)/shard_map/ppermute | solution.py:286
  79.8 14.3 %collective-permute-start.3 = (bf16[1024,256]{1,0:T(8,128)(2,1)S(1)}, bf16[1024,256]{1,0:T(8,128)(2,1)S(1)}, u32[]{:S(2)}, u32[]{:S(2)}) collective-permute-start(bf16[1024,256]{1,0:T(8,128)(2,1)S(1)} %collective-permute-done.1), channel_id=1, source_target_pairs={{0,4},{4,8},{8,12},{12,16},{16,20},{20,24},{24,28},{28,0},{1,5},{5... | collective-permute-start | bytes 1572872 | tf_op jit(solution)/shard_map/ppermute | solution.py:269
  79.8 14.4 %collective-permute-start.4 = (bf16[1024,256]{1,0:T(8,128)(2,1)S(1)}, bf16[1024,256]{1,0:T(8,128)(2,1)S(1)}, u32[]{:S(2)}, u32[]{:S(2)}) collective-permute-start(bf16[1024,256]{1,0:T(8,128)(2,1)S(1)} %collective-permute-done.2), channel_id=1, source_target_pairs={{0,28},{4,0},{8,4},{12,8},{16,12},{20,16},{24,20},{28,24},{1,29},{... | collective-permute-start | bytes 1572872 | tf_op jit(solution)/shard_map/ppermute | solution.py:272
  85.3 24.1 %collective-permute-start.12 = (bf16[2,256,1024]{2,1,0:T(8,128)(2,1)S(1)}, bf16[2,256,1024]{2,1,0:T(8,128)(2,1)S(1)}, u32[]{:S(2)}, u32[]{:S(2)}) collective-permute-start(bf16[2,256,1024]{2,1,0:T(8,128)(2,1)S(1)} %pad_maximum_fusion.7), channel_id=1, source_target_pairs={{0,32},{32,64},{64,96},{96,0},{1,33},{33,65},{65,97},{97,1},{2,34}... | collective-permute-start | bytes 3145736 | tf_op jit(solution)/shard_map/ppermute | solution.py:287
  86.6 12.5 %collective-permute-start.13 = (bf16[256,1024]{1,0:T(8,128)(2,1)S(1)}, bf16[256,1024]{1,0:T(8,128)(2,1)S(1)}, u32[]{:S(2)}, u32[]{:S(2)}) collective-permute-start(bf16[256,1024]{1,0:T(8,128)(2,1)S(1)} %collective-permute-done.9), channel_id=1, source_target_pairs={{0,96},{32,0},{64,32},{96,64},{1,97},{33,1},{65,33},{97,65},{2,98}... | collective-permute-start | bytes 1572872 | tf_op jit(solution)/shard_map/ppermute | solution.py:288
  94.1 13.4 %collective-permute-start.5 = (bf16[1024,256]{1,0:T(8,128)(2,1)S(1)}, bf16[1024,256]{1,0:T(8,128)(2,1)S(1)}, u32[]{:S(2)}, u32[]{:S(2)}) collective-permute-start(bf16[1024,256]{1,0:T(8,128)(2,1)S(1)} %collective-permute-done.3), channel_id=1, source_target_pairs={{0,4},{4,8},{8,12},{12,16},{16,20},{20,24},{24,28},{28,0},{1,5},{5... | collective-permute-start | bytes 1572872 | tf_op jit(solution)/shard_map/ppermute | solution.py:269
  94.1 13.4 %collective-permute-start.6 = (bf16[1024,256]{1,0:T(8,128)(2,1)S(1)}, bf16[1024,256]{1,0:T(8,128)(2,1)S(1)}, u32[]{:S(2)}, u32[]{:S(2)}) collective-permute-start(bf16[1024,256]{1,0:T(8,128)(2,1)S(1)} %collective-permute-done.4), channel_id=1, source_target_pairs={{0,28},{4,0},{8,4},{12,8},{16,12},{20,16},{24,20},{28,24},{1,29},{... | collective-permute-start | bytes 1572872 | tf_op jit(solution)/shard_map/ppermute | solution.py:272
  99.2 11.6 %collective-permute-start.14 = (bf16[256,1024]{1,0:T(8,128)(2,1)S(1)}, bf16[256,1024]{1,0:T(8,128)(2,1)S(1)}, u32[]{:S(2)}, u32[]{:S(2)}) collective-permute-start(bf16[256,1024]{1,0:T(8,128)(2,1)S(1)} %collective-permute-done.13), channel_id=1, source_target_pairs={{0,96},{32,0},{64,32},{96,64},{1,97},{33,1},{65,33},{97,65},{2,98}... | collective-permute-start | bytes 1572872 | tf_op jit(solution)/shard_map/ppermute | solution.py:289
  107.5 12.5 %collective-permute-start.7 = (bf16[1024,256]{1,0:T(8,128)(2,1)S(1)}, bf16[1024,256]{1,0:T(8,128)(2,1)S(1)}, u32[]{:S(2)}, u32[]{:S(2)}) collective-permute-start(bf16[1024,256]{1,0:T(8,128)(2,1)S(1)} %collective-permute-done.5), channel_id=1, source_target_pairs={{0,4},{4,8},{8,12},{12,16},{16,20},{20,24},{24,28},{28,0},{1,5},{5... | collective-permute-start | bytes 1572872 | tf_op jit(solution)/shard_map/ppermute | solution.py:269
  144.5 10.5 %collective-permute-start.25 = (bf16[512,256]{1,0:T(8,128)(2,1)S(1)}, bf16[512,256]{1,0:T(8,128)(2,1)S(1)}, u32[]{:S(2)}, u32[]{:S(2)}) collective-permute-start(bf16[512,256]{1,0:T(8,128)(2,1)S(1)} %get-tuple-element.20), channel_id=1, source_target_pairs={{0,4},{4,8},{8,12},{12,16},{16,20},{20,24},{24,28},{28,0},{1,5},{5... | collective-permute-start | bytes 786440 | tf_op jit(solution)/shard_map/ppermute | solution.py:269
  144.6 10.5 %collective-permute-start.26 = (bf16[512,256]{1,0:T(8,128)(2,1)S(1)}, bf16[512,256]{1,0:T(8,128)(2,1)S(1)}, u32[]{:S(2)}, u32[]{:S(2)}) collective-permute-start(bf16[512,256]{1,0:T(8,128)(2,1)S(1)} %get-tuple-element.20), channel_id=1, source_target_pairs={{0,28},{4,0},{8,4},{12,8},{16,12},{20,16},{24,20},{28,24},{1,29},{... | collective-permute-start | bytes 786440 | tf_op jit(solution)/shard_map/ppermute | solution.py:272
  147.8 12.8 %collective-permute-start.20 = (bf16[512,256]{1,0:T(8,128)(2,1)S(1)}, bf16[512,256]{1,0:T(8,128)(2,1)S(1)}, u32[]{:S(2)}, u32[]{:S(2)}) collective-permute-start(bf16[512,256]{1,0:T(8,128)(2,1)S(1)} %collective-permute-done.18), channel_id=1, source_target_pairs={{0,4},{4,8},{8,12},{12,16},{16,20},{20,24},{24,28},{28,0},{1,5},{5... | collective-permute-start | bytes 786440 | tf_op jit(solution)/shard_map/ppermute | solution.py:269
  147.8 12.8 %collective-permute-start.21 = (bf16[512,256]{1,0:T(8,128)(2,1)S(1)}, bf16[512,256]{1,0:T(8,128)(2,1)S(1)}, u32[]{:S(2)}, u32[]{:S(2)}) collective-permute-start(bf16[512,256]{1,0:T(8,128)(2,1)S(1)} %collective-permute-done.19), channel_id=1, source_target_pairs={{0,28},{4,0},{8,4},{12,8},{16,12},{20,16},{24,20},{28,24},{1,29},{... | collective-permute-start | bytes 786440 | tf_op jit(solution)/shard_map/ppermute | solution.py:272
  155.0 11.2 %collective-permute-start.27 = (bf16[512,256]{1,0:T(8,128)(2,1)S(1)}, bf16[512,256]{1,0:T(8,128)(2,1)S(1)}, u32[]{:S(2)}, u32[]{:S(2)}) collective-permute-start(bf16[512,256]{1,0:T(8,128)(2,1)S(1)} %collective-permute-done.25), channel_id=1, source_target_pairs={{0,4},{4,8},{8,12},{12,16},{16,20},{20,24},{24,28},{28,0},{1,5},{5... | collective-permute-start | bytes 786440 | tf_op jit(solution)/shard_map/ppermute | solution.py:269
  155.1 11.2 %collective-permute-start.28 = (bf16[512,256]{1,0:T(8,128)(2,1)S(1)}, bf16[512,256]{1,0:T(8,128)(2,1)S(1)}, u32[]{:S(2)}, u32[]{:S(2)}) collective-permute-start(bf16[512,256]{1,0:T(8,128)(2,1)S(1)} %collective-permute-done.26), channel_id=1, source_target_pairs={{0,28},{4,0},{8,4},{12,8},{16,12},{20,16},{24,20},{28,24},{1,29},{... | collective-permute-start | bytes 786440 | tf_op jit(solution)/shard_map/ppermute | solution.py:272
  160.6 11.2 %collective-permute-start.22 = (bf16[512,256]{1,0:T(8,128)(2,1)S(1)}, bf16[512,256]{1,0:T(8,128)(2,1)S(1)}, u32[]{:S(2)}, u32[]{:S(2)}) collective-permute-start(bf16[512,256]{1,0:T(8,128)(2,1)S(1)} %collective-permute-done.20), channel_id=1, source_target_pairs={{0,4},{4,8},{8,12},{12,16},{16,20},{20,24},{24,28},{28,0},{1,5},{5... | collective-permute-start | bytes 786440 | tf_op jit(solution)/shard_map/ppermute | solution.py:269
  160.7 11.2 %collective-permute-start.23 = (bf16[512,256]{1,0:T(8,128)(2,1)S(1)}, bf16[512,256]{1,0:T(8,128)(2,1)S(1)}, u32[]{:S(2)}, u32[]{:S(2)}) collective-permute-start(bf16[512,256]{1,0:T(8,128)(2,1)S(1)} %collective-permute-done.21), channel_id=1, source_target_pairs={{0,28},{4,0},{8,4},{12,8},{16,12},{20,16},{24,20},{28,24},{1,29},{... | collective-permute-start | bytes 786440 | tf_op jit(solution)/shard_map/ppermute | solution.py:272
  166.3 11.7 %collective-permute-start.29 = (bf16[512,256]{1,0:T(8,128)(2,1)S(1)}, bf16[512,256]{1,0:T(8,128)(2,1)S(1)}, u32[]{:S(2)}, u32[]{:S(2)}) collective-permute-start(bf16[512,256]{1,0:T(8,128)(2,1)S(1)} %collective-permute-done.27), channel_id=1, source_target_pairs={{0,4},{4,8},{8,12},{12,16},{16,20},{20,24},{24,28},{28,0},{1,5},{5... | collective-permute-start | bytes 786440 | tf_op jit(solution)/shard_map/ppermute | solution.py:269
  187.1 15.6 %collective-permute-start.33 = (bf16[1024,256]{1,0:T(8,128)(2,1)S(1)}, bf16[1024,256]{1,0:T(8,128)(2,1)S(1)}, u32[]{:S(2)}, u32[]{:S(2)}) collective-permute-start(bf16[1024,256]{1,0:T(8,128)(2,1)S(1)} %fusion.18), channel_id=1, source_target_pairs={{0,1},{1,0},{2,3},{3,2},{4,5},{5,4},{6,7},{7,6},{8,9},{9,8},{10,11... | collective-permute-start | bytes 1572872 | tf_op jit(solution)/shard_map/ppermute | solution.py:315
  (14 other events, 131.5 us)

commit v7 on v6

--- a/solution.py
+++ b/solution.py
@@ -93,10 +93,12 @@
     pltpu.sync_copy(vector_ref, label_ref)
 
 
-def add_slots(even_ref, odd_ref, label_ref, slot_ref):
+def clear(even_ref, odd_ref):
     even_ref[...] = jnp.zeros_like(even_ref)
     odd_ref[...] = jnp.zeros_like(odd_ref)
 
+
+def add_slots(even_ref, odd_ref, label_ref, slot_ref):
     def add(s, carry):
         for u in range(4):
             at = s * 8 + 2 * u
@@ -127,6 +129,7 @@
 def collect_kernel(
     mask_ref, slot_ref, core_ref, base_ref, pattern_ref, even_ref, odd_ref, vector_ref, label_ref
 ):
+    clear(even_ref, odd_ref)
     read_labels(slot_ref, vector_ref, label_ref)
     add_slots(even_ref, odd_ref, label_ref, slot_ref)
     row, col, half_own = where_am_i()
@@ -157,13 +160,17 @@
 
 
 def assemble_kernel(
-    slot_ref, base_ref, pattern_ref, ks_ref, own_ref, panel_ref,
-    even_ref, odd_ref, vector_ref, label_ref, *, scale,
+    far_ref, base_ref, pattern_ref, ks_ref, own_ref, panel_ref,
+    even_ref, odd_ref, vector_ref, label_ref, slot_ref, sem, *, scale,
 ):
     step = pl.program_id(0)
 
     @pl.when(step == 0)
     def _():
+        load = pltpu.make_async_copy(far_ref, slot_ref, sem)
+        load.start()
+        clear(even_ref, odd_ref)
+        load.wait()
         read_labels(slot_ref, vector_ref, label_ref)
         add_slots(even_ref, odd_ref, label_ref, slot_ref)
 
@@ -192,7 +199,7 @@
                     own_ref[pl.ds(r0, 32), at] = x
         return carry
 
-    lax.fori_loop(0, 8, body, 0, unroll=2)
+    lax.fori_loop(0, 8, body, 0, unroll=4)
 
 
 VMEM = pl.BlockSpec(memory_space=pltpu.VMEM)
@@ -207,6 +214,7 @@
         in_specs=[SMEM, SMEM, VMEM, VMEM, VMEM],
         out_specs=VMEM,
         scratch_shapes=[pltpu.SMEM((tasks,), jnp.int32), pltpu.SMEM((2 * tasks,), jnp.int32)],
+        compiler_params=pltpu.CompilerParams(vmem_limit_bytes=12 * 2**20),
         name="contribute",
     )(owner, block, left, right, weight)
 
@@ -230,6 +238,7 @@
         out_specs=(VMEM, VMEM),
         scratch_shapes=ADDERS,
         cost_estimate=pl.CostEstimate(flops=1 << 20, bytes_accessed=1 << 23, transcendentals=0),
+        compiler_params=pltpu.CompilerParams(vmem_limit_bytes=20 * 2**20),
         name="collect",
     )(mask, slots, core)
 
@@ -246,13 +255,18 @@
             jax.ShapeDtypeStruct((3, 256, 512), jnp.bfloat16),
         ),
         grid=(4,),
-        in_specs=[VMEM, pl.BlockSpec((256, 512), quarter), pl.BlockSpec((256, 512), quarter)],
+        in_specs=[
+            pl.BlockSpec(memory_space=pl.ANY),
+            pl.BlockSpec((256, 512), quarter),
+            pl.BlockSpec((256, 512), quarter),
+        ],
         out_specs=(
             pl.BlockSpec((256, 256), quarter),
             pl.BlockSpec((256, 256), quarter),
             pl.BlockSpec((3, 256, 512), lambda i: (0, 0, 0)),
         ),
-        scratch_shapes=ADDERS,
+        scratch_shapes=ADDERS + [pltpu.VMEM((257, 8, 128), jnp.bfloat16), pltpu.SemaphoreType.DMA],
+        compiler_params=pltpu.CompilerParams(vmem_limit_bytes=20 * 2**20),
         name="assemble",
     )(slots, base, pattern)
 

time: 204 us -> 203 us (level)
  Pallas kernels: 23.2 us -> 16 us
  waiting for transfers between devices: 78.1 us -> 81.9 us
  local copies, waits for them, and re-layouts: 5.51 us -> 8.19 us
    unnamed x28 -> x34, local copies, waits for them, and re-layouts: 3.01 us -> 6.73 us
    ppermute x11, waiting for transfers between devices: 41.5 us -> 45 us  [gather_z(): up = lax.ppermute(up, 'z', ring_of(8, 1))]
    pallas_call x1, Pallas kernels: 9.89 us -> 7.15 us  [collect(): pl.pallas_call(collect_kernel, out_shape=(jax.ShapeDtypeStruct((1024, 512...]
    pallas_call x1, Pallas kernels: 7.79 us -> 5.16 us  [assemble(): pl.pallas_call(functools.partial(assemble_kernel, scale=COUPLING / math.s...]
  transfers between devices with their start and end apart: 34 -> 34, of which waited for: 23 -> 23; matrix products, arithmetic and copies ran while one was open for 5% -> 3% of each run, Pallas kernels for 5% -> 4%
where the time goes in v7:
time: 203 us
  waiting for transfers between devices  81.9 us (40%)
  starting transfers between devices  51.9 us (26%)
  blocking collectives  32.4 us (16%)
  Pallas kernels  16 us (8%)
  matrix products  9.3 us (5%)
  local copies, waits for them, and re-layouts  8.19 us (4%)
  other arithmetic  2.2 us (1%)
    ppermute x11, waiting for transfers between devices, gather_z(): up = lax.ppermute(up, 'z', ring_of(8, 1))  45 us
    all_to_all x1, blocking collectives, local(): lax.all_to_all(outgoing, AXES[:4], split_axis=0, concat_axis=0, tiled=True)  32.4 us
    ppermute x10, starting transfers between devices, gather_z(): down = lax.ppermute(down, 'z', ring_of(8, -1))  32 us
    ppermute x3, waiting for transfers between devices, product(): away = lax.ppermute(part, 'yhi', SWAP)  22.4 us
    dot_general x4, matrix products, dot(): return jnp.einsum('dmk,dkn->mn', a, b, preferred_element_type=jnp.float32)  9.3 us
    ppermute x3, starting transfers between devices, product(): away = lax.ppermute(part, 'yhi', SWAP)  8.8 us
    pallas_call x1, Pallas kernels, collect(): pl.pallas_call(collect_kernel, out_shape=(jax.ShapeDtypeStruct((1024, 512...  7.15 us
    unnamed x34, local copies, waits for them, and re-layouts  6.73 us
  transfers between devices with their start and end apart: 34, of which 23 were waited for; matrix products, arithmetic and copies ran while one was open for 3% of the time, Pallas kernels for 4%

profile of v7, /device:TPU:2, one launch (start us, length us, event | category | flops | bytes accessed | tf_op | source)
XLA Modules:
  0.0 202.9 jit_solution(14512665375286400418)
XLA Ops:
  5.2 3.6 %contribute.1 = bf16[128,9,2,128]{3,2,1,0:T(2,128)(2,1)S(1)} custom-call(s32[128]{0:T(128)S(1)} %bitcast.78, s32[128]{0:T(128)S(1)} %copy-done.5, bf16[128,32,128]{2,1,0:T(8,128)(2,1)S(1)} %copy-done.1, bf16[128,32,128]{2,1,0:T(8,128)(2,1)S(1)} %copy-done.2, f32[128,128]{1,0:T(8,128)S(1)} %copy-done.3), custom_call_target="tpu_custom_call" | custom-call | tf_op jit(solution)/shard_map/contribute/pallas_call | solution.py:211
  8.9 32.4 %all_to_all.5 = bf16[128,9,2,128]{3,2,1,0:T(2,128)(2,1)S(1)} all-to-all(bf16[128,9,2,128]{3,2,1,0:T(2,128)(2,1)S(1)} %contribute.1), channel_id=1, replica_groups=mesh['ylo'=2,'x'=4,'z'=8,'core'=2,'yhi'=2] {'ylo','x','z','core'}, dimensions={0} | all-to-all | bytes 1179648 | tf_op jit(solution)/shard_map/all_to_all | solution.py:339
  41.9 3.0 %collective-permute-start = (bf16[257,8,128]{2,1,0:T(8,128)(2,1)S(1)}, bf16[257,8,128]{2,1,0:T(8,128)(2,1)S(1)}, u32[]{:S(2)}, u32[]{:S(2)}) collective-permute-start(bf16[257,8,128]{2,1,0:T(8,128)(2,1)S(1)} %pad_maximum_fusion.8.slot_ref), channel_id=1, source_target_pairs={{0,1},{1,0},{2,3},{3,2},{4,5},{5,4},{6,7},{7,6},{8,9},{9,8},{10,11... | collective-permute-start | bytes 1579016 | tf_op jit(solution)/shard_map/ppermute | solution.py:346
  46.6 7.1 %collect.1 = (f32[1024,512]{1,0:T(8,128)S(1)}, bf16[1024,512]{1,0:T(8,128)(2,1)S(1)}) custom-call(s32[32,16]{1,0:T(8,128)S(1)} %copy.10.mask_ref, bf16[257,8,128]{2,1,0:T(8,128)(2,1)S(1)} %pad_maximum_fusion.8.slot_ref, f32[1024,512]{1,0:T(8,128)S(1)} %copy-done), custom_call_target="tpu_custom_call" | custom-call | flops 1048576 | bytes 8388608 | tf_op jit(solution)/shard_map/collect/pallas_call | solution.py:231
  53.8 4.5 %collective-permute-done.far_ref = bf16[257,8,128]{2,1,0:T(8,128)(2,1)S(1)} collective-permute-done((bf16[257,8,128]{2,1,0:T(8,128)(2,1)S(1)}, bf16[257,8,128]{2,1,0:T(8,128)(2,1)S(1)}, u32[]{:S(2)}, u32[]{:S(2)}) %collective-permute-start) | collective-permute-done | bytes 526368 | tf_op jit(solution)/shard_map/ppermute | solution.py:346
  58.3 5.2 %assemble.1 = (f32[1024,256]{1,0:T(8,128)}, bf16[1024,256]{1,0:T(8,128)(2,1)S(1)}, bf16[3,256,512]{2,1,0:T(8,128)(2,1)S(1)}) custom-call(bf16[257,8,128]{2,1,0:T(8,128)(2,1)S(1)} %collective-permute-done.far_ref, f32[1024,512]{1,0:T(8,128)S(1)} %get-tuple-element.9.base_ref, bf16[1024,512]{1,0:T(8,128)(2,1)S(1)} %get-tuple-element.10.pattern_ref), custom_call_target="tpu_custom_call" | custom-call | tf_op jit(solution)/shard_map/assemble/pallas_call | solution.py:250
  72.2 6.5 %collective-permute-done.1 = bf16[1024,256]{1,0:T(8,128)(2,1)S(1)} collective-permute-done((bf16[1024,256]{1,0:T(8,128)(2,1)S(1)}, bf16[1024,256]{1,0:T(8,128)(2,1)S(1)}, u32[]{:S(2)}, u32[]{:S(2)}) %collective-permute-start.1) | collective-permute-done | bytes 524320 | tf_op jit(solution)/shard_map/ppermute | solution.py:283
  78.7 3.2 %collective-permute-start.4 = (bf16[1024,256]{1,0:T(8,128)(2,1)S(1)}, bf16[1024,256]{1,0:T(8,128)(2,1)S(1)}, u32[]{:S(2)}, u32[]{:S(2)}) collective-permute-start(bf16[1024,256]{1,0:T(8,128)(2,1)S(1)} %collective-permute-done.2), channel_id=1, source_target_pairs={{0,28},{4,0},{8,4},{12,8},{16,12},{20,16},{24,20},{28,24},{1,29},{... | collective-permute-start | bytes 1572872 | tf_op jit(solution)/shard_map/ppermute | solution.py:286
  85.6 7.4 %collective-permute-done.3 = bf16[1024,256]{1,0:T(8,128)(2,1)S(1)} collective-permute-done((bf16[1024,256]{1,0:T(8,128)(2,1)S(1)}, bf16[1024,256]{1,0:T(8,128)(2,1)S(1)}, u32[]{:S(2)}, u32[]{:S(2)}) %collective-permute-start.3) | collective-permute-done | bytes 524320 | tf_op jit(solution)/shard_map/ppermute | solution.py:283
  93.0 3.3 %collective-permute-start.6 = (bf16[1024,256]{1,0:T(8,128)(2,1)S(1)}, bf16[1024,256]{1,0:T(8,128)(2,1)S(1)}, u32[]{:S(2)}, u32[]{:S(2)}) collective-permute-start(bf16[1024,256]{1,0:T(8,128)(2,1)S(1)} %collective-permute-done.4), channel_id=1, source_target_pairs={{0,28},{4,0},{8,4},{12,8},{16,12},{20,16},{24,20},{28,24},{1,29},{... | collective-permute-start | bytes 1572872 | tf_op jit(solution)/shard_map/ppermute | solution.py:286
  98.4 8.0 %collective-permute-done.5 = bf16[1024,256]{1,0:T(8,128)(2,1)S(1)} collective-permute-done((bf16[1024,256]{1,0:T(8,128)(2,1)S(1)}, bf16[1024,256]{1,0:T(8,128)(2,1)S(1)}, u32[]{:S(2)}, u32[]{:S(2)}) %collective-permute-start.5) | collective-permute-done | bytes 524320 | tf_op jit(solution)/shard_map/ppermute | solution.py:283
  108.9 9.9 %collective-permute-done.7 = bf16[1024,256]{1,0:T(8,128)(2,1)S(1)} collective-permute-done((bf16[1024,256]{1,0:T(8,128)(2,1)S(1)}, bf16[1024,256]{1,0:T(8,128)(2,1)S(1)}, u32[]{:S(2)}, u32[]{:S(2)}) %collective-permute-start.7) | collective-permute-done | bytes 524320 | tf_op jit(solution)/shard_map/ppermute | solution.py:283
  124.2 3.0 %collective-permute-start.16 = (bf16[512,256]{1,0:T(8,128)(2,1)S(1)}, bf16[512,256]{1,0:T(8,128)(2,1)S(1)}, u32[]{:S(2)}, u32[]{:S(2)}) collective-permute-start(bf16[512,256]{1,0:T(8,128)(2,1)S(1)} %get-tuple-element.22), channel_id=1, source_target_pairs={{0,1},{1,0},{2,3},{3,2},{4,5},{5,4},{6,7},{7,6},{8,9},{9,8},{10,11... | collective-permute-start | bytes 786440 | tf_op jit(solution)/shard_map/ppermute | solution.py:329
  127.2 7.0 %collective-permute-done.16 = bf16[512,256]{1,0:T(8,128)(2,1)S(1)} collective-permute-done((bf16[512,256]{1,0:T(8,128)(2,1)S(1)}, bf16[512,256]{1,0:T(8,128)(2,1)S(1)}, u32[]{:S(2)}, u32[]{:S(2)}) %collective-permute-start.16) | collective-permute-done | bytes 262176 | tf_op jit(solution)/shard_map/ppermute | solution.py:329
  137.3 3.2 %collective-permute-start.19 = (bf16[512,256]{1,0:T(8,128)(2,1)S(1)}, bf16[512,256]{1,0:T(8,128)(2,1)S(1)}, u32[]{:S(2)}, u32[]{:S(2)}) collective-permute-start(bf16[512,256]{1,0:T(8,128)(2,1)S(1)} %get-tuple-element.17), channel_id=1, source_target_pairs={{0,28},{4,0},{8,4},{12,8},{16,12},{20,16},{24,20},{28,24},{1,29},{... | collective-permute-start | bytes 786440 | tf_op jit(solution)/shard_map/ppermute | solution.py:286
  143.5 3.2 %collective-permute-start.26 = (bf16[512,256]{1,0:T(8,128)(2,1)S(1)}, bf16[512,256]{1,0:T(8,128)(2,1)S(1)}, u32[]{:S(2)}, u32[]{:S(2)}) collective-permute-start(bf16[512,256]{1,0:T(8,128)(2,1)S(1)} %get-tuple-element.20), channel_id=1, source_target_pairs={{0,28},{4,0},{8,4},{12,8},{16,12},{20,16},{24,20},{28,24},{1,29},{... | collective-permute-start | bytes 786440 | tf_op jit(solution)/shard_map/ppermute | solution.py:286
  146.7 3.3 %collective-permute-start.21 = (bf16[512,256]{1,0:T(8,128)(2,1)S(1)}, bf16[512,256]{1,0:T(8,128)(2,1)S(1)}, u32[]{:S(2)}, u32[]{:S(2)}) collective-permute-start(bf16[512,256]{1,0:T(8,128)(2,1)S(1)} %collective-permute-done.19), channel_id=1, source_target_pairs={{0,28},{4,0},{8,4},{12,8},{16,12},{20,16},{24,20},{28,24},{1,29},{... | collective-permute-start | bytes 786440 | tf_op jit(solution)/shard_map/ppermute | solution.py:286
  150.1 3.8 %collective-permute-done.25 = bf16[512,256]{1,0:T(8,128)(2,1)S(1)} collective-permute-done((bf16[512,256]{1,0:T(8,128)(2,1)S(1)}, bf16[512,256]{1,0:T(8,128)(2,1)S(1)}, u32[]{:S(2)}, u32[]{:S(2)}) %collective-permute-start.25) | collective-permute-done | bytes 262176 | tf_op jit(solution)/shard_map/ppermute | solution.py:283
  154.0 3.3 %collective-permute-start.28 = (bf16[512,256]{1,0:T(8,128)(2,1)S(1)}, bf16[512,256]{1,0:T(8,128)(2,1)S(1)}, u32[]{:S(2)}, u32[]{:S(2)}) collective-permute-start(bf16[512,256]{1,0:T(8,128)(2,1)S(1)} %collective-permute-done.26), channel_id=1, source_target_pairs={{0,28},{4,0},{8,4},{12,8},{16,12},{20,16},{24,20},{28,24},{1,29},{... | collective-permute-start | bytes 786440 | tf_op jit(solution)/shard_map/ppermute | solution.py:286
  159.6 3.3 %collective-permute-start.23 = (bf16[512,256]{1,0:T(8,128)(2,1)S(1)}, bf16[512,256]{1,0:T(8,128)(2,1)S(1)}, u32[]{:S(2)}, u32[]{:S(2)}) collective-permute-start(bf16[512,256]{1,0:T(8,128)(2,1)S(1)} %collective-permute-done.21), channel_id=1, source_target_pairs={{0,28},{4,0},{8,4},{12,8},{16,12},{20,16},{24,20},{28,24},{1,29},{... | collective-permute-start | bytes 786440 | tf_op jit(solution)/shard_map/ppermute | solution.py:286
  165.2 3.3 %collective-permute-start.30 = (bf16[512,256]{1,0:T(8,128)(2,1)S(1)}, bf16[512,256]{1,0:T(8,128)(2,1)S(1)}, u32[]{:S(2)}, u32[]{:S(2)}) collective-permute-start(bf16[512,256]{1,0:T(8,128)(2,1)S(1)} %collective-permute-done.28), channel_id=1, source_target_pairs={{0,28},{4,0},{8,4},{12,8},{16,12},{20,16},{24,20},{28,24},{1,29},{... | collective-permute-start | bytes 786440 | tf_op jit(solution)/shard_map/ppermute | solution.py:286
  173.1 3.7 %collective-permute-start.31 = (bf16[512,256]{1,0:T(8,128)(2,1)S(1)}, bf16[512,256]{1,0:T(8,128)(2,1)S(1)}, u32[]{:S(2)}, u32[]{:S(2)}) collective-permute-start(bf16[512,256]{1,0:T(8,128)(2,1)S(1)} %collective-permute-done.30), channel_id=1, source_target_pairs={{0,28},{4,0},{8,4},{12,8},{16,12},{20,16},{24,20},{28,24},{1,29},{... | collective-permute-start | bytes 786440 | tf_op jit(solution)/shard_map/ppermute | solution.py:286
  186.0 2.9 %collective-permute-start.33 = (bf16[1024,256]{1,0:T(8,128)(2,1)S(1)}, bf16[1024,256]{1,0:T(8,128)(2,1)S(1)}, u32[]{:S(2)}, u32[]{:S(2)}) collective-permute-start(bf16[1024,256]{1,0:T(8,128)(2,1)S(1)} %fusion.18), channel_id=1, source_target_pairs={{0,1},{1,0},{2,3},{3,2},{4,5},{5,4},{6,7},{7,6},{8,9},{9,8},{10,11... | collective-permute-start | bytes 1572872 | tf_op jit(solution)/shard_map/ppermute | solution.py:329
  188.9 12.7 %collective-permute-done.33 = bf16[1024,256]{1,0:T(8,128)(2,1)S(1)} collective-permute-done((bf16[1024,256]{1,0:T(8,128)(2,1)S(1)}, bf16[1024,256]{1,0:T(8,128)(2,1)S(1)}, u32[]{:S(2)}, u32[]{:S(2)}) %collective-permute-start.33) | collective-permute-done | bytes 524320 | tf_op jit(solution)/shard_map/ppermute | solution.py:329
  (111 shorter events, 54.8 us)
Async XLA Ops:
  41.9 16.3 %collective-permute-start = (bf16[257,8,128]{2,1,0:T(8,128)(2,1)S(1)}, bf16[257,8,128]{2,1,0:T(8,128)(2,1)S(1)}, u32[]{:S(2)}, u32[]{:S(2)}) collective-permute-start(bf16[257,8,128]{2,1,0:T(8,128)(2,1)S(1)} %pad_maximum_fusion.8.slot_ref), channel_id=1, source_target_pairs={{0,1},{1,0},{2,3},{3,2},{4,5},{5,4},{6,7},{7,6},{8,9},{9,8},{10,11... | collective-permute-start | bytes 1579016 | tf_op jit(solution)/shard_map/ppermute | solution.py:346
  63.4 15.2 %collective-permute-start.1 = (bf16[1024,256]{1,0:T(8,128)(2,1)S(1)}, bf16[1024,256]{1,0:T(8,128)(2,1)S(1)}, u32[]{:S(2)}, u32[]{:S(2)}) collective-permute-start(bf16[1024,256]{1,0:T(8,128)(2,1)S(1)} %get-tuple-element.12), channel_id=1, source_target_pairs={{0,4},{4,8},{8,12},{12,16},{16,20},{20,24},{24,28},{28,0},{1,5},{5... | collective-permute-start | bytes 1572872 | tf_op jit(solution)/shard_map/ppermute | solution.py:283
  64.7 14.0 %collective-permute-start.2 = (bf16[1024,256]{1,0:T(8,128)(2,1)S(1)}, bf16[1024,256]{1,0:T(8,128)(2,1)S(1)}, u32[]{:S(2)}, u32[]{:S(2)}) collective-permute-start(bf16[1024,256]{1,0:T(8,128)(2,1)S(1)} %get-tuple-element.12), channel_id=1, source_target_pairs={{0,28},{4,0},{8,4},{12,8},{16,12},{20,16},{24,20},{28,24},{1,29},{... | collective-permute-start | bytes 1572872 | tf_op jit(solution)/shard_map/ppermute | solution.py:286
  68.5 14.1 %collective-permute-start.9 = (bf16[256,1024]{1,0:T(8,128)(2,1)S(1)}, bf16[256,1024]{1,0:T(8,128)(2,1)S(1)}, u32[]{:S(2)}, u32[]{:S(2)}) collective-permute-start(bf16[256,1024]{1,0:T(8,128)(2,1)S(1)} %pad_maximum_fusion.9), channel_id=1, source_target_pairs={{0,128},{128,0},{1,129},{129,1},{2,130},{130,2},{3,131},{131,3},{4... | collective-permute-start | bytes 1572872 | tf_op jit(solution)/shard_map/ppermute | solution.py:298
  69.6 13.7 %collective-permute-start.10 = (bf16[256,1024]{1,0:T(8,128)(2,1)S(1)}, bf16[256,1024]{1,0:T(8,128)(2,1)S(1)}, u32[]{:S(2)}, u32[]{:S(2)}) collective-permute-start(bf16[256,1024]{1,0:T(8,128)(2,1)S(1)} %pad_maximum_fusion.9), channel_id=1, source_target_pairs={{0,32},{32,64},{64,96},{96,0},{1,33},{33,65},{65,97},{97,1},{2,34}... | collective-permute-start | bytes 1572872 | tf_op jit(solution)/shard_map/ppermute | solution.py:299
  70.9 22.1 %collective-permute-start.11 = (bf16[256,1024]{1,0:T(8,128)(2,1)S(1)}, bf16[256,1024]{1,0:T(8,128)(2,1)S(1)}, u32[]{:S(2)}, u32[]{:S(2)}) collective-permute-start(bf16[256,1024]{1,0:T(8,128)(2,1)S(1)} %pad_maximum_fusion.9), channel_id=1, source_target_pairs={{0,96},{32,0},{64,32},{96,64},{1,97},{33,1},{65,33},{97,65},{2,98}... | collective-permute-start | bytes 1572872 | tf_op jit(solution)/shard_map/ppermute | solution.py:300
  78.7 14.3 %collective-permute-start.3 = (bf16[1024,256]{1,0:T(8,128)(2,1)S(1)}, bf16[1024,256]{1,0:T(8,128)(2,1)S(1)}, u32[]{:S(2)}, u32[]{:S(2)}) collective-permute-start(bf16[1024,256]{1,0:T(8,128)(2,1)S(1)} %collective-permute-done.1), channel_id=1, source_target_pairs={{0,4},{4,8},{8,12},{12,16},{16,20},{20,24},{24,28},{28,0},{1,5},{5... | collective-permute-start | bytes 1572872 | tf_op jit(solution)/shard_map/ppermute | solution.py:283
  78.7 14.4 %collective-permute-start.4 = (bf16[1024,256]{1,0:T(8,128)(2,1)S(1)}, bf16[1024,256]{1,0:T(8,128)(2,1)S(1)}, u32[]{:S(2)}, u32[]{:S(2)}) collective-permute-start(bf16[1024,256]{1,0:T(8,128)(2,1)S(1)} %collective-permute-done.2), channel_id=1, source_target_pairs={{0,28},{4,0},{8,4},{12,8},{16,12},{20,16},{24,20},{28,24},{1,29},{... | collective-permute-start | bytes 1572872 | tf_op jit(solution)/shard_map/ppermute | solution.py:286
  83.4 24.1 %collective-permute-start.12 = (bf16[2,256,1024]{2,1,0:T(8,128)(2,1)S(1)}, bf16[2,256,1024]{2,1,0:T(8,128)(2,1)S(1)}, u32[]{:S(2)}, u32[]{:S(2)}) collective-permute-start(bf16[2,256,1024]{2,1,0:T(8,128)(2,1)S(1)} %pad_maximum_fusion.7), channel_id=1, source_target_pairs={{0,32},{32,64},{64,96},{96,0},{1,33},{33,65},{65,97},{97,1},{2,34}... | collective-permute-start | bytes 3145736 | tf_op jit(solution)/shard_map/ppermute | solution.py:301
  84.7 12.5 %collective-permute-start.13 = (bf16[256,1024]{1,0:T(8,128)(2,1)S(1)}, bf16[256,1024]{1,0:T(8,128)(2,1)S(1)}, u32[]{:S(2)}, u32[]{:S(2)}) collective-permute-start(bf16[256,1024]{1,0:T(8,128)(2,1)S(1)} %collective-permute-done.9), channel_id=1, source_target_pairs={{0,96},{32,0},{64,32},{96,64},{1,97},{33,1},{65,33},{97,65},{2,98}... | collective-permute-start | bytes 1572872 | tf_op jit(solution)/shard_map/ppermute | solution.py:302
  93.0 13.4 %collective-permute-start.5 = (bf16[1024,256]{1,0:T(8,128)(2,1)S(1)}, bf16[1024,256]{1,0:T(8,128)(2,1)S(1)}, u32[]{:S(2)}, u32[]{:S(2)}) collective-permute-start(bf16[1024,256]{1,0:T(8,128)(2,1)S(1)} %collective-permute-done.3), channel_id=1, source_target_pairs={{0,4},{4,8},{8,12},{12,16},{16,20},{20,24},{24,28},{28,0},{1,5},{5... | collective-permute-start | bytes 1572872 | tf_op jit(solution)/shard_map/ppermute | solution.py:283
  93.0 13.4 %collective-permute-start.6 = (bf16[1024,256]{1,0:T(8,128)(2,1)S(1)}, bf16[1024,256]{1,0:T(8,128)(2,1)S(1)}, u32[]{:S(2)}, u32[]{:S(2)}) collective-permute-start(bf16[1024,256]{1,0:T(8,128)(2,1)S(1)} %collective-permute-done.4), channel_id=1, source_target_pairs={{0,28},{4,0},{8,4},{12,8},{16,12},{20,16},{24,20},{28,24},{1,29},{... | collective-permute-start | bytes 1572872 | tf_op jit(solution)/shard_map/ppermute | solution.py:286
  97.3 11.6 %collective-permute-start.14 = (bf16[256,1024]{1,0:T(8,128)(2,1)S(1)}, bf16[256,1024]{1,0:T(8,128)(2,1)S(1)}, u32[]{:S(2)}, u32[]{:S(2)}) collective-permute-start(bf16[256,1024]{1,0:T(8,128)(2,1)S(1)} %collective-permute-done.13), channel_id=1, source_target_pairs={{0,96},{32,0},{64,32},{96,64},{1,97},{33,1},{65,33},{97,65},{2,98}... | collective-permute-start | bytes 1572872 | tf_op jit(solution)/shard_map/ppermute | solution.py:303
  106.4 12.5 %collective-permute-start.7 = (bf16[1024,256]{1,0:T(8,128)(2,1)S(1)}, bf16[1024,256]{1,0:T(8,128)(2,1)S(1)}, u32[]{:S(2)}, u32[]{:S(2)}) collective-permute-start(bf16[1024,256]{1,0:T(8,128)(2,1)S(1)} %collective-permute-done.5), channel_id=1, source_target_pairs={{0,4},{4,8},{8,12},{12,16},{16,20},{20,24},{24,28},{28,0},{1,5},{5... | collective-permute-start | bytes 1572872 | tf_op jit(solution)/shard_map/ppermute | solution.py:283
  143.4 10.5 %collective-permute-start.25 = (bf16[512,256]{1,0:T(8,128)(2,1)S(1)}, bf16[512,256]{1,0:T(8,128)(2,1)S(1)}, u32[]{:S(2)}, u32[]{:S(2)}) collective-permute-start(bf16[512,256]{1,0:T(8,128)(2,1)S(1)} %get-tuple-element.20), channel_id=1, source_target_pairs={{0,4},{4,8},{8,12},{12,16},{16,20},{20,24},{24,28},{28,0},{1,5},{5... | collective-permute-start | bytes 786440 | tf_op jit(solution)/shard_map/ppermute | solution.py:283
  143.5 10.5 %collective-permute-start.26 = (bf16[512,256]{1,0:T(8,128)(2,1)S(1)}, bf16[512,256]{1,0:T(8,128)(2,1)S(1)}, u32[]{:S(2)}, u32[]{:S(2)}) collective-permute-start(bf16[512,256]{1,0:T(8,128)(2,1)S(1)} %get-tuple-element.20), channel_id=1, source_target_pairs={{0,28},{4,0},{8,4},{12,8},{16,12},{20,16},{24,20},{28,24},{1,29},{... | collective-permute-start | bytes 786440 | tf_op jit(solution)/shard_map/ppermute | solution.py:286
  146.7 12.8 %collective-permute-start.20 = (bf16[512,256]{1,0:T(8,128)(2,1)S(1)}, bf16[512,256]{1,0:T(8,128)(2,1)S(1)}, u32[]{:S(2)}, u32[]{:S(2)}) collective-permute-start(bf16[512,256]{1,0:T(8,128)(2,1)S(1)} %collective-permute-done.18), channel_id=1, source_target_pairs={{0,4},{4,8},{8,12},{12,16},{16,20},{20,24},{24,28},{28,0},{1,5},{5... | collective-permute-start | bytes 786440 | tf_op jit(solution)/shard_map/ppermute | solution.py:283
  146.7 12.8 %collective-permute-start.21 = (bf16[512,256]{1,0:T(8,128)(2,1)S(1)}, bf16[512,256]{1,0:T(8,128)(2,1)S(1)}, u32[]{:S(2)}, u32[]{:S(2)}) collective-permute-start(bf16[512,256]{1,0:T(8,128)(2,1)S(1)} %collective-permute-done.19), channel_id=1, source_target_pairs={{0,28},{4,0},{8,4},{12,8},{16,12},{20,16},{24,20},{28,24},{1,29},{... | collective-permute-start | bytes 786440 | tf_op jit(solution)/shard_map/ppermute | solution.py:286
  153.9 11.2 %collective-permute-start.27 = (bf16[512,256]{1,0:T(8,128)(2,1)S(1)}, bf16[512,256]{1,0:T(8,128)(2,1)S(1)}, u32[]{:S(2)}, u32[]{:S(2)}) collective-permute-start(bf16[512,256]{1,0:T(8,128)(2,1)S(1)} %collective-permute-done.25), channel_id=1, source_target_pairs={{0,4},{4,8},{8,12},{12,16},{16,20},{20,24},{24,28},{28,0},{1,5},{5... | collective-permute-start | bytes 786440 | tf_op jit(solution)/shard_map/ppermute | solution.py:283
  154.0 11.2 %collective-permute-start.28 = (bf16[512,256]{1,0:T(8,128)(2,1)S(1)}, bf16[512,256]{1,0:T(8,128)(2,1)S(1)}, u32[]{:S(2)}, u32[]{:S(2)}) collective-permute-start(bf16[512,256]{1,0:T(8,128)(2,1)S(1)} %collective-permute-done.26), channel_id=1, source_target_pairs={{0,28},{4,0},{8,4},{12,8},{16,12},{20,16},{24,20},{28,24},{1,29},{... | collective-permute-start | bytes 786440 | tf_op jit(solution)/shard_map/ppermute | solution.py:286
  159.5 11.2 %collective-permute-start.22 = (bf16[512,256]{1,0:T(8,128)(2,1)S(1)}, bf16[512,256]{1,0:T(8,128)(2,1)S(1)}, u32[]{:S(2)}, u32[]{:S(2)}) collective-permute-start(bf16[512,256]{1,0:T(8,128)(2,1)S(1)} %collective-permute-done.20), channel_id=1, source_target_pairs={{0,4},{4,8},{8,12},{12,16},{16,20},{20,24},{24,28},{28,0},{1,5},{5... | collective-permute-start | bytes 786440 | tf_op jit(solution)/shard_map/ppermute | solution.py:283
  159.6 11.2 %collective-permute-start.23 = (bf16[512,256]{1,0:T(8,128)(2,1)S(1)}, bf16[512,256]{1,0:T(8,128)(2,1)S(1)}, u32[]{:S(2)}, u32[]{:S(2)}) collective-permute-start(bf16[512,256]{1,0:T(8,128)(2,1)S(1)} %collective-permute-done.21), channel_id=1, source_target_pairs={{0,28},{4,0},{8,4},{12,8},{16,12},{20,16},{24,20},{28,24},{1,29},{... | collective-permute-start | bytes 786440 | tf_op jit(solution)/shard_map/ppermute | solution.py:286
  165.2 11.7 %collective-permute-start.29 = (bf16[512,256]{1,0:T(8,128)(2,1)S(1)}, bf16[512,256]{1,0:T(8,128)(2,1)S(1)}, u32[]{:S(2)}, u32[]{:S(2)}) collective-permute-start(bf16[512,256]{1,0:T(8,128)(2,1)S(1)} %collective-permute-done.27), channel_id=1, source_target_pairs={{0,4},{4,8},{8,12},{12,16},{16,20},{20,24},{24,28},{28,0},{1,5},{5... | collective-permute-start | bytes 786440 | tf_op jit(solution)/shard_map/ppermute | solution.py:283
  186.0 15.6 %collective-permute-start.33 = (bf16[1024,256]{1,0:T(8,128)(2,1)S(1)}, bf16[1024,256]{1,0:T(8,128)(2,1)S(1)}, u32[]{:S(2)}, u32[]{:S(2)}) collective-permute-start(bf16[1024,256]{1,0:T(8,128)(2,1)S(1)} %fusion.18), channel_id=1, source_target_pairs={{0,1},{1,0},{2,3},{3,2},{4,5},{5,4},{6,7},{7,6},{8,9},{9,8},{10,11... | collective-permute-start | bytes 1572872 | tf_op jit(solution)/shard_map/ppermute | solution.py:329
  (17 other events, 115.3 us)

commit v8 on v7

--- a/solution.py
+++ b/solution.py
@@ -214,7 +214,6 @@
         in_specs=[SMEM, SMEM, VMEM, VMEM, VMEM],
         out_specs=VMEM,
         scratch_shapes=[pltpu.SMEM((tasks,), jnp.int32), pltpu.SMEM((2 * tasks,), jnp.int32)],
-        compiler_params=pltpu.CompilerParams(vmem_limit_bytes=12 * 2**20),
         name="contribute",
     )(owner, block, left, right, weight)
 

time: 203 us -> 201 us (level)
  local copies, waits for them, and re-layouts: 8.19 us -> 3.6 us
    unnamed x34 -> x24, local copies, waits for them, and re-layouts: 6.73 us -> 2.14 us
where the time goes in v8:
time: 201 us; the launch traced here: 200 us
  waiting for transfers between devices  81.7 us (41%)
  starting transfers between devices  52.1 us (26%)
  blocking collectives  32.6 us (16%)
  Pallas kernels  17.8 us (9%)
  matrix products  9.3 us (5%)
  local copies, waits for them, and re-layouts  3.6 us (2%)
  other arithmetic  2.2 us (1%)
    ppermute x11, waiting for transfers between devices, gather_z(): up = lax.ppermute(up, 'z', ring_of(8, 1))  44.8 us
    all_to_all x1, blocking collectives, local(): lax.all_to_all(outgoing, AXES[:4], split_axis=0, concat_axis=0, tiled=True)  32.6 us
    ppermute x10, starting transfers between devices, gather_z(): down = lax.ppermute(down, 'z', ring_of(8, -1))  32.2 us
    ppermute x3, waiting for transfers between devices, product(): away = lax.ppermute(part, 'yhi', SWAP)  22.4 us
    dot_general x4, matrix products, dot(): return jnp.einsum('dmk,dkn->mn', a, b, preferred_element_type=jnp.float32)  9.3 us
    ppermute x3, starting transfers between devices, product(): away = lax.ppermute(part, 'yhi', SWAP)  8.8 us
    pallas_call x1, Pallas kernels, collect(): pl.pallas_call(collect_kernel, out_shape=(jax.ShapeDtypeStruct((1024, 512...  7.15 us
    pallas_call x1, Pallas kernels, contribute(): pl.pallas_call(contribute_kernel, out_shape=jax.ShapeDtypeStruct((tasks,...  5.48 us
  transfers between devices with their start and end apart: 34, of which 23 were waited for; matrix products, arithmetic and copies ran while one was open for 3% of the time, Pallas kernels for 4%

profile of v8, /device:TPU:2, one launch (start us, length us, event | category | flops | bytes accessed | tf_op | source)
XLA Modules:
  0.0 200.3 jit_solution(16576093014741763683)
XLA Ops:
  0.6 5.5 %contribute.1 = bf16[128,9,2,128]{3,2,1,0:T(2,128)(2,1)} custom-call(s32[128]{0:T(128)} %bitcast.81, s32[128]{0:T(128)} %block_ref.1, bf16[128,32,128]{2,1,0:T(8,128)(2,1)} %left_ref.1, bf16[128,32,128]{2,1,0:T(8,128)(2,1)} %right_ref.1, f32[128,128]{1,0:T(8,128)} %weight_ref.1), custom_call_target="tpu_custom_call" | custom-call | tf_op jit(solution)/shard_map/contribute/pallas_call | solution.py:211
  6.1 32.6 %all_to_all.5 = bf16[128,9,2,128]{3,2,1,0:T(2,128)(2,1)S(1)} all-to-all(bf16[128,9,2,128]{3,2,1,0:T(2,128)(2,1)} %contribute.1), channel_id=1, replica_groups=mesh['ylo'=2,'x'=4,'z'=8,'core'=2,'yhi'=2] {'ylo','x','z','core'}, dimensions={0} | all-to-all | bytes 1179648 | tf_op jit(solution)/shard_map/all_to_all | solution.py:338
  39.4 3.0 %collective-permute-start = (bf16[257,8,128]{2,1,0:T(8,128)(2,1)S(1)}, bf16[257,8,128]{2,1,0:T(8,128)(2,1)S(1)}, u32[]{:S(2)}, u32[]{:S(2)}) collective-permute-start(bf16[257,8,128]{2,1,0:T(8,128)(2,1)S(1)} %pad_maximum_fusion.8.slot_ref), channel_id=1, source_target_pairs={{0,1},{1,0},{2,3},{3,2},{4,5},{5,4},{6,7},{7,6},{8,9},{9,8},{10,11... | collective-permute-start | bytes 1579016 | tf_op jit(solution)/shard_map/ppermute | solution.py:345
  44.0 7.1 %collect.1 = (f32[1024,512]{1,0:T(8,128)S(1)}, bf16[1024,512]{1,0:T(8,128)(2,1)S(1)}) custom-call(s32[32,16]{1,0:T(8,128)S(1)} %copy.10.mask_ref, bf16[257,8,128]{2,1,0:T(8,128)(2,1)S(1)} %pad_maximum_fusion.8.slot_ref, f32[1024,512]{1,0:T(8,128)S(1)} %copy-done), custom_call_target="tpu_custom_call" | custom-call | flops 1048576 | bytes 8388608 | tf_op jit(solution)/shard_map/collect/pallas_call | solution.py:230
  51.2 4.5 %collective-permute-done.far_ref = bf16[257,8,128]{2,1,0:T(8,128)(2,1)S(1)} collective-permute-done((bf16[257,8,128]{2,1,0:T(8,128)(2,1)S(1)}, bf16[257,8,128]{2,1,0:T(8,128)(2,1)S(1)}, u32[]{:S(2)}, u32[]{:S(2)}) %collective-permute-start) | collective-permute-done | bytes 526368 | tf_op jit(solution)/shard_map/ppermute | solution.py:345
  55.7 5.1 %assemble.1 = (f32[1024,256]{1,0:T(8,128)}, bf16[1024,256]{1,0:T(8,128)(2,1)S(1)}, bf16[3,256,512]{2,1,0:T(8,128)(2,1)S(1)}) custom-call(bf16[257,8,128]{2,1,0:T(8,128)(2,1)S(1)} %collective-permute-done.far_ref, f32[1024,512]{1,0:T(8,128)S(1)} %get-tuple-element.9.base_ref, bf16[1024,512]{1,0:T(8,128)(2,1)S(1)} %get-tuple-element.10.pattern_ref), custom_call_target="tpu_custom_call" | custom-call | tf_op jit(solution)/shard_map/assemble/pallas_call | solution.py:249
  69.6 6.5 %collective-permute-done.1 = bf16[1024,256]{1,0:T(8,128)(2,1)S(1)} collective-permute-done((bf16[1024,256]{1,0:T(8,128)(2,1)S(1)}, bf16[1024,256]{1,0:T(8,128)(2,1)S(1)}, u32[]{:S(2)}, u32[]{:S(2)}) %collective-permute-start.1) | collective-permute-done | bytes 524320 | tf_op jit(solution)/shard_map/ppermute | solution.py:282
  76.1 3.2 %collective-permute-start.4 = (bf16[1024,256]{1,0:T(8,128)(2,1)S(1)}, bf16[1024,256]{1,0:T(8,128)(2,1)S(1)}, u32[]{:S(2)}, u32[]{:S(2)}) collective-permute-start(bf16[1024,256]{1,0:T(8,128)(2,1)S(1)} %collective-permute-done.2), channel_id=1, source_target_pairs={{0,28},{4,0},{8,4},{12,8},{16,12},{20,16},{24,20},{28,24},{1,29},{... | collective-permute-start | bytes 1572872 | tf_op jit(solution)/shard_map/ppermute | solution.py:285
  83.0 7.4 %collective-permute-done.3 = bf16[1024,256]{1,0:T(8,128)(2,1)S(1)} collective-permute-done((bf16[1024,256]{1,0:T(8,128)(2,1)S(1)}, bf16[1024,256]{1,0:T(8,128)(2,1)S(1)}, u32[]{:S(2)}, u32[]{:S(2)}) %collective-permute-start.3) | collective-permute-done | bytes 524320 | tf_op jit(solution)/shard_map/ppermute | solution.py:282
  90.4 3.3 %collective-permute-start.6 = (bf16[1024,256]{1,0:T(8,128)(2,1)S(1)}, bf16[1024,256]{1,0:T(8,128)(2,1)S(1)}, u32[]{:S(2)}, u32[]{:S(2)}) collective-permute-start(bf16[1024,256]{1,0:T(8,128)(2,1)S(1)} %collective-permute-done.4), channel_id=1, source_target_pairs={{0,28},{4,0},{8,4},{12,8},{16,12},{20,16},{24,20},{28,24},{1,29},{... | collective-permute-start | bytes 1572872 | tf_op jit(solution)/shard_map/ppermute | solution.py:285
  95.8 8.0 %collective-permute-done.5 = bf16[1024,256]{1,0:T(8,128)(2,1)S(1)} collective-permute-done((bf16[1024,256]{1,0:T(8,128)(2,1)S(1)}, bf16[1024,256]{1,0:T(8,128)(2,1)S(1)}, u32[]{:S(2)}, u32[]{:S(2)}) %collective-permute-start.5) | collective-permute-done | bytes 524320 | tf_op jit(solution)/shard_map/ppermute | solution.py:282
  106.3 9.9 %collective-permute-done.7 = bf16[1024,256]{1,0:T(8,128)(2,1)S(1)} collective-permute-done((bf16[1024,256]{1,0:T(8,128)(2,1)S(1)}, bf16[1024,256]{1,0:T(8,128)(2,1)S(1)}, u32[]{:S(2)}, u32[]{:S(2)}) %collective-permute-start.7) | collective-permute-done | bytes 524320 | tf_op jit(solution)/shard_map/ppermute | solution.py:282
  121.6 3.0 %collective-permute-start.16 = (bf16[512,256]{1,0:T(8,128)(2,1)S(1)}, bf16[512,256]{1,0:T(8,128)(2,1)S(1)}, u32[]{:S(2)}, u32[]{:S(2)}) collective-permute-start(bf16[512,256]{1,0:T(8,128)(2,1)S(1)} %get-tuple-element.22), channel_id=1, source_target_pairs={{0,1},{1,0},{2,3},{3,2},{4,5},{5,4},{6,7},{7,6},{8,9},{9,8},{10,11... | collective-permute-start | bytes 786440 | tf_op jit(solution)/shard_map/ppermute | solution.py:328
  124.6 7.0 %collective-permute-done.16 = bf16[512,256]{1,0:T(8,128)(2,1)S(1)} collective-permute-done((bf16[512,256]{1,0:T(8,128)(2,1)S(1)}, bf16[512,256]{1,0:T(8,128)(2,1)S(1)}, u32[]{:S(2)}, u32[]{:S(2)}) %collective-permute-start.16) | collective-permute-done | bytes 262176 | tf_op jit(solution)/shard_map/ppermute | solution.py:328
  134.7 3.2 %collective-permute-start.19 = (bf16[512,256]{1,0:T(8,128)(2,1)S(1)}, bf16[512,256]{1,0:T(8,128)(2,1)S(1)}, u32[]{:S(2)}, u32[]{:S(2)}) collective-permute-start(bf16[512,256]{1,0:T(8,128)(2,1)S(1)} %get-tuple-element.17), channel_id=1, source_target_pairs={{0,28},{4,0},{8,4},{12,8},{16,12},{20,16},{24,20},{28,24},{1,29},{... | collective-permute-start | bytes 786440 | tf_op jit(solution)/shard_map/ppermute | solution.py:285
  140.9 3.2 %collective-permute-start.26 = (bf16[512,256]{1,0:T(8,128)(2,1)S(1)}, bf16[512,256]{1,0:T(8,128)(2,1)S(1)}, u32[]{:S(2)}, u32[]{:S(2)}) collective-permute-start(bf16[512,256]{1,0:T(8,128)(2,1)S(1)} %get-tuple-element.20), channel_id=1, source_target_pairs={{0,28},{4,0},{8,4},{12,8},{16,12},{20,16},{24,20},{28,24},{1,29},{... | collective-permute-start | bytes 786440 | tf_op jit(solution)/shard_map/ppermute | solution.py:285
  144.1 3.5 %collective-permute-start.21 = (bf16[512,256]{1,0:T(8,128)(2,1)S(1)}, bf16[512,256]{1,0:T(8,128)(2,1)S(1)}, u32[]{:S(2)}, u32[]{:S(2)}) collective-permute-start(bf16[512,256]{1,0:T(8,128)(2,1)S(1)} %collective-permute-done.19), channel_id=1, source_target_pairs={{0,28},{4,0},{8,4},{12,8},{16,12},{20,16},{24,20},{28,24},{1,29},{... | collective-permute-start | bytes 786440 | tf_op jit(solution)/shard_map/ppermute | solution.py:285
  147.7 3.6 %collective-permute-done.25 = bf16[512,256]{1,0:T(8,128)(2,1)S(1)} collective-permute-done((bf16[512,256]{1,0:T(8,128)(2,1)S(1)}, bf16[512,256]{1,0:T(8,128)(2,1)S(1)}, u32[]{:S(2)}, u32[]{:S(2)}) %collective-permute-start.25) | collective-permute-done | bytes 262176 | tf_op jit(solution)/shard_map/ppermute | solution.py:282
  151.4 3.3 %collective-permute-start.28 = (bf16[512,256]{1,0:T(8,128)(2,1)S(1)}, bf16[512,256]{1,0:T(8,128)(2,1)S(1)}, u32[]{:S(2)}, u32[]{:S(2)}) collective-permute-start(bf16[512,256]{1,0:T(8,128)(2,1)S(1)} %collective-permute-done.26), channel_id=1, source_target_pairs={{0,28},{4,0},{8,4},{12,8},{16,12},{20,16},{24,20},{28,24},{1,29},{... | collective-permute-start | bytes 786440 | tf_op jit(solution)/shard_map/ppermute | solution.py:285
  157.0 3.3 %collective-permute-start.23 = (bf16[512,256]{1,0:T(8,128)(2,1)S(1)}, bf16[512,256]{1,0:T(8,128)(2,1)S(1)}, u32[]{:S(2)}, u32[]{:S(2)}) collective-permute-start(bf16[512,256]{1,0:T(8,128)(2,1)S(1)} %collective-permute-done.21), channel_id=1, source_target_pairs={{0,28},{4,0},{8,4},{12,8},{16,12},{20,16},{24,20},{28,24},{1,29},{... | collective-permute-start | bytes 786440 | tf_op jit(solution)/shard_map/ppermute | solution.py:285
  162.6 3.3 %collective-permute-start.30 = (bf16[512,256]{1,0:T(8,128)(2,1)S(1)}, bf16[512,256]{1,0:T(8,128)(2,1)S(1)}, u32[]{:S(2)}, u32[]{:S(2)}) collective-permute-start(bf16[512,256]{1,0:T(8,128)(2,1)S(1)} %collective-permute-done.28), channel_id=1, source_target_pairs={{0,28},{4,0},{8,4},{12,8},{16,12},{20,16},{24,20},{28,24},{1,29},{... | collective-permute-start | bytes 786440 | tf_op jit(solution)/shard_map/ppermute | solution.py:285
  170.5 3.7 %collective-permute-start.31 = (bf16[512,256]{1,0:T(8,128)(2,1)S(1)}, bf16[512,256]{1,0:T(8,128)(2,1)S(1)}, u32[]{:S(2)}, u32[]{:S(2)}) collective-permute-start(bf16[512,256]{1,0:T(8,128)(2,1)S(1)} %collective-permute-done.30), channel_id=1, source_target_pairs={{0,28},{4,0},{8,4},{12,8},{16,12},{20,16},{24,20},{28,24},{1,29},{... | collective-permute-start | bytes 786440 | tf_op jit(solution)/shard_map/ppermute | solution.py:285
  183.4 2.9 %collective-permute-start.33 = (bf16[1024,256]{1,0:T(8,128)(2,1)S(1)}, bf16[1024,256]{1,0:T(8,128)(2,1)S(1)}, u32[]{:S(2)}, u32[]{:S(2)}) collective-permute-start(bf16[1024,256]{1,0:T(8,128)(2,1)S(1)} %fusion.18), channel_id=1, source_target_pairs={{0,1},{1,0},{2,3},{3,2},{4,5},{5,4},{6,7},{7,6},{8,9},{9,8},{10,11... | collective-permute-start | bytes 1572872 | tf_op jit(solution)/shard_map/ppermute | solution.py:328
  186.3 12.7 %collective-permute-done.33 = bf16[1024,256]{1,0:T(8,128)(2,1)S(1)} collective-permute-done((bf16[1024,256]{1,0:T(8,128)(2,1)S(1)}, bf16[1024,256]{1,0:T(8,128)(2,1)S(1)}, u32[]{:S(2)}, u32[]{:S(2)}) %collective-permute-start.33) | collective-permute-done | bytes 524320 | tf_op jit(solution)/shard_map/ppermute | solution.py:328
  (101 shorter events, 50.2 us)
Async XLA Ops:
  39.4 16.3 %collective-permute-start = (bf16[257,8,128]{2,1,0:T(8,128)(2,1)S(1)}, bf16[257,8,128]{2,1,0:T(8,128)(2,1)S(1)}, u32[]{:S(2)}, u32[]{:S(2)}) collective-permute-start(bf16[257,8,128]{2,1,0:T(8,128)(2,1)S(1)} %pad_maximum_fusion.8.slot_ref), channel_id=1, source_target_pairs={{0,1},{1,0},{2,3},{3,2},{4,5},{5,4},{6,7},{7,6},{8,9},{9,8},{10,11... | collective-permute-start | bytes 1579016 | tf_op jit(solution)/shard_map/ppermute | solution.py:345
  60.8 15.2 %collective-permute-start.1 = (bf16[1024,256]{1,0:T(8,128)(2,1)S(1)}, bf16[1024,256]{1,0:T(8,128)(2,1)S(1)}, u32[]{:S(2)}, u32[]{:S(2)}) collective-permute-start(bf16[1024,256]{1,0:T(8,128)(2,1)S(1)} %get-tuple-element.12), channel_id=1, source_target_pairs={{0,4},{4,8},{8,12},{12,16},{16,20},{20,24},{24,28},{28,0},{1,5},{5... | collective-permute-start | bytes 1572872 | tf_op jit(solution)/shard_map/ppermute | solution.py:282
  62.1 14.0 %collective-permute-start.2 = (bf16[1024,256]{1,0:T(8,128)(2,1)S(1)}, bf16[1024,256]{1,0:T(8,128)(2,1)S(1)}, u32[]{:S(2)}, u32[]{:S(2)}) collective-permute-start(bf16[1024,256]{1,0:T(8,128)(2,1)S(1)} %get-tuple-element.12), channel_id=1, source_target_pairs={{0,28},{4,0},{8,4},{12,8},{16,12},{20,16},{24,20},{28,24},{1,29},{... | collective-permute-start | bytes 1572872 | tf_op jit(solution)/shard_map/ppermute | solution.py:285
  65.9 14.1 %collective-permute-start.9 = (bf16[256,1024]{1,0:T(8,128)(2,1)S(1)}, bf16[256,1024]{1,0:T(8,128)(2,1)S(1)}, u32[]{:S(2)}, u32[]{:S(2)}) collective-permute-start(bf16[256,1024]{1,0:T(8,128)(2,1)S(1)} %pad_maximum_fusion.9), channel_id=1, source_target_pairs={{0,128},{128,0},{1,129},{129,1},{2,130},{130,2},{3,131},{131,3},{4... | collective-permute-start | bytes 1572872 | tf_op jit(solution)/shard_map/ppermute | solution.py:297
  67.0 13.7 %collective-permute-start.10 = (bf16[256,1024]{1,0:T(8,128)(2,1)S(1)}, bf16[256,1024]{1,0:T(8,128)(2,1)S(1)}, u32[]{:S(2)}, u32[]{:S(2)}) collective-permute-start(bf16[256,1024]{1,0:T(8,128)(2,1)S(1)} %pad_maximum_fusion.9), channel_id=1, source_target_pairs={{0,32},{32,64},{64,96},{96,0},{1,33},{33,65},{65,97},{97,1},{2,34}... | collective-permute-start | bytes 1572872 | tf_op jit(solution)/shard_map/ppermute | solution.py:298
  68.3 22.1 %collective-permute-start.11 = (bf16[256,1024]{1,0:T(8,128)(2,1)S(1)}, bf16[256,1024]{1,0:T(8,128)(2,1)S(1)}, u32[]{:S(2)}, u32[]{:S(2)}) collective-permute-start(bf16[256,1024]{1,0:T(8,128)(2,1)S(1)} %pad_maximum_fusion.9), channel_id=1, source_target_pairs={{0,96},{32,0},{64,32},{96,64},{1,97},{33,1},{65,33},{97,65},{2,98}... | collective-permute-start | bytes 1572872 | tf_op jit(solution)/shard_map/ppermute | solution.py:299
  76.1 14.3 %collective-permute-start.3 = (bf16[1024,256]{1,0:T(8,128)(2,1)S(1)}, bf16[1024,256]{1,0:T(8,128)(2,1)S(1)}, u32[]{:S(2)}, u32[]{:S(2)}) collective-permute-start(bf16[1024,256]{1,0:T(8,128)(2,1)S(1)} %collective-permute-done.1), channel_id=1, source_target_pairs={{0,4},{4,8},{8,12},{12,16},{16,20},{20,24},{24,28},{28,0},{1,5},{5... | collective-permute-start | bytes 1572872 | tf_op jit(solution)/shard_map/ppermute | solution.py:282
  76.1 14.4 %collective-permute-start.4 = (bf16[1024,256]{1,0:T(8,128)(2,1)S(1)}, bf16[1024,256]{1,0:T(8,128)(2,1)S(1)}, u32[]{:S(2)}, u32[]{:S(2)}) collective-permute-start(bf16[1024,256]{1,0:T(8,128)(2,1)S(1)} %collective-permute-done.2), channel_id=1, source_target_pairs={{0,28},{4,0},{8,4},{12,8},{16,12},{20,16},{24,20},{28,24},{1,29},{... | collective-permute-start | bytes 1572872 | tf_op jit(solution)/shard_map/ppermute | solution.py:285
  80.8 24.1 %collective-permute-start.12 = (bf16[2,256,1024]{2,1,0:T(8,128)(2,1)S(1)}, bf16[2,256,1024]{2,1,0:T(8,128)(2,1)S(1)}, u32[]{:S(2)}, u32[]{:S(2)}) collective-permute-start(bf16[2,256,1024]{2,1,0:T(8,128)(2,1)S(1)} %pad_maximum_fusion.7), channel_id=1, source_target_pairs={{0,32},{32,64},{64,96},{96,0},{1,33},{33,65},{65,97},{97,1},{2,34}... | collective-permute-start | bytes 3145736 | tf_op jit(solution)/shard_map/ppermute | solution.py:300
  82.1 12.5 %collective-permute-start.13 = (bf16[256,1024]{1,0:T(8,128)(2,1)S(1)}, bf16[256,1024]{1,0:T(8,128)(2,1)S(1)}, u32[]{:S(2)}, u32[]{:S(2)}) collective-permute-start(bf16[256,1024]{1,0:T(8,128)(2,1)S(1)} %collective-permute-done.9), channel_id=1, source_target_pairs={{0,96},{32,0},{64,32},{96,64},{1,97},{33,1},{65,33},{97,65},{2,98}... | collective-permute-start | bytes 1572872 | tf_op jit(solution)/shard_map/ppermute | solution.py:301
  90.4 13.4 %collective-permute-start.5 = (bf16[1024,256]{1,0:T(8,128)(2,1)S(1)}, bf16[1024,256]{1,0:T(8,128)(2,1)S(1)}, u32[]{:S(2)}, u32[]{:S(2)}) collective-permute-start(bf16[1024,256]{1,0:T(8,128)(2,1)S(1)} %collective-permute-done.3), channel_id=1, source_target_pairs={{0,4},{4,8},{8,12},{12,16},{16,20},{20,24},{24,28},{28,0},{1,5},{5... | collective-permute-start | bytes 1572872 | tf_op jit(solution)/shard_map/ppermute | solution.py:282
  90.4 13.4 %collective-permute-start.6 = (bf16[1024,256]{1,0:T(8,128)(2,1)S(1)}, bf16[1024,256]{1,0:T(8,128)(2,1)S(1)}, u32[]{:S(2)}, u32[]{:S(2)}) collective-permute-start(bf16[1024,256]{1,0:T(8,128)(2,1)S(1)} %collective-permute-done.4), channel_id=1, source_target_pairs={{0,28},{4,0},{8,4},{12,8},{16,12},{20,16},{24,20},{28,24},{1,29},{... | collective-permute-start | bytes 1572872 | tf_op jit(solution)/shard_map/ppermute | solution.py:285
  94.7 11.6 %collective-permute-start.14 = (bf16[256,1024]{1,0:T(8,128)(2,1)S(1)}, bf16[256,1024]{1,0:T(8,128)(2,1)S(1)}, u32[]{:S(2)}, u32[]{:S(2)}) collective-permute-start(bf16[256,1024]{1,0:T(8,128)(2,1)S(1)} %collective-permute-done.13), channel_id=1, source_target_pairs={{0,96},{32,0},{64,32},{96,64},{1,97},{33,1},{65,33},{97,65},{2,98}... | collective-permute-start | bytes 1572872 | tf_op jit(solution)/shard_map/ppermute | solution.py:302
  103.8 12.5 %collective-permute-start.7 = (bf16[1024,256]{1,0:T(8,128)(2,1)S(1)}, bf16[1024,256]{1,0:T(8,128)(2,1)S(1)}, u32[]{:S(2)}, u32[]{:S(2)}) collective-permute-start(bf16[1024,256]{1,0:T(8,128)(2,1)S(1)} %collective-permute-done.5), channel_id=1, source_target_pairs={{0,4},{4,8},{8,12},{12,16},{16,20},{20,24},{24,28},{28,0},{1,5},{5... | collective-permute-start | bytes 1572872 | tf_op jit(solution)/shard_map/ppermute | solution.py:282
  140.8 10.5 %collective-permute-start.25 = (bf16[512,256]{1,0:T(8,128)(2,1)S(1)}, bf16[512,256]{1,0:T(8,128)(2,1)S(1)}, u32[]{:S(2)}, u32[]{:S(2)}) collective-permute-start(bf16[512,256]{1,0:T(8,128)(2,1)S(1)} %get-tuple-element.20), channel_id=1, source_target_pairs={{0,4},{4,8},{8,12},{12,16},{16,20},{20,24},{24,28},{28,0},{1,5},{5... | collective-permute-start | bytes 786440 | tf_op jit(solution)/shard_map/ppermute | solution.py:282
  140.9 10.5 %collective-permute-start.26 = (bf16[512,256]{1,0:T(8,128)(2,1)S(1)}, bf16[512,256]{1,0:T(8,128)(2,1)S(1)}, u32[]{:S(2)}, u32[]{:S(2)}) collective-permute-start(bf16[512,256]{1,0:T(8,128)(2,1)S(1)} %get-tuple-element.20), channel_id=1, source_target_pairs={{0,28},{4,0},{8,4},{12,8},{16,12},{20,16},{24,20},{28,24},{1,29},{... | collective-permute-start | bytes 786440 | tf_op jit(solution)/shard_map/ppermute | solution.py:285
  144.1 12.8 %collective-permute-start.20 = (bf16[512,256]{1,0:T(8,128)(2,1)S(1)}, bf16[512,256]{1,0:T(8,128)(2,1)S(1)}, u32[]{:S(2)}, u32[]{:S(2)}) collective-permute-start(bf16[512,256]{1,0:T(8,128)(2,1)S(1)} %collective-permute-done.18), channel_id=1, source_target_pairs={{0,4},{4,8},{8,12},{12,16},{16,20},{20,24},{24,28},{28,0},{1,5},{5... | collective-permute-start | bytes 786440 | tf_op jit(solution)/shard_map/ppermute | solution.py:282
  144.1 12.8 %collective-permute-start.21 = (bf16[512,256]{1,0:T(8,128)(2,1)S(1)}, bf16[512,256]{1,0:T(8,128)(2,1)S(1)}, u32[]{:S(2)}, u32[]{:S(2)}) collective-permute-start(bf16[512,256]{1,0:T(8,128)(2,1)S(1)} %collective-permute-done.19), channel_id=1, source_target_pairs={{0,28},{4,0},{8,4},{12,8},{16,12},{20,16},{24,20},{28,24},{1,29},{... | collective-permute-start | bytes 786440 | tf_op jit(solution)/shard_map/ppermute | solution.py:285
  151.3 11.2 %collective-permute-start.27 = (bf16[512,256]{1,0:T(8,128)(2,1)S(1)}, bf16[512,256]{1,0:T(8,128)(2,1)S(1)}, u32[]{:S(2)}, u32[]{:S(2)}) collective-permute-start(bf16[512,256]{1,0:T(8,128)(2,1)S(1)} %collective-permute-done.25), channel_id=1, source_target_pairs={{0,4},{4,8},{8,12},{12,16},{16,20},{20,24},{24,28},{28,0},{1,5},{5... | collective-permute-start | bytes 786440 | tf_op jit(solution)/shard_map/ppermute | solution.py:282
  151.4 11.2 %collective-permute-start.28 = (bf16[512,256]{1,0:T(8,128)(2,1)S(1)}, bf16[512,256]{1,0:T(8,128)(2,1)S(1)}, u32[]{:S(2)}, u32[]{:S(2)}) collective-permute-start(bf16[512,256]{1,0:T(8,128)(2,1)S(1)} %collective-permute-done.26), channel_id=1, source_target_pairs={{0,28},{4,0},{8,4},{12,8},{16,12},{20,16},{24,20},{28,24},{1,29},{... | collective-permute-start | bytes 786440 | tf_op jit(solution)/shard_map/ppermute | solution.py:285
  156.9 11.2 %collective-permute-start.22 = (bf16[512,256]{1,0:T(8,128)(2,1)S(1)}, bf16[512,256]{1,0:T(8,128)(2,1)S(1)}, u32[]{:S(2)}, u32[]{:S(2)}) collective-permute-start(bf16[512,256]{1,0:T(8,128)(2,1)S(1)} %collective-permute-done.20), channel_id=1, source_target_pairs={{0,4},{4,8},{8,12},{12,16},{16,20},{20,24},{24,28},{28,0},{1,5},{5... | collective-permute-start | bytes 786440 | tf_op jit(solution)/shard_map/ppermute | solution.py:282
  157.0 11.2 %collective-permute-start.23 = (bf16[512,256]{1,0:T(8,128)(2,1)S(1)}, bf16[512,256]{1,0:T(8,128)(2,1)S(1)}, u32[]{:S(2)}, u32[]{:S(2)}) collective-permute-start(bf16[512,256]{1,0:T(8,128)(2,1)S(1)} %collective-permute-done.21), channel_id=1, source_target_pairs={{0,28},{4,0},{8,4},{12,8},{16,12},{20,16},{24,20},{28,24},{1,29},{... | collective-permute-start | bytes 786440 | tf_op jit(solution)/shard_map/ppermute | solution.py:285
  162.6 11.7 %collective-permute-start.29 = (bf16[512,256]{1,0:T(8,128)(2,1)S(1)}, bf16[512,256]{1,0:T(8,128)(2,1)S(1)}, u32[]{:S(2)}, u32[]{:S(2)}) collective-permute-start(bf16[512,256]{1,0:T(8,128)(2,1)S(1)} %collective-permute-done.27), channel_id=1, source_target_pairs={{0,4},{4,8},{8,12},{12,16},{16,20},{20,24},{24,28},{28,0},{1,5},{5... | collective-permute-start | bytes 786440 | tf_op jit(solution)/shard_map/ppermute | solution.py:282
  183.4 15.6 %collective-permute-start.33 = (bf16[1024,256]{1,0:T(8,128)(2,1)S(1)}, bf16[1024,256]{1,0:T(8,128)(2,1)S(1)}, u32[]{:S(2)}, u32[]{:S(2)}) collective-permute-start(bf16[1024,256]{1,0:T(8,128)(2,1)S(1)} %fusion.18), channel_id=1, source_target_pairs={{0,1},{1,0},{2,3},{3,2},{4,5},{5,4},{6,7},{7,6},{8,9},{9,8},{10,11... | collective-permute-start | bytes 1572872 | tf_op jit(solution)/shard_map/ppermute | solution.py:328
  (12 other events, 112.7 us)

commit v9 on v8

--- a/solution.py
+++ b/solution.py
@@ -41,7 +41,12 @@
             out_ref[o * 8 + u] = jnp.zeros((9, 2, 128), jnp.bfloat16)
         return carry
 
-    lax.fori_loop(0, owners // 8, clear, 0)
+    step = pl.program_id(0)
+    tasks = left_ref.shape[0]
+
+    @pl.when(step == 0)
+    def _():
+        lax.fori_loop(0, owners // 8, clear, 0)
 
     def body(g, carry):
         base = pl.multiple_of(g * 16, 16)
@@ -65,14 +70,15 @@
                 ]
                 tiles.append(pick(rows, group).reshape(4, 2, 128).astype(jnp.bfloat16))
         for t, tile in enumerate(tiles):
-            owner = owner_ref[base + t]
+            task = step * tasks + base + t
+            owner = owner_ref[task]
             slot = count_ref[owner]
             count_ref[owner] = slot + 1
-            tag_ref[owner * 2 + slot] = block_ref[base + t]
+            tag_ref[owner * 2 + slot] = block_ref[task]
             out_ref[owner, pl.ds(slot * 4, 4)] = tile
         return carry
 
-    lax.fori_loop(0, left_ref.shape[0] // 16, body, 0)
+    lax.fori_loop(0, tasks // 16, body, 0)
 
     def label(o, carry):
         for u in range(8):
@@ -83,7 +89,9 @@
             out_ref[o * 8 + u, 8] = tile.astype(jnp.bfloat16)
         return carry
 
-    lax.fori_loop(0, owners // 8, label, 0)
+    @pl.when(step == pl.num_programs(0) - 1)
+    def _():
+        lax.fori_loop(0, owners // 8, label, 0)
 
 
 def read_labels(slot_ref, vector_ref, label_ref):
@@ -211,8 +219,15 @@
     return pl.pallas_call(
         contribute_kernel,
         out_shape=jax.ShapeDtypeStruct((tasks, 9, 2, 128), jnp.bfloat16),
-        in_specs=[SMEM, SMEM, VMEM, VMEM, VMEM],
-        out_specs=VMEM,
+        grid=(2,),
+        in_specs=[
+            SMEM,
+            SMEM,
+            pl.BlockSpec((tasks // 2, 32, 128), lambda i: (i, 0, 0)),
+            pl.BlockSpec((tasks // 2, 32, 128), lambda i: (i, 0, 0)),
+            pl.BlockSpec((tasks // 2, 128), lambda i: (i, 0)),
+        ],
+        out_specs=pl.BlockSpec((tasks, 9, 2, 128), lambda i: (0, 0, 0, 0)),
         scratch_shapes=[pltpu.SMEM((tasks,), jnp.int32), pltpu.SMEM((2 * tasks,), jnp.int32)],
         name="contribute",
     )(owner, block, left, right, weight)

time: 201 us -> 200 us (level)
  no operation moved by 1% of the time
where the time goes in v9:
time: 200 us
  waiting for transfers between devices  81.7 us (41%)
  starting transfers between devices  52.1 us (26%)
  blocking collectives  32.6 us (16%)
  Pallas kernels  17.5 us (9%)
  matrix products  9.3 us (5%)
  local copies, waits for them, and re-layouts  3.6 us (2%)
  other arithmetic  2.2 us (1%)
    ppermute x11, waiting for transfers between devices, gather_z(): up = lax.ppermute(up, 'z', ring_of(8, 1))  44.8 us
    all_to_all x1, blocking collectives, local(): lax.all_to_all(outgoing, AXES[:4], split_axis=0, concat_axis=0, tiled=True)  32.6 us
    ppermute x10, starting transfers between devices, gather_z(): down = lax.ppermute(down, 'z', ring_of(8, -1))  32.2 us
    ppermute x3, waiting for transfers between devices, product(): away = lax.ppermute(part, 'yhi', SWAP)  22.4 us
    dot_general x4, matrix products, dot(): return jnp.einsum('dmk,dkn->mn', a, b, preferred_element_type=jnp.float32)  9.3 us
    ppermute x3, starting transfers between devices, product(): away = lax.ppermute(part, 'yhi', SWAP)  8.78 us
    pallas_call x1, Pallas kernels, collect(): pl.pallas_call(collect_kernel, out_shape=(jax.ShapeDtypeStruct((1024, 512...  7.15 us
    pallas_call x1, Pallas kernels, contribute(): pl.pallas_call(contribute_kernel, out_shape=jax.ShapeDtypeStruct((tasks,...  5.19 us
  transfers between devices with their start and end apart: 34, of which 23 were waited for; matrix products, arithmetic and copies ran while one was open for 3% of the time, Pallas kernels for 4%

profile of v9, /device:TPU:2, one launch (start us, length us, event | category | flops | bytes accessed | tf_op | source)
XLA Modules:
  0.0 200.1 jit_solution(4414556284128283436)
XLA Ops:
  0.6 5.2 %contribute.1 = bf16[128,9,2,128]{3,2,1,0:T(2,128)(2,1)} custom-call(s32[128]{0:T(128)} %bitcast.81, s32[128]{0:T(128)} %block_ref.1, bf16[128,32,128]{2,1,0:T(8,128)(2,1)} %left_ref.1, bf16[128,32,128]{2,1,0:T(8,128)(2,1)} %right_ref.1, f32[128,128]{1,0:T(8,128)} %weight_ref.1), custom_call_target="tpu_custom_call" | custom-call | tf_op jit(solution)/shard_map/contribute/pallas_call | solution.py:219
  5.8 32.6 %all_to_all.5 = bf16[128,9,2,128]{3,2,1,0:T(2,128)(2,1)S(1)} all-to-all(bf16[128,9,2,128]{3,2,1,0:T(2,128)(2,1)} %contribute.1), channel_id=1, replica_groups=mesh['ylo'=2,'x'=4,'z'=8,'core'=2,'yhi'=2] {'ylo','x','z','core'}, dimensions={0} | all-to-all | bytes 1179648 | tf_op jit(solution)/shard_map/all_to_all | solution.py:353
  39.1 3.0 %collective-permute-start = (bf16[257,8,128]{2,1,0:T(8,128)(2,1)S(1)}, bf16[257,8,128]{2,1,0:T(8,128)(2,1)S(1)}, u32[]{:S(2)}, u32[]{:S(2)}) collective-permute-start(bf16[257,8,128]{2,1,0:T(8,128)(2,1)S(1)} %pad_maximum_fusion.8.slot_ref), channel_id=1, source_target_pairs={{0,1},{1,0},{2,3},{3,2},{4,5},{5,4},{6,7},{7,6},{8,9},{9,8},{10,11... | collective-permute-start | bytes 1579016 | tf_op jit(solution)/shard_map/ppermute | solution.py:360
  43.8 7.1 %collect.1 = (f32[1024,512]{1,0:T(8,128)S(1)}, bf16[1024,512]{1,0:T(8,128)(2,1)S(1)}) custom-call(s32[32,16]{1,0:T(8,128)S(1)} %copy.10.mask_ref, bf16[257,8,128]{2,1,0:T(8,128)(2,1)S(1)} %pad_maximum_fusion.8.slot_ref, f32[1024,512]{1,0:T(8,128)S(1)} %copy-done), custom_call_target="tpu_custom_call" | custom-call | flops 1048576 | bytes 8388608 | tf_op jit(solution)/shard_map/collect/pallas_call | solution.py:245
  50.9 4.5 %collective-permute-done.far_ref = bf16[257,8,128]{2,1,0:T(8,128)(2,1)S(1)} collective-permute-done((bf16[257,8,128]{2,1,0:T(8,128)(2,1)S(1)}, bf16[257,8,128]{2,1,0:T(8,128)(2,1)S(1)}, u32[]{:S(2)}, u32[]{:S(2)}) %collective-permute-start) | collective-permute-done | bytes 526368 | tf_op jit(solution)/shard_map/ppermute | solution.py:360
  55.4 5.1 %assemble.1 = (f32[1024,256]{1,0:T(8,128)}, bf16[1024,256]{1,0:T(8,128)(2,1)S(1)}, bf16[3,256,512]{2,1,0:T(8,128)(2,1)S(1)}) custom-call(bf16[257,8,128]{2,1,0:T(8,128)(2,1)S(1)} %collective-permute-done.far_ref, f32[1024,512]{1,0:T(8,128)S(1)} %get-tuple-element.9.base_ref, bf16[1024,512]{1,0:T(8,128)(2,1)S(1)} %get-tuple-element.10.pattern_ref), custom_call_target="tpu_custom_call" | custom-call | tf_op jit(solution)/shard_map/assemble/pallas_call | solution.py:264
  69.3 6.5 %collective-permute-done.1 = bf16[1024,256]{1,0:T(8,128)(2,1)S(1)} collective-permute-done((bf16[1024,256]{1,0:T(8,128)(2,1)S(1)}, bf16[1024,256]{1,0:T(8,128)(2,1)S(1)}, u32[]{:S(2)}, u32[]{:S(2)}) %collective-permute-start.1) | collective-permute-done | bytes 524320 | tf_op jit(solution)/shard_map/ppermute | solution.py:297
  75.8 3.2 %collective-permute-start.4 = (bf16[1024,256]{1,0:T(8,128)(2,1)S(1)}, bf16[1024,256]{1,0:T(8,128)(2,1)S(1)}, u32[]{:S(2)}, u32[]{:S(2)}) collective-permute-start(bf16[1024,256]{1,0:T(8,128)(2,1)S(1)} %collective-permute-done.2), channel_id=1, source_target_pairs={{0,28},{4,0},{8,4},{12,8},{16,12},{20,16},{24,20},{28,24},{1,29},{... | collective-permute-start | bytes 1572872 | tf_op jit(solution)/shard_map/ppermute | solution.py:300
  82.7 7.4 %collective-permute-done.3 = bf16[1024,256]{1,0:T(8,128)(2,1)S(1)} collective-permute-done((bf16[1024,256]{1,0:T(8,128)(2,1)S(1)}, bf16[1024,256]{1,0:T(8,128)(2,1)S(1)}, u32[]{:S(2)}, u32[]{:S(2)}) %collective-permute-start.3) | collective-permute-done | bytes 524320 | tf_op jit(solution)/shard_map/ppermute | solution.py:297
  90.2 3.3 %collective-permute-start.6 = (bf16[1024,256]{1,0:T(8,128)(2,1)S(1)}, bf16[1024,256]{1,0:T(8,128)(2,1)S(1)}, u32[]{:S(2)}, u32[]{:S(2)}) collective-permute-start(bf16[1024,256]{1,0:T(8,128)(2,1)S(1)} %collective-permute-done.4), channel_id=1, source_target_pairs={{0,28},{4,0},{8,4},{12,8},{16,12},{20,16},{24,20},{28,24},{1,29},{... | collective-permute-start | bytes 1572872 | tf_op jit(solution)/shard_map/ppermute | solution.py:300
  95.5 8.0 %collective-permute-done.5 = bf16[1024,256]{1,0:T(8,128)(2,1)S(1)} collective-permute-done((bf16[1024,256]{1,0:T(8,128)(2,1)S(1)}, bf16[1024,256]{1,0:T(8,128)(2,1)S(1)}, u32[]{:S(2)}, u32[]{:S(2)}) %collective-permute-start.5) | collective-permute-done | bytes 524320 | tf_op jit(solution)/shard_map/ppermute | solution.py:297
  106.0 9.9 %collective-permute-done.7 = bf16[1024,256]{1,0:T(8,128)(2,1)S(1)} collective-permute-done((bf16[1024,256]{1,0:T(8,128)(2,1)S(1)}, bf16[1024,256]{1,0:T(8,128)(2,1)S(1)}, u32[]{:S(2)}, u32[]{:S(2)}) %collective-permute-start.7) | collective-permute-done | bytes 524320 | tf_op jit(solution)/shard_map/ppermute | solution.py:297
  121.3 3.0 %collective-permute-start.16 = (bf16[512,256]{1,0:T(8,128)(2,1)S(1)}, bf16[512,256]{1,0:T(8,128)(2,1)S(1)}, u32[]{:S(2)}, u32[]{:S(2)}) collective-permute-start(bf16[512,256]{1,0:T(8,128)(2,1)S(1)} %get-tuple-element.22), channel_id=1, source_target_pairs={{0,1},{1,0},{2,3},{3,2},{4,5},{5,4},{6,7},{7,6},{8,9},{9,8},{10,11... | collective-permute-start | bytes 786440 | tf_op jit(solution)/shard_map/ppermute | solution.py:343
  124.3 7.0 %collective-permute-done.16 = bf16[512,256]{1,0:T(8,128)(2,1)S(1)} collective-permute-done((bf16[512,256]{1,0:T(8,128)(2,1)S(1)}, bf16[512,256]{1,0:T(8,128)(2,1)S(1)}, u32[]{:S(2)}, u32[]{:S(2)}) %collective-permute-start.16) | collective-permute-done | bytes 262176 | tf_op jit(solution)/shard_map/ppermute | solution.py:343
  134.4 3.2 %collective-permute-start.19 = (bf16[512,256]{1,0:T(8,128)(2,1)S(1)}, bf16[512,256]{1,0:T(8,128)(2,1)S(1)}, u32[]{:S(2)}, u32[]{:S(2)}) collective-permute-start(bf16[512,256]{1,0:T(8,128)(2,1)S(1)} %get-tuple-element.17), channel_id=1, source_target_pairs={{0,28},{4,0},{8,4},{12,8},{16,12},{20,16},{24,20},{28,24},{1,29},{... | collective-permute-start | bytes 786440 | tf_op jit(solution)/shard_map/ppermute | solution.py:300
  140.6 3.2 %collective-permute-start.26 = (bf16[512,256]{1,0:T(8,128)(2,1)S(1)}, bf16[512,256]{1,0:T(8,128)(2,1)S(1)}, u32[]{:S(2)}, u32[]{:S(2)}) collective-permute-start(bf16[512,256]{1,0:T(8,128)(2,1)S(1)} %get-tuple-element.20), channel_id=1, source_target_pairs={{0,28},{4,0},{8,4},{12,8},{16,12},{20,16},{24,20},{28,24},{1,29},{... | collective-permute-start | bytes 786440 | tf_op jit(solution)/shard_map/ppermute | solution.py:300
  143.9 3.5 %collective-permute-start.21 = (bf16[512,256]{1,0:T(8,128)(2,1)S(1)}, bf16[512,256]{1,0:T(8,128)(2,1)S(1)}, u32[]{:S(2)}, u32[]{:S(2)}) collective-permute-start(bf16[512,256]{1,0:T(8,128)(2,1)S(1)} %collective-permute-done.19), channel_id=1, source_target_pairs={{0,28},{4,0},{8,4},{12,8},{16,12},{20,16},{24,20},{28,24},{1,29},{... | collective-permute-start | bytes 786440 | tf_op jit(solution)/shard_map/ppermute | solution.py:300
  147.4 3.6 %collective-permute-done.25 = bf16[512,256]{1,0:T(8,128)(2,1)S(1)} collective-permute-done((bf16[512,256]{1,0:T(8,128)(2,1)S(1)}, bf16[512,256]{1,0:T(8,128)(2,1)S(1)}, u32[]{:S(2)}, u32[]{:S(2)}) %collective-permute-start.25) | collective-permute-done | bytes 262176 | tf_op jit(solution)/shard_map/ppermute | solution.py:297
  151.1 3.3 %collective-permute-start.28 = (bf16[512,256]{1,0:T(8,128)(2,1)S(1)}, bf16[512,256]{1,0:T(8,128)(2,1)S(1)}, u32[]{:S(2)}, u32[]{:S(2)}) collective-permute-start(bf16[512,256]{1,0:T(8,128)(2,1)S(1)} %collective-permute-done.26), channel_id=1, source_target_pairs={{0,28},{4,0},{8,4},{12,8},{16,12},{20,16},{24,20},{28,24},{1,29},{... | collective-permute-start | bytes 786440 | tf_op jit(solution)/shard_map/ppermute | solution.py:300
  156.7 3.3 %collective-permute-start.23 = (bf16[512,256]{1,0:T(8,128)(2,1)S(1)}, bf16[512,256]{1,0:T(8,128)(2,1)S(1)}, u32[]{:S(2)}, u32[]{:S(2)}) collective-permute-start(bf16[512,256]{1,0:T(8,128)(2,1)S(1)} %collective-permute-done.21), channel_id=1, source_target_pairs={{0,28},{4,0},{8,4},{12,8},{16,12},{20,16},{24,20},{28,24},{1,29},{... | collective-permute-start | bytes 786440 | tf_op jit(solution)/shard_map/ppermute | solution.py:300
  162.3 3.3 %collective-permute-start.30 = (bf16[512,256]{1,0:T(8,128)(2,1)S(1)}, bf16[512,256]{1,0:T(8,128)(2,1)S(1)}, u32[]{:S(2)}, u32[]{:S(2)}) collective-permute-start(bf16[512,256]{1,0:T(8,128)(2,1)S(1)} %collective-permute-done.28), channel_id=1, source_target_pairs={{0,28},{4,0},{8,4},{12,8},{16,12},{20,16},{24,20},{28,24},{1,29},{... | collective-permute-start | bytes 786440 | tf_op jit(solution)/shard_map/ppermute | solution.py:300
  170.3 3.7 %collective-permute-start.31 = (bf16[512,256]{1,0:T(8,128)(2,1)S(1)}, bf16[512,256]{1,0:T(8,128)(2,1)S(1)}, u32[]{:S(2)}, u32[]{:S(2)}) collective-permute-start(bf16[512,256]{1,0:T(8,128)(2,1)S(1)} %collective-permute-done.30), channel_id=1, source_target_pairs={{0,28},{4,0},{8,4},{12,8},{16,12},{20,16},{24,20},{28,24},{1,29},{... | collective-permute-start | bytes 786440 | tf_op jit(solution)/shard_map/ppermute | solution.py:300
  183.1 2.9 %collective-permute-start.33 = (bf16[1024,256]{1,0:T(8,128)(2,1)S(1)}, bf16[1024,256]{1,0:T(8,128)(2,1)S(1)}, u32[]{:S(2)}, u32[]{:S(2)}) collective-permute-start(bf16[1024,256]{1,0:T(8,128)(2,1)S(1)} %fusion.18), channel_id=1, source_target_pairs={{0,1},{1,0},{2,3},{3,2},{4,5},{5,4},{6,7},{7,6},{8,9},{9,8},{10,11... | collective-permute-start | bytes 1572872 | tf_op jit(solution)/shard_map/ppermute | solution.py:343
  186.0 12.7 %collective-permute-done.33 = bf16[1024,256]{1,0:T(8,128)(2,1)S(1)} collective-permute-done((bf16[1024,256]{1,0:T(8,128)(2,1)S(1)}, bf16[1024,256]{1,0:T(8,128)(2,1)S(1)}, u32[]{:S(2)}, u32[]{:S(2)}) %collective-permute-start.33) | collective-permute-done | bytes 524320 | tf_op jit(solution)/shard_map/ppermute | solution.py:343
  (101 shorter events, 50.2 us)
Async XLA Ops:
  39.1 16.3 %collective-permute-start = (bf16[257,8,128]{2,1,0:T(8,128)(2,1)S(1)}, bf16[257,8,128]{2,1,0:T(8,128)(2,1)S(1)}, u32[]{:S(2)}, u32[]{:S(2)}) collective-permute-start(bf16[257,8,128]{2,1,0:T(8,128)(2,1)S(1)} %pad_maximum_fusion.8.slot_ref), channel_id=1, source_target_pairs={{0,1},{1,0},{2,3},{3,2},{4,5},{5,4},{6,7},{7,6},{8,9},{9,8},{10,11... | collective-permute-start | bytes 1579016 | tf_op jit(solution)/shard_map/ppermute | solution.py:360
  60.6 15.2 %collective-permute-start.1 = (bf16[1024,256]{1,0:T(8,128)(2,1)S(1)}, bf16[1024,256]{1,0:T(8,128)(2,1)S(1)}, u32[]{:S(2)}, u32[]{:S(2)}) collective-permute-start(bf16[1024,256]{1,0:T(8,128)(2,1)S(1)} %get-tuple-element.12), channel_id=1, source_target_pairs={{0,4},{4,8},{8,12},{12,16},{16,20},{20,24},{24,28},{28,0},{1,5},{5... | collective-permute-start | bytes 1572872 | tf_op jit(solution)/shard_map/ppermute | solution.py:297
  61.8 14.0 %collective-permute-start.2 = (bf16[1024,256]{1,0:T(8,128)(2,1)S(1)}, bf16[1024,256]{1,0:T(8,128)(2,1)S(1)}, u32[]{:S(2)}, u32[]{:S(2)}) collective-permute-start(bf16[1024,256]{1,0:T(8,128)(2,1)S(1)} %get-tuple-element.12), channel_id=1, source_target_pairs={{0,28},{4,0},{8,4},{12,8},{16,12},{20,16},{24,20},{28,24},{1,29},{... | collective-permute-start | bytes 1572872 | tf_op jit(solution)/shard_map/ppermute | solution.py:300
  65.6 14.1 %collective-permute-start.9 = (bf16[256,1024]{1,0:T(8,128)(2,1)S(1)}, bf16[256,1024]{1,0:T(8,128)(2,1)S(1)}, u32[]{:S(2)}, u32[]{:S(2)}) collective-permute-start(bf16[256,1024]{1,0:T(8,128)(2,1)S(1)} %pad_maximum_fusion.9), channel_id=1, source_target_pairs={{0,128},{128,0},{1,129},{129,1},{2,130},{130,2},{3,131},{131,3},{4... | collective-permute-start | bytes 1572872 | tf_op jit(solution)/shard_map/ppermute | solution.py:312
  66.7 13.7 %collective-permute-start.10 = (bf16[256,1024]{1,0:T(8,128)(2,1)S(1)}, bf16[256,1024]{1,0:T(8,128)(2,1)S(1)}, u32[]{:S(2)}, u32[]{:S(2)}) collective-permute-start(bf16[256,1024]{1,0:T(8,128)(2,1)S(1)} %pad_maximum_fusion.9), channel_id=1, source_target_pairs={{0,32},{32,64},{64,96},{96,0},{1,33},{33,65},{65,97},{97,1},{2,34}... | collective-permute-start | bytes 1572872 | tf_op jit(solution)/shard_map/ppermute | solution.py:313
  68.0 22.1 %collective-permute-start.11 = (bf16[256,1024]{1,0:T(8,128)(2,1)S(1)}, bf16[256,1024]{1,0:T(8,128)(2,1)S(1)}, u32[]{:S(2)}, u32[]{:S(2)}) collective-permute-start(bf16[256,1024]{1,0:T(8,128)(2,1)S(1)} %pad_maximum_fusion.9), channel_id=1, source_target_pairs={{0,96},{32,0},{64,32},{96,64},{1,97},{33,1},{65,33},{97,65},{2,98}... | collective-permute-start | bytes 1572872 | tf_op jit(solution)/shard_map/ppermute | solution.py:314
  75.8 14.3 %collective-permute-start.3 = (bf16[1024,256]{1,0:T(8,128)(2,1)S(1)}, bf16[1024,256]{1,0:T(8,128)(2,1)S(1)}, u32[]{:S(2)}, u32[]{:S(2)}) collective-permute-start(bf16[1024,256]{1,0:T(8,128)(2,1)S(1)} %collective-permute-done.1), channel_id=1, source_target_pairs={{0,4},{4,8},{8,12},{12,16},{16,20},{20,24},{24,28},{28,0},{1,5},{5... | collective-permute-start | bytes 1572872 | tf_op jit(solution)/shard_map/ppermute | solution.py:297
  75.8 14.4 %collective-permute-start.4 = (bf16[1024,256]{1,0:T(8,128)(2,1)S(1)}, bf16[1024,256]{1,0:T(8,128)(2,1)S(1)}, u32[]{:S(2)}, u32[]{:S(2)}) collective-permute-start(bf16[1024,256]{1,0:T(8,128)(2,1)S(1)} %collective-permute-done.2), channel_id=1, source_target_pairs={{0,28},{4,0},{8,4},{12,8},{16,12},{20,16},{24,20},{28,24},{1,29},{... | collective-permute-start | bytes 1572872 | tf_op jit(solution)/shard_map/ppermute | solution.py:300
  80.5 24.1 %collective-permute-start.12 = (bf16[2,256,1024]{2,1,0:T(8,128)(2,1)S(1)}, bf16[2,256,1024]{2,1,0:T(8,128)(2,1)S(1)}, u32[]{:S(2)}, u32[]{:S(2)}) collective-permute-start(bf16[2,256,1024]{2,1,0:T(8,128)(2,1)S(1)} %pad_maximum_fusion.7), channel_id=1, source_target_pairs={{0,32},{32,64},{64,96},{96,0},{1,33},{33,65},{65,97},{97,1},{2,34}... | collective-permute-start | bytes 3145736 | tf_op jit(solution)/shard_map/ppermute | solution.py:315
  81.8 12.5 %collective-permute-start.13 = (bf16[256,1024]{1,0:T(8,128)(2,1)S(1)}, bf16[256,1024]{1,0:T(8,128)(2,1)S(1)}, u32[]{:S(2)}, u32[]{:S(2)}) collective-permute-start(bf16[256,1024]{1,0:T(8,128)(2,1)S(1)} %collective-permute-done.9), channel_id=1, source_target_pairs={{0,96},{32,0},{64,32},{96,64},{1,97},{33,1},{65,33},{97,65},{2,98}... | collective-permute-start | bytes 1572872 | tf_op jit(solution)/shard_map/ppermute | solution.py:316
  90.1 13.4 %collective-permute-start.5 = (bf16[1024,256]{1,0:T(8,128)(2,1)S(1)}, bf16[1024,256]{1,0:T(8,128)(2,1)S(1)}, u32[]{:S(2)}, u32[]{:S(2)}) collective-permute-start(bf16[1024,256]{1,0:T(8,128)(2,1)S(1)} %collective-permute-done.3), channel_id=1, source_target_pairs={{0,4},{4,8},{8,12},{12,16},{16,20},{20,24},{24,28},{28,0},{1,5},{5... | collective-permute-start | bytes 1572872 | tf_op jit(solution)/shard_map/ppermute | solution.py:297
  90.2 13.4 %collective-permute-start.6 = (bf16[1024,256]{1,0:T(8,128)(2,1)S(1)}, bf16[1024,256]{1,0:T(8,128)(2,1)S(1)}, u32[]{:S(2)}, u32[]{:S(2)}) collective-permute-start(bf16[1024,256]{1,0:T(8,128)(2,1)S(1)} %collective-permute-done.4), channel_id=1, source_target_pairs={{0,28},{4,0},{8,4},{12,8},{16,12},{20,16},{24,20},{28,24},{1,29},{... | collective-permute-start | bytes 1572872 | tf_op jit(solution)/shard_map/ppermute | solution.py:300
  94.4 11.6 %collective-permute-start.14 = (bf16[256,1024]{1,0:T(8,128)(2,1)S(1)}, bf16[256,1024]{1,0:T(8,128)(2,1)S(1)}, u32[]{:S(2)}, u32[]{:S(2)}) collective-permute-start(bf16[256,1024]{1,0:T(8,128)(2,1)S(1)} %collective-permute-done.13), channel_id=1, source_target_pairs={{0,96},{32,0},{64,32},{96,64},{1,97},{33,1},{65,33},{97,65},{2,98}... | collective-permute-start | bytes 1572872 | tf_op jit(solution)/shard_map/ppermute | solution.py:317
  103.5 12.5 %collective-permute-start.7 = (bf16[1024,256]{1,0:T(8,128)(2,1)S(1)}, bf16[1024,256]{1,0:T(8,128)(2,1)S(1)}, u32[]{:S(2)}, u32[]{:S(2)}) collective-permute-start(bf16[1024,256]{1,0:T(8,128)(2,1)S(1)} %collective-permute-done.5), channel_id=1, source_target_pairs={{0,4},{4,8},{8,12},{12,16},{16,20},{20,24},{24,28},{28,0},{1,5},{5... | collective-permute-start | bytes 1572872 | tf_op jit(solution)/shard_map/ppermute | solution.py:297
  140.5 10.5 %collective-permute-start.25 = (bf16[512,256]{1,0:T(8,128)(2,1)S(1)}, bf16[512,256]{1,0:T(8,128)(2,1)S(1)}, u32[]{:S(2)}, u32[]{:S(2)}) collective-permute-start(bf16[512,256]{1,0:T(8,128)(2,1)S(1)} %get-tuple-element.20), channel_id=1, source_target_pairs={{0,4},{4,8},{8,12},{12,16},{16,20},{20,24},{24,28},{28,0},{1,5},{5... | collective-permute-start | bytes 786440 | tf_op jit(solution)/shard_map/ppermute | solution.py:297
  140.6 10.5 %collective-permute-start.26 = (bf16[512,256]{1,0:T(8,128)(2,1)S(1)}, bf16[512,256]{1,0:T(8,128)(2,1)S(1)}, u32[]{:S(2)}, u32[]{:S(2)}) collective-permute-start(bf16[512,256]{1,0:T(8,128)(2,1)S(1)} %get-tuple-element.20), channel_id=1, source_target_pairs={{0,28},{4,0},{8,4},{12,8},{16,12},{20,16},{24,20},{28,24},{1,29},{... | collective-permute-start | bytes 786440 | tf_op jit(solution)/shard_map/ppermute | solution.py:300
  143.8 12.8 %collective-permute-start.20 = (bf16[512,256]{1,0:T(8,128)(2,1)S(1)}, bf16[512,256]{1,0:T(8,128)(2,1)S(1)}, u32[]{:S(2)}, u32[]{:S(2)}) collective-permute-start(bf16[512,256]{1,0:T(8,128)(2,1)S(1)} %collective-permute-done.18), channel_id=1, source_target_pairs={{0,4},{4,8},{8,12},{12,16},{16,20},{20,24},{24,28},{28,0},{1,5},{5... | collective-permute-start | bytes 786440 | tf_op jit(solution)/shard_map/ppermute | solution.py:297
  143.9 12.8 %collective-permute-start.21 = (bf16[512,256]{1,0:T(8,128)(2,1)S(1)}, bf16[512,256]{1,0:T(8,128)(2,1)S(1)}, u32[]{:S(2)}, u32[]{:S(2)}) collective-permute-start(bf16[512,256]{1,0:T(8,128)(2,1)S(1)} %collective-permute-done.19), channel_id=1, source_target_pairs={{0,28},{4,0},{8,4},{12,8},{16,12},{20,16},{24,20},{28,24},{1,29},{... | collective-permute-start | bytes 786440 | tf_op jit(solution)/shard_map/ppermute | solution.py:300
  151.0 11.2 %collective-permute-start.27 = (bf16[512,256]{1,0:T(8,128)(2,1)S(1)}, bf16[512,256]{1,0:T(8,128)(2,1)S(1)}, u32[]{:S(2)}, u32[]{:S(2)}) collective-permute-start(bf16[512,256]{1,0:T(8,128)(2,1)S(1)} %collective-permute-done.25), channel_id=1, source_target_pairs={{0,4},{4,8},{8,12},{12,16},{16,20},{20,24},{24,28},{28,0},{1,5},{5... | collective-permute-start | bytes 786440 | tf_op jit(solution)/shard_map/ppermute | solution.py:297
  151.1 11.2 %collective-permute-start.28 = (bf16[512,256]{1,0:T(8,128)(2,1)S(1)}, bf16[512,256]{1,0:T(8,128)(2,1)S(1)}, u32[]{:S(2)}, u32[]{:S(2)}) collective-permute-start(bf16[512,256]{1,0:T(8,128)(2,1)S(1)} %collective-permute-done.26), channel_id=1, source_target_pairs={{0,28},{4,0},{8,4},{12,8},{16,12},{20,16},{24,20},{28,24},{1,29},{... | collective-permute-start | bytes 786440 | tf_op jit(solution)/shard_map/ppermute | solution.py:300
  156.7 11.2 %collective-permute-start.22 = (bf16[512,256]{1,0:T(8,128)(2,1)S(1)}, bf16[512,256]{1,0:T(8,128)(2,1)S(1)}, u32[]{:S(2)}, u32[]{:S(2)}) collective-permute-start(bf16[512,256]{1,0:T(8,128)(2,1)S(1)} %collective-permute-done.20), channel_id=1, source_target_pairs={{0,4},{4,8},{8,12},{12,16},{16,20},{20,24},{24,28},{28,0},{1,5},{5... | collective-permute-start | bytes 786440 | tf_op jit(solution)/shard_map/ppermute | solution.py:297
  156.7 11.2 %collective-permute-start.23 = (bf16[512,256]{1,0:T(8,128)(2,1)S(1)}, bf16[512,256]{1,0:T(8,128)(2,1)S(1)}, u32[]{:S(2)}, u32[]{:S(2)}) collective-permute-start(bf16[512,256]{1,0:T(8,128)(2,1)S(1)} %collective-permute-done.21), channel_id=1, source_target_pairs={{0,28},{4,0},{8,4},{12,8},{16,12},{20,16},{24,20},{28,24},{1,29},{... | collective-permute-start | bytes 786440 | tf_op jit(solution)/shard_map/ppermute | solution.py:300
  162.3 11.7 %collective-permute-start.29 = (bf16[512,256]{1,0:T(8,128)(2,1)S(1)}, bf16[512,256]{1,0:T(8,128)(2,1)S(1)}, u32[]{:S(2)}, u32[]{:S(2)}) collective-permute-start(bf16[512,256]{1,0:T(8,128)(2,1)S(1)} %collective-permute-done.27), channel_id=1, source_target_pairs={{0,4},{4,8},{8,12},{12,16},{16,20},{20,24},{24,28},{28,0},{1,5},{5... | collective-permute-start | bytes 786440 | tf_op jit(solution)/shard_map/ppermute | solution.py:297
  183.1 15.6 %collective-permute-start.33 = (bf16[1024,256]{1,0:T(8,128)(2,1)S(1)}, bf16[1024,256]{1,0:T(8,128)(2,1)S(1)}, u32[]{:S(2)}, u32[]{:S(2)}) collective-permute-start(bf16[1024,256]{1,0:T(8,128)(2,1)S(1)} %fusion.18), channel_id=1, source_target_pairs={{0,1},{1,0},{2,3},{3,2},{4,5},{5,4},{6,7},{7,6},{8,9},{9,8},{10,11... | collective-permute-start | bytes 1572872 | tf_op jit(solution)/shard_map/ppermute | solution.py:343
  (12 other events, 112.4 us)

commit v10 on v9

--- a/solution.py
+++ b/solution.py
@@ -219,13 +219,13 @@
     return pl.pallas_call(
         contribute_kernel,
         out_shape=jax.ShapeDtypeStruct((tasks, 9, 2, 128), jnp.bfloat16),
-        grid=(2,),
+        grid=(4,),
         in_specs=[
             SMEM,
             SMEM,
-            pl.BlockSpec((tasks // 2, 32, 128), lambda i: (i, 0, 0)),
-            pl.BlockSpec((tasks // 2, 32, 128), lambda i: (i, 0, 0)),
-            pl.BlockSpec((tasks // 2, 128), lambda i: (i, 0)),
+            pl.BlockSpec((tasks // 4, 32, 128), lambda i: (i, 0, 0)),
+            pl.BlockSpec((tasks // 4, 32, 128), lambda i: (i, 0, 0)),
+            pl.BlockSpec((tasks // 4, 128), lambda i: (i, 0)),
         ],
         out_specs=pl.BlockSpec((tasks, 9, 2, 128), lambda i: (0, 0, 0, 0)),
         scratch_shapes=[pltpu.SMEM((tasks,), jnp.int32), pltpu.SMEM((2 * tasks,), jnp.int32)],

time: 200 us -> 201 us (level)
  no operation moved by 1% of the time
where the time goes in v10:
time: 201 us; the launch traced here: 200 us
  waiting for transfers between devices  81.7 us (41%)
  starting transfers between devices  52.1 us (26%)
  blocking collectives  32.6 us (16%)
  Pallas kernels  17.8 us (9%)
  matrix products  9.3 us (5%)
  local copies, waits for them, and re-layouts  3.6 us (2%)
  other arithmetic  2.2 us (1%)
    ppermute x11, waiting for transfers between devices, gather_z(): up = lax.ppermute(up, 'z', ring_of(8, 1))  44.8 us
    all_to_all x1, blocking collectives, local(): lax.all_to_all(outgoing, AXES[:4], split_axis=0, concat_axis=0, tiled=True)  32.6 us
    ppermute x10, starting transfers between devices, gather_z(): down = lax.ppermute(down, 'z', ring_of(8, -1))  32.2 us
    ppermute x3, waiting for transfers between devices, product(): away = lax.ppermute(part, 'yhi', SWAP)  22.4 us
    dot_general x4, matrix products, dot(): return jnp.einsum('dmk,dkn->mn', a, b, preferred_element_type=jnp.float32)  9.3 us
    ppermute x3, starting transfers between devices, product(): away = lax.ppermute(part, 'yhi', SWAP)  8.8 us
    pallas_call x1, Pallas kernels, collect(): pl.pallas_call(collect_kernel, out_shape=(jax.ShapeDtypeStruct((1024, 512...  7.15 us
    pallas_call x1, Pallas kernels, contribute(): pl.pallas_call(contribute_kernel, out_shape=jax.ShapeDtypeStruct((tasks,...  5.54 us
  transfers between devices with their start and end apart: 34, of which 23 were waited for; matrix products, arithmetic and copies ran while one was open for 3% of the time, Pallas kernels for 4%

profile of v10, /device:TPU:2, one launch (start us, length us, event | category | flops | bytes accessed | tf_op | source)
XLA Modules:
  0.0 200.4 jit_solution(15525667990421909122)
XLA Ops:
  0.6 5.5 %contribute.1 = bf16[128,9,2,128]{3,2,1,0:T(2,128)(2,1)} custom-call(s32[128]{0:T(128)} %bitcast.81, s32[128]{0:T(128)} %block_ref.1, bf16[128,32,128]{2,1,0:T(8,128)(2,1)} %left_ref.1, bf16[128,32,128]{2,1,0:T(8,128)(2,1)} %right_ref.1, f32[128,128]{1,0:T(8,128)} %weight_ref.1), custom_call_target="tpu_custom_call" | custom-call | tf_op jit(solution)/shard_map/contribute/pallas_call | solution.py:219
  6.2 32.6 %all_to_all.5 = bf16[128,9,2,128]{3,2,1,0:T(2,128)(2,1)S(1)} all-to-all(bf16[128,9,2,128]{3,2,1,0:T(2,128)(2,1)} %contribute.1), channel_id=1, replica_groups=mesh['ylo'=2,'x'=4,'z'=8,'core'=2,'yhi'=2] {'ylo','x','z','core'}, dimensions={0} | all-to-all | bytes 1179648 | tf_op jit(solution)/shard_map/all_to_all | solution.py:353
  39.4 3.0 %collective-permute-start = (bf16[257,8,128]{2,1,0:T(8,128)(2,1)S(1)}, bf16[257,8,128]{2,1,0:T(8,128)(2,1)S(1)}, u32[]{:S(2)}, u32[]{:S(2)}) collective-permute-start(bf16[257,8,128]{2,1,0:T(8,128)(2,1)S(1)} %pad_maximum_fusion.8.slot_ref), channel_id=1, source_target_pairs={{0,1},{1,0},{2,3},{3,2},{4,5},{5,4},{6,7},{7,6},{8,9},{9,8},{10,11... | collective-permute-start | bytes 1579016 | tf_op jit(solution)/shard_map/ppermute | solution.py:360
  44.1 7.1 %collect.1 = (f32[1024,512]{1,0:T(8,128)S(1)}, bf16[1024,512]{1,0:T(8,128)(2,1)S(1)}) custom-call(s32[32,16]{1,0:T(8,128)S(1)} %copy.10.mask_ref, bf16[257,8,128]{2,1,0:T(8,128)(2,1)S(1)} %pad_maximum_fusion.8.slot_ref, f32[1024,512]{1,0:T(8,128)S(1)} %copy-done), custom_call_target="tpu_custom_call" | custom-call | flops 1048576 | bytes 8388608 | tf_op jit(solution)/shard_map/collect/pallas_call | solution.py:245
  51.2 4.5 %collective-permute-done.far_ref = bf16[257,8,128]{2,1,0:T(8,128)(2,1)S(1)} collective-permute-done((bf16[257,8,128]{2,1,0:T(8,128)(2,1)S(1)}, bf16[257,8,128]{2,1,0:T(8,128)(2,1)S(1)}, u32[]{:S(2)}, u32[]{:S(2)}) %collective-permute-start) | collective-permute-done | bytes 526368 | tf_op jit(solution)/shard_map/ppermute | solution.py:360
  55.8 5.1 %assemble.1 = (f32[1024,256]{1,0:T(8,128)}, bf16[1024,256]{1,0:T(8,128)(2,1)S(1)}, bf16[3,256,512]{2,1,0:T(8,128)(2,1)S(1)}) custom-call(bf16[257,8,128]{2,1,0:T(8,128)(2,1)S(1)} %collective-permute-done.far_ref, f32[1024,512]{1,0:T(8,128)S(1)} %get-tuple-element.9.base_ref, bf16[1024,512]{1,0:T(8,128)(2,1)S(1)} %get-tuple-element.10.pattern_ref), custom_call_target="tpu_custom_call" | custom-call | tf_op jit(solution)/shard_map/assemble/pallas_call | solution.py:264
  69.7 6.5 %collective-permute-done.1 = bf16[1024,256]{1,0:T(8,128)(2,1)S(1)} collective-permute-done((bf16[1024,256]{1,0:T(8,128)(2,1)S(1)}, bf16[1024,256]{1,0:T(8,128)(2,1)S(1)}, u32[]{:S(2)}, u32[]{:S(2)}) %collective-permute-start.1) | collective-permute-done | bytes 524320 | tf_op jit(solution)/shard_map/ppermute | solution.py:297
  76.1 3.2 %collective-permute-start.4 = (bf16[1024,256]{1,0:T(8,128)(2,1)S(1)}, bf16[1024,256]{1,0:T(8,128)(2,1)S(1)}, u32[]{:S(2)}, u32[]{:S(2)}) collective-permute-start(bf16[1024,256]{1,0:T(8,128)(2,1)S(1)} %collective-permute-done.2), channel_id=1, source_target_pairs={{0,28},{4,0},{8,4},{12,8},{16,12},{20,16},{24,20},{28,24},{1,29},{... | collective-permute-start | bytes 1572872 | tf_op jit(solution)/shard_map/ppermute | solution.py:300
  83.0 7.4 %collective-permute-done.3 = bf16[1024,256]{1,0:T(8,128)(2,1)S(1)} collective-permute-done((bf16[1024,256]{1,0:T(8,128)(2,1)S(1)}, bf16[1024,256]{1,0:T(8,128)(2,1)S(1)}, u32[]{:S(2)}, u32[]{:S(2)}) %collective-permute-start.3) | collective-permute-done | bytes 524320 | tf_op jit(solution)/shard_map/ppermute | solution.py:297
  90.5 3.3 %collective-permute-start.6 = (bf16[1024,256]{1,0:T(8,128)(2,1)S(1)}, bf16[1024,256]{1,0:T(8,128)(2,1)S(1)}, u32[]{:S(2)}, u32[]{:S(2)}) collective-permute-start(bf16[1024,256]{1,0:T(8,128)(2,1)S(1)} %collective-permute-done.4), channel_id=1, source_target_pairs={{0,28},{4,0},{8,4},{12,8},{16,12},{20,16},{24,20},{28,24},{1,29},{... | collective-permute-start | bytes 1572872 | tf_op jit(solution)/shard_map/ppermute | solution.py:300
  95.9 8.0 %collective-permute-done.5 = bf16[1024,256]{1,0:T(8,128)(2,1)S(1)} collective-permute-done((bf16[1024,256]{1,0:T(8,128)(2,1)S(1)}, bf16[1024,256]{1,0:T(8,128)(2,1)S(1)}, u32[]{:S(2)}, u32[]{:S(2)}) %collective-permute-start.5) | collective-permute-done | bytes 524320 | tf_op jit(solution)/shard_map/ppermute | solution.py:297
  106.4 9.9 %collective-permute-done.7 = bf16[1024,256]{1,0:T(8,128)(2,1)S(1)} collective-permute-done((bf16[1024,256]{1,0:T(8,128)(2,1)S(1)}, bf16[1024,256]{1,0:T(8,128)(2,1)S(1)}, u32[]{:S(2)}, u32[]{:S(2)}) %collective-permute-start.7) | collective-permute-done | bytes 524320 | tf_op jit(solution)/shard_map/ppermute | solution.py:297
  121.6 3.0 %collective-permute-start.16 = (bf16[512,256]{1,0:T(8,128)(2,1)S(1)}, bf16[512,256]{1,0:T(8,128)(2,1)S(1)}, u32[]{:S(2)}, u32[]{:S(2)}) collective-permute-start(bf16[512,256]{1,0:T(8,128)(2,1)S(1)} %get-tuple-element.22), channel_id=1, source_target_pairs={{0,1},{1,0},{2,3},{3,2},{4,5},{5,4},{6,7},{7,6},{8,9},{9,8},{10,11... | collective-permute-start | bytes 786440 | tf_op jit(solution)/shard_map/ppermute | solution.py:343
  124.6 7.0 %collective-permute-done.16 = bf16[512,256]{1,0:T(8,128)(2,1)S(1)} collective-permute-done((bf16[512,256]{1,0:T(8,128)(2,1)S(1)}, bf16[512,256]{1,0:T(8,128)(2,1)S(1)}, u32[]{:S(2)}, u32[]{:S(2)}) %collective-permute-start.16) | collective-permute-done | bytes 262176 | tf_op jit(solution)/shard_map/ppermute | solution.py:343
  134.8 3.2 %collective-permute-start.19 = (bf16[512,256]{1,0:T(8,128)(2,1)S(1)}, bf16[512,256]{1,0:T(8,128)(2,1)S(1)}, u32[]{:S(2)}, u32[]{:S(2)}) collective-permute-start(bf16[512,256]{1,0:T(8,128)(2,1)S(1)} %get-tuple-element.17), channel_id=1, source_target_pairs={{0,28},{4,0},{8,4},{12,8},{16,12},{20,16},{24,20},{28,24},{1,29},{... | collective-permute-start | bytes 786440 | tf_op jit(solution)/shard_map/ppermute | solution.py:300
  140.9 3.2 %collective-permute-start.26 = (bf16[512,256]{1,0:T(8,128)(2,1)S(1)}, bf16[512,256]{1,0:T(8,128)(2,1)S(1)}, u32[]{:S(2)}, u32[]{:S(2)}) collective-permute-start(bf16[512,256]{1,0:T(8,128)(2,1)S(1)} %get-tuple-element.20), channel_id=1, source_target_pairs={{0,28},{4,0},{8,4},{12,8},{16,12},{20,16},{24,20},{28,24},{1,29},{... | collective-permute-start | bytes 786440 | tf_op jit(solution)/shard_map/ppermute | solution.py:300
  144.2 3.5 %collective-permute-start.21 = (bf16[512,256]{1,0:T(8,128)(2,1)S(1)}, bf16[512,256]{1,0:T(8,128)(2,1)S(1)}, u32[]{:S(2)}, u32[]{:S(2)}) collective-permute-start(bf16[512,256]{1,0:T(8,128)(2,1)S(1)} %collective-permute-done.19), channel_id=1, source_target_pairs={{0,28},{4,0},{8,4},{12,8},{16,12},{20,16},{24,20},{28,24},{1,29},{... | collective-permute-start | bytes 786440 | tf_op jit(solution)/shard_map/ppermute | solution.py:300
  147.8 3.6 %collective-permute-done.25 = bf16[512,256]{1,0:T(8,128)(2,1)S(1)} collective-permute-done((bf16[512,256]{1,0:T(8,128)(2,1)S(1)}, bf16[512,256]{1,0:T(8,128)(2,1)S(1)}, u32[]{:S(2)}, u32[]{:S(2)}) %collective-permute-start.25) | collective-permute-done | bytes 262176 | tf_op jit(solution)/shard_map/ppermute | solution.py:297
  151.4 3.3 %collective-permute-start.28 = (bf16[512,256]{1,0:T(8,128)(2,1)S(1)}, bf16[512,256]{1,0:T(8,128)(2,1)S(1)}, u32[]{:S(2)}, u32[]{:S(2)}) collective-permute-start(bf16[512,256]{1,0:T(8,128)(2,1)S(1)} %collective-permute-done.26), channel_id=1, source_target_pairs={{0,28},{4,0},{8,4},{12,8},{16,12},{20,16},{24,20},{28,24},{1,29},{... | collective-permute-start | bytes 786440 | tf_op jit(solution)/shard_map/ppermute | solution.py:300
  157.0 3.3 %collective-permute-start.23 = (bf16[512,256]{1,0:T(8,128)(2,1)S(1)}, bf16[512,256]{1,0:T(8,128)(2,1)S(1)}, u32[]{:S(2)}, u32[]{:S(2)}) collective-permute-start(bf16[512,256]{1,0:T(8,128)(2,1)S(1)} %collective-permute-done.21), channel_id=1, source_target_pairs={{0,28},{4,0},{8,4},{12,8},{16,12},{20,16},{24,20},{28,24},{1,29},{... | collective-permute-start | bytes 786440 | tf_op jit(solution)/shard_map/ppermute | solution.py:300
  162.7 3.3 %collective-permute-start.30 = (bf16[512,256]{1,0:T(8,128)(2,1)S(1)}, bf16[512,256]{1,0:T(8,128)(2,1)S(1)}, u32[]{:S(2)}, u32[]{:S(2)}) collective-permute-start(bf16[512,256]{1,0:T(8,128)(2,1)S(1)} %collective-permute-done.28), channel_id=1, source_target_pairs={{0,28},{4,0},{8,4},{12,8},{16,12},{20,16},{24,20},{28,24},{1,29},{... | collective-permute-start | bytes 786440 | tf_op jit(solution)/shard_map/ppermute | solution.py:300
  170.6 3.7 %collective-permute-start.31 = (bf16[512,256]{1,0:T(8,128)(2,1)S(1)}, bf16[512,256]{1,0:T(8,128)(2,1)S(1)}, u32[]{:S(2)}, u32[]{:S(2)}) collective-permute-start(bf16[512,256]{1,0:T(8,128)(2,1)S(1)} %collective-permute-done.30), channel_id=1, source_target_pairs={{0,28},{4,0},{8,4},{12,8},{16,12},{20,16},{24,20},{28,24},{1,29},{... | collective-permute-start | bytes 786440 | tf_op jit(solution)/shard_map/ppermute | solution.py:300
  183.5 2.9 %collective-permute-start.33 = (bf16[1024,256]{1,0:T(8,128)(2,1)S(1)}, bf16[1024,256]{1,0:T(8,128)(2,1)S(1)}, u32[]{:S(2)}, u32[]{:S(2)}) collective-permute-start(bf16[1024,256]{1,0:T(8,128)(2,1)S(1)} %fusion.18), channel_id=1, source_target_pairs={{0,1},{1,0},{2,3},{3,2},{4,5},{5,4},{6,7},{7,6},{8,9},{9,8},{10,11... | collective-permute-start | bytes 1572872 | tf_op jit(solution)/shard_map/ppermute | solution.py:343
  186.4 12.7 %collective-permute-done.33 = bf16[1024,256]{1,0:T(8,128)(2,1)S(1)} collective-permute-done((bf16[1024,256]{1,0:T(8,128)(2,1)S(1)}, bf16[1024,256]{1,0:T(8,128)(2,1)S(1)}, u32[]{:S(2)}, u32[]{:S(2)}) %collective-permute-start.33) | collective-permute-done | bytes 524320 | tf_op jit(solution)/shard_map/ppermute | solution.py:343
  (101 shorter events, 50.2 us)
Async XLA Ops:
  39.4 16.3 %collective-permute-start = (bf16[257,8,128]{2,1,0:T(8,128)(2,1)S(1)}, bf16[257,8,128]{2,1,0:T(8,128)(2,1)S(1)}, u32[]{:S(2)}, u32[]{:S(2)}) collective-permute-start(bf16[257,8,128]{2,1,0:T(8,128)(2,1)S(1)} %pad_maximum_fusion.8.slot_ref), channel_id=1, source_target_pairs={{0,1},{1,0},{2,3},{3,2},{4,5},{5,4},{6,7},{7,6},{8,9},{9,8},{10,11... | collective-permute-start | bytes 1579016 | tf_op jit(solution)/shard_map/ppermute | solution.py:360
  60.9 15.2 %collective-permute-start.1 = (bf16[1024,256]{1,0:T(8,128)(2,1)S(1)}, bf16[1024,256]{1,0:T(8,128)(2,1)S(1)}, u32[]{:S(2)}, u32[]{:S(2)}) collective-permute-start(bf16[1024,256]{1,0:T(8,128)(2,1)S(1)} %get-tuple-element.12), channel_id=1, source_target_pairs={{0,4},{4,8},{8,12},{12,16},{16,20},{20,24},{24,28},{28,0},{1,5},{5... | collective-permute-start | bytes 1572872 | tf_op jit(solution)/shard_map/ppermute | solution.py:297
  62.2 14.0 %collective-permute-start.2 = (bf16[1024,256]{1,0:T(8,128)(2,1)S(1)}, bf16[1024,256]{1,0:T(8,128)(2,1)S(1)}, u32[]{:S(2)}, u32[]{:S(2)}) collective-permute-start(bf16[1024,256]{1,0:T(8,128)(2,1)S(1)} %get-tuple-element.12), channel_id=1, source_target_pairs={{0,28},{4,0},{8,4},{12,8},{16,12},{20,16},{24,20},{28,24},{1,29},{... | collective-permute-start | bytes 1572872 | tf_op jit(solution)/shard_map/ppermute | solution.py:300
  65.9 14.1 %collective-permute-start.9 = (bf16[256,1024]{1,0:T(8,128)(2,1)S(1)}, bf16[256,1024]{1,0:T(8,128)(2,1)S(1)}, u32[]{:S(2)}, u32[]{:S(2)}) collective-permute-start(bf16[256,1024]{1,0:T(8,128)(2,1)S(1)} %pad_maximum_fusion.9), channel_id=1, source_target_pairs={{0,128},{128,0},{1,129},{129,1},{2,130},{130,2},{3,131},{131,3},{4... | collective-permute-start | bytes 1572872 | tf_op jit(solution)/shard_map/ppermute | solution.py:312
  67.0 13.7 %collective-permute-start.10 = (bf16[256,1024]{1,0:T(8,128)(2,1)S(1)}, bf16[256,1024]{1,0:T(8,128)(2,1)S(1)}, u32[]{:S(2)}, u32[]{:S(2)}) collective-permute-start(bf16[256,1024]{1,0:T(8,128)(2,1)S(1)} %pad_maximum_fusion.9), channel_id=1, source_target_pairs={{0,32},{32,64},{64,96},{96,0},{1,33},{33,65},{65,97},{97,1},{2,34}... | collective-permute-start | bytes 1572872 | tf_op jit(solution)/shard_map/ppermute | solution.py:313
  68.3 22.1 %collective-permute-start.11 = (bf16[256,1024]{1,0:T(8,128)(2,1)S(1)}, bf16[256,1024]{1,0:T(8,128)(2,1)S(1)}, u32[]{:S(2)}, u32[]{:S(2)}) collective-permute-start(bf16[256,1024]{1,0:T(8,128)(2,1)S(1)} %pad_maximum_fusion.9), channel_id=1, source_target_pairs={{0,96},{32,0},{64,32},{96,64},{1,97},{33,1},{65,33},{97,65},{2,98}... | collective-permute-start | bytes 1572872 | tf_op jit(solution)/shard_map/ppermute | solution.py:314
  76.1 14.3 %collective-permute-start.3 = (bf16[1024,256]{1,0:T(8,128)(2,1)S(1)}, bf16[1024,256]{1,0:T(8,128)(2,1)S(1)}, u32[]{:S(2)}, u32[]{:S(2)}) collective-permute-start(bf16[1024,256]{1,0:T(8,128)(2,1)S(1)} %collective-permute-done.1), channel_id=1, source_target_pairs={{0,4},{4,8},{8,12},{12,16},{16,20},{20,24},{24,28},{28,0},{1,5},{5... | collective-permute-start | bytes 1572872 | tf_op jit(solution)/shard_map/ppermute | solution.py:297
  76.1 14.4 %collective-permute-start.4 = (bf16[1024,256]{1,0:T(8,128)(2,1)S(1)}, bf16[1024,256]{1,0:T(8,128)(2,1)S(1)}, u32[]{:S(2)}, u32[]{:S(2)}) collective-permute-start(bf16[1024,256]{1,0:T(8,128)(2,1)S(1)} %collective-permute-done.2), channel_id=1, source_target_pairs={{0,28},{4,0},{8,4},{12,8},{16,12},{20,16},{24,20},{28,24},{1,29},{... | collective-permute-start | bytes 1572872 | tf_op jit(solution)/shard_map/ppermute | solution.py:300
  80.8 24.1 %collective-permute-start.12 = (bf16[2,256,1024]{2,1,0:T(8,128)(2,1)S(1)}, bf16[2,256,1024]{2,1,0:T(8,128)(2,1)S(1)}, u32[]{:S(2)}, u32[]{:S(2)}) collective-permute-start(bf16[2,256,1024]{2,1,0:T(8,128)(2,1)S(1)} %pad_maximum_fusion.7), channel_id=1, source_target_pairs={{0,32},{32,64},{64,96},{96,0},{1,33},{33,65},{65,97},{97,1},{2,34}... | collective-permute-start | bytes 3145736 | tf_op jit(solution)/shard_map/ppermute | solution.py:315
  82.2 12.5 %collective-permute-start.13 = (bf16[256,1024]{1,0:T(8,128)(2,1)S(1)}, bf16[256,1024]{1,0:T(8,128)(2,1)S(1)}, u32[]{:S(2)}, u32[]{:S(2)}) collective-permute-start(bf16[256,1024]{1,0:T(8,128)(2,1)S(1)} %collective-permute-done.9), channel_id=1, source_target_pairs={{0,96},{32,0},{64,32},{96,64},{1,97},{33,1},{65,33},{97,65},{2,98}... | collective-permute-start | bytes 1572872 | tf_op jit(solution)/shard_map/ppermute | solution.py:316
  90.5 13.4 %collective-permute-start.5 = (bf16[1024,256]{1,0:T(8,128)(2,1)S(1)}, bf16[1024,256]{1,0:T(8,128)(2,1)S(1)}, u32[]{:S(2)}, u32[]{:S(2)}) collective-permute-start(bf16[1024,256]{1,0:T(8,128)(2,1)S(1)} %collective-permute-done.3), channel_id=1, source_target_pairs={{0,4},{4,8},{8,12},{12,16},{16,20},{20,24},{24,28},{28,0},{1,5},{5... | collective-permute-start | bytes 1572872 | tf_op jit(solution)/shard_map/ppermute | solution.py:297
  90.5 13.4 %collective-permute-start.6 = (bf16[1024,256]{1,0:T(8,128)(2,1)S(1)}, bf16[1024,256]{1,0:T(8,128)(2,1)S(1)}, u32[]{:S(2)}, u32[]{:S(2)}) collective-permute-start(bf16[1024,256]{1,0:T(8,128)(2,1)S(1)} %collective-permute-done.4), channel_id=1, source_target_pairs={{0,28},{4,0},{8,4},{12,8},{16,12},{20,16},{24,20},{28,24},{1,29},{... | collective-permute-start | bytes 1572872 | tf_op jit(solution)/shard_map/ppermute | solution.py:300
  94.7 11.6 %collective-permute-start.14 = (bf16[256,1024]{1,0:T(8,128)(2,1)S(1)}, bf16[256,1024]{1,0:T(8,128)(2,1)S(1)}, u32[]{:S(2)}, u32[]{:S(2)}) collective-permute-start(bf16[256,1024]{1,0:T(8,128)(2,1)S(1)} %collective-permute-done.13), channel_id=1, source_target_pairs={{0,96},{32,0},{64,32},{96,64},{1,97},{33,1},{65,33},{97,65},{2,98}... | collective-permute-start | bytes 1572872 | tf_op jit(solution)/shard_map/ppermute | solution.py:317
  103.8 12.5 %collective-permute-start.7 = (bf16[1024,256]{1,0:T(8,128)(2,1)S(1)}, bf16[1024,256]{1,0:T(8,128)(2,1)S(1)}, u32[]{:S(2)}, u32[]{:S(2)}) collective-permute-start(bf16[1024,256]{1,0:T(8,128)(2,1)S(1)} %collective-permute-done.5), channel_id=1, source_target_pairs={{0,4},{4,8},{8,12},{12,16},{16,20},{20,24},{24,28},{28,0},{1,5},{5... | collective-permute-start | bytes 1572872 | tf_op jit(solution)/shard_map/ppermute | solution.py:297
  140.8 10.5 %collective-permute-start.25 = (bf16[512,256]{1,0:T(8,128)(2,1)S(1)}, bf16[512,256]{1,0:T(8,128)(2,1)S(1)}, u32[]{:S(2)}, u32[]{:S(2)}) collective-permute-start(bf16[512,256]{1,0:T(8,128)(2,1)S(1)} %get-tuple-element.20), channel_id=1, source_target_pairs={{0,4},{4,8},{8,12},{12,16},{16,20},{20,24},{24,28},{28,0},{1,5},{5... | collective-permute-start | bytes 786440 | tf_op jit(solution)/shard_map/ppermute | solution.py:297
  140.9 10.5 %collective-permute-start.26 = (bf16[512,256]{1,0:T(8,128)(2,1)S(1)}, bf16[512,256]{1,0:T(8,128)(2,1)S(1)}, u32[]{:S(2)}, u32[]{:S(2)}) collective-permute-start(bf16[512,256]{1,0:T(8,128)(2,1)S(1)} %get-tuple-element.20), channel_id=1, source_target_pairs={{0,28},{4,0},{8,4},{12,8},{16,12},{20,16},{24,20},{28,24},{1,29},{... | collective-permute-start | bytes 786440 | tf_op jit(solution)/shard_map/ppermute | solution.py:300
  144.2 12.8 %collective-permute-start.20 = (bf16[512,256]{1,0:T(8,128)(2,1)S(1)}, bf16[512,256]{1,0:T(8,128)(2,1)S(1)}, u32[]{:S(2)}, u32[]{:S(2)}) collective-permute-start(bf16[512,256]{1,0:T(8,128)(2,1)S(1)} %collective-permute-done.18), channel_id=1, source_target_pairs={{0,4},{4,8},{8,12},{12,16},{16,20},{20,24},{24,28},{28,0},{1,5},{5... | collective-permute-start | bytes 786440 | tf_op jit(solution)/shard_map/ppermute | solution.py:297
  144.2 12.8 %collective-permute-start.21 = (bf16[512,256]{1,0:T(8,128)(2,1)S(1)}, bf16[512,256]{1,0:T(8,128)(2,1)S(1)}, u32[]{:S(2)}, u32[]{:S(2)}) collective-permute-start(bf16[512,256]{1,0:T(8,128)(2,1)S(1)} %collective-permute-done.19), channel_id=1, source_target_pairs={{0,28},{4,0},{8,4},{12,8},{16,12},{20,16},{24,20},{28,24},{1,29},{... | collective-permute-start | bytes 786440 | tf_op jit(solution)/shard_map/ppermute | solution.py:300
  151.4 11.2 %collective-permute-start.27 = (bf16[512,256]{1,0:T(8,128)(2,1)S(1)}, bf16[512,256]{1,0:T(8,128)(2,1)S(1)}, u32[]{:S(2)}, u32[]{:S(2)}) collective-permute-start(bf16[512,256]{1,0:T(8,128)(2,1)S(1)} %collective-permute-done.25), channel_id=1, source_target_pairs={{0,4},{4,8},{8,12},{12,16},{16,20},{20,24},{24,28},{28,0},{1,5},{5... | collective-permute-start | bytes 786440 | tf_op jit(solution)/shard_map/ppermute | solution.py:297
  151.4 11.2 %collective-permute-start.28 = (bf16[512,256]{1,0:T(8,128)(2,1)S(1)}, bf16[512,256]{1,0:T(8,128)(2,1)S(1)}, u32[]{:S(2)}, u32[]{:S(2)}) collective-permute-start(bf16[512,256]{1,0:T(8,128)(2,1)S(1)} %collective-permute-done.26), channel_id=1, source_target_pairs={{0,28},{4,0},{8,4},{12,8},{16,12},{20,16},{24,20},{28,24},{1,29},{... | collective-permute-start | bytes 786440 | tf_op jit(solution)/shard_map/ppermute | solution.py:300
  157.0 11.2 %collective-permute-start.22 = (bf16[512,256]{1,0:T(8,128)(2,1)S(1)}, bf16[512,256]{1,0:T(8,128)(2,1)S(1)}, u32[]{:S(2)}, u32[]{:S(2)}) collective-permute-start(bf16[512,256]{1,0:T(8,128)(2,1)S(1)} %collective-permute-done.20), channel_id=1, source_target_pairs={{0,4},{4,8},{8,12},{12,16},{16,20},{20,24},{24,28},{28,0},{1,5},{5... | collective-permute-start | bytes 786440 | tf_op jit(solution)/shard_map/ppermute | solution.py:297
  157.0 11.2 %collective-permute-start.23 = (bf16[512,256]{1,0:T(8,128)(2,1)S(1)}, bf16[512,256]{1,0:T(8,128)(2,1)S(1)}, u32[]{:S(2)}, u32[]{:S(2)}) collective-permute-start(bf16[512,256]{1,0:T(8,128)(2,1)S(1)} %collective-permute-done.21), channel_id=1, source_target_pairs={{0,28},{4,0},{8,4},{12,8},{16,12},{20,16},{24,20},{28,24},{1,29},{... | collective-permute-start | bytes 786440 | tf_op jit(solution)/shard_map/ppermute | solution.py:300
  162.6 11.7 %collective-permute-start.29 = (bf16[512,256]{1,0:T(8,128)(2,1)S(1)}, bf16[512,256]{1,0:T(8,128)(2,1)S(1)}, u32[]{:S(2)}, u32[]{:S(2)}) collective-permute-start(bf16[512,256]{1,0:T(8,128)(2,1)S(1)} %collective-permute-done.27), channel_id=1, source_target_pairs={{0,4},{4,8},{8,12},{12,16},{16,20},{20,24},{24,28},{28,0},{1,5},{5... | collective-permute-start | bytes 786440 | tf_op jit(solution)/shard_map/ppermute | solution.py:297
  183.5 15.6 %collective-permute-start.33 = (bf16[1024,256]{1,0:T(8,128)(2,1)S(1)}, bf16[1024,256]{1,0:T(8,128)(2,1)S(1)}, u32[]{:S(2)}, u32[]{:S(2)}) collective-permute-start(bf16[1024,256]{1,0:T(8,128)(2,1)S(1)} %fusion.18), channel_id=1, source_target_pairs={{0,1},{1,0},{2,3},{3,2},{4,5},{5,4},{6,7},{7,6},{8,9},{9,8},{10,11... | collective-permute-start | bytes 1572872 | tf_op jit(solution)/shard_map/ppermute | solution.py:343
  (12 other events, 112.8 us)
